TPU v7x, 128 devices: a whole 4x4x4 slice. The times are simulated.
128 devices in a mesh: ctx: 32 (over z, x, y_lo), tp: 4 (over y_hi, core).
Axes of the slice: x: 4, y: 4 (y_hi: 2, y_lo: 2; y = y_hi * 2 + y_lo), z: 4, core: 2. Of those that a mesh axis runs over, the one named last changes fastest.
Arguments:
- signal: bfloat16 [4096, 2048], P('ctx', 'tp'), may hold values from -6 to 6
- gate: bfloat16 [4096, 2048], P('ctx', 'tp'), may hold values from -6 to 6
- filt: bfloat16 [4096, 2048], P('ctx', 'tp'), may hold values from -0.25 to 0.25
- bias: float32 [2048], P('tp'), may hold values from -2 to 2
- doc_ids: int32 [4096], replicated, may hold values from 0 to 3, never falling along the last dimension, each value on 1 to 3840 neighbouring positions
- block_perm: int32 [64], replicated, may hold values from 0 to 63, each once
- out_weight: bfloat16 [2048, 2048], P('tp'), may hold values from -0.125 to 0.125
Outputs:
- mixed: bfloat16 [4096, 2048], P('ctx', 'tp')
Inputs may be any that keep to these rules, and one draw needn't show every extreme that they name: `doc_ids`: ids never fall along the sequence; each document is a run of 1 to 3840 positions, one exactly 3840. `block_perm`: each block number once.
All inputs are finite; a program needn't handle non-finite values.
Results may differ from a plain program's by a relative error of at most 0.012.
Values may be sent and summed in bfloat16 or wider, within the bound.
No kernel may reach another device: no remote copies, remote signals or barrier semaphores. Data moves between devices by JAX's collectives and lax.ppermute only.
A program may use at most 64 MiB of HBM per device.

v0:
```python
import jax
import jax.numpy as jnp
from jax import lax
from jax.experimental import pallas as pl
from jax.experimental.pallas import tpu as pltpu
from jax.sharding import PartitionSpec as P

SPAN = 64
DOC_COUNT = 4


CHANNELS_PER_STEP = 2


def conv_kernel(bias_ref, f_ref, x_ref, doc_ref, mz_ref, y_ref):
    blocks, span = x_ref.shape[1], x_ref.shape[2]
    seq = blocks * span
    lanes = 2 * span
    docs = doc_ref[...]
    lead = docs[:, 0:1]
    last = docs[:, span - 1 : span]
    lead_rows = docs == lead
    last_rows = (docs == last) & (docs != lead)
    doc_rows = [docs == doc for doc in range(DOC_COUNT)]
    for k in range(x_ref.shape[0]):
        channel = pl.program_id(0) * x_ref.shape[0] + k
        frow = f_ref[k].astype(jnp.float32)
        frow = jnp.concatenate([frow, jnp.zeros((1, lanes), jnp.float32)], axis=1)
        fb = jnp.broadcast_to(frow, (span, seq + lanes))
        tt = pltpu.roll(fb, 0, 1, stride=1, stride_axis=0)[:, :seq].astype(jnp.bfloat16)
        x = x_ref[k]
        zero = jnp.zeros_like(x)
        z_lead = jnp.dot(jnp.where(lead_rows, x, zero), tt, preferred_element_type=jnp.float32)
        z_last = jnp.dot(jnp.where(last_rows, x, zero), tt, preferred_element_type=jnp.float32)
        zm = z_lead * mz_ref[0] + z_last * mz_ref[1]
        acc = zm[:, :lanes]
        for pair in range(1, seq // lanes):
            acc = acc + pltpu.roll(zm[:, pair * lanes : (pair + 1) * lanes], 2 * pair, 0)
        y = acc[:, :span] + pltpu.roll(acc[:, span:], 1, 0)
        planes = jnp.concatenate([jnp.where(rows, x, zero) for rows in doc_rows], axis=0)
        local = jnp.dot(planes, tt[:, :span], preferred_element_type=jnp.float32)
        for doc in range(DOC_COUNT):
            y = y + jnp.where(doc_rows[doc], local[doc * blocks : (doc + 1) * blocks], 0.0)
        y = y + bias_ref[channel] * x.astype(jnp.float32)
        y_ref[k] = y.astype(y_ref.dtype)


def pallas_conv(x_cm, f_cm, doc_ids, bias_cm):
    chans, seq = x_cm.shape
    span = SPAN
    blocks = seq // span
    step = CHANNELS_PER_STEP
    xb = x_cm.reshape(chans, blocks, span)
    docb = doc_ids.reshape(blocks, span)
    ends = jnp.sum(doc_ids[None, None, :] <= jnp.stack([docb[:, 0], docb[:, -1]])[:, :, None], axis=2)
    rel = lax.broadcasted_iota(jnp.int32, (blocks, seq), 1)
    pos = rel + span * lax.broadcasted_iota(jnp.int32, (blocks, seq), 0)
    mz = ((rel >= span)[None] & (pos[None] < ends[:, :, None])).astype(jnp.float32)
    return pl.pallas_call(
        conv_kernel,
        grid=(chans // step,),
        in_specs=[
            pl.BlockSpec(memory_space=pltpu.SMEM),
            pl.BlockSpec((step, 1, seq), lambda c: (c, 0, 0)),
            pl.BlockSpec((step, blocks, span), lambda c: (c, 0, 0)),
            pl.BlockSpec((blocks, span), lambda c: (0, 0)),
            pl.BlockSpec((2, blocks, seq), lambda c: (0, 0, 0)),
        ],
        out_specs=pl.BlockSpec((step, blocks, span), lambda c: (c, 0, 0)),
        out_shape=jax.ShapeDtypeStruct((chans, blocks, span), jnp.bfloat16),
    )(bias_cm, f_cm.reshape(chans, 1, seq), xb, docb, mz)


def body(signal, gate, filt, bias, doc_ids, block_perm, out_weight):
    span = SPAN
    rows, chans = signal.shape
    blocks = block_perm.shape[0]
    seq = blocks * span
    n_ctx = seq // rows
    per_dev = chans // n_ctx
    ctx_index = lax.axis_index("ctx")

    inverse = jnp.zeros((blocks,), jnp.int32).at[block_perm].set(jnp.arange(blocks, dtype=jnp.int32))

    def slots_to_natural(a):
        return jnp.take(a.reshape(per_dev, blocks, span), inverse, axis=1).reshape(per_dev, seq)

    packed = jnp.stack(
        [a.reshape(rows, n_ctx, per_dev) for a in (signal, filt)], axis=2
    ).reshape(rows, n_ctx * 2 * per_dev)
    arrived = lax.all_to_all(packed, "ctx", 1, 0, tiled=True).T
    x_cm = slots_to_natural(arrived[:per_dev])
    f_cm = arrived[per_dev:]
    bias_cm = lax.dynamic_slice_in_dim(bias, ctx_index * per_dev, per_dev)
    pre = pallas_conv(x_cm, f_cm, doc_ids, bias_cm)
    pre_slots = jnp.take(pre, block_perm, axis=1)
    pre_slots = pre_slots.reshape(per_dev, seq).T
    pre_local = lax.all_to_all(pre_slots, "ctx", 0, 1, tiled=True)
    gated_local = (gate.astype(jnp.float32) * pre_local.astype(jnp.float32)).astype(jnp.bfloat16)
    tp_index = lax.axis_index("tp")
    n_tp = out_weight.shape[1] // chans
    high, core = tp_index // 2, tp_index % 2
    w_split = out_weight.reshape(chans, n_tp // 2, 2, chans)
    w_other = lax.dynamic_index_in_dim(w_split, 1 - core, axis=2, keepdims=False)
    p_other = jnp.dot(
        gated_local, w_other.reshape(chans, -1), preferred_element_type=jnp.float32
    )
    recv_core = lax.ppermute(p_other.astype(jnp.bfloat16), "tp", [(i, i ^ 1) for i in range(n_tp)])
    w_mine = lax.dynamic_index_in_dim(w_split, core, axis=2, keepdims=False)
    p_mine = jnp.dot(gated_local, w_mine.reshape(chans, -1), preferred_element_type=jnp.float32)
    p_mine = p_mine + recv_core.astype(jnp.float32)
    send_high = lax.dynamic_slice_in_dim(p_mine, (1 - high) * chans, chans, axis=1)
    keep_high = lax.dynamic_slice_in_dim(p_mine, high * chans, chans, axis=1)
    recv_high = lax.ppermute(
        send_high.astype(jnp.bfloat16), "tp", [(i, i ^ 2) for i in range(n_tp)]
    )
    return (keep_high + recv_high.astype(jnp.float32)).astype(jnp.bfloat16)


def solution(mesh):
    return jax.shard_map(
        body,
        mesh=mesh,
        in_specs=(P("ctx", "tp"), P("ctx", "tp"), P("ctx", "tp"), P("tp"), P(), P(), P("tp", None)),
        out_specs=P("ctx", "tp"),
        check_vma=False,
    )
```

profile of v0, /device:TPU:1, one launch (start us, length us, event | category | flops | bytes accessed | tf_op | source)
XLA Modules:
  0.0 65.0 jit_solution(8396299054124210433)
XLA Ops:
  0.0 1.0 %copy.52 = bf16[128,512]{0,1:T(8,128)(2,1)S(1)} copy(bf16[128,512]{1,0:T(8,128)(2,1)} %param.9) | data formatting | bytes 262144 | tf_op args[0]
  1.1 1.0 %copy.53 = bf16[128,512]{0,1:T(8,128)(2,1)S(1)} copy(bf16[128,512]{1,0:T(8,128)(2,1)} %param.11) | data formatting | bytes 262144 | tf_op args[2]
  2.1 0.7 %copy.54 = bf16[128,32,2,16]{0,3,2,1:T(8,128)(2,1)} copy(bf16[128,32,2,16]{0,3,1,2:T(8,128)(2,1)S(1)} %pad_maximum_fusion) | data formatting | bytes 524288 | tf_op jit(solution)/shard_map/stack | solution.py:88
  2.8 9.7 %all-to-all-start = ((bf16[128,32,32]{0,2,1:T(8,128)(2,1)}), bf16[128,32,32]{0,2,1:T(8,128)(2,1)S(1)}, u32[]{:S(2)}, u32[]{:S(2)}) async-start(bf16[128,32,32]{0,2,1:T(8,128)(2,1)} %bitcast.2), calls=%async_computation | async-start | bytes 524288 | tf_op jit(solution)/shard_map/all_to_all | solution.py:91
  12.6 0.8 %scatter_custom_fusion = s32[64]{0:T(128)S(1)} fusion(s32[64]{0:T(128)S(1)} %compare_select_fusion, s32[64]{0:T(128)S(1)} %iota.20, s32[]{:T(128)} %constant.54.clone.1), kind=kCustom, calls=%fused_computation.32 | custom fusion | bytes 260 | tf_op jit(solution)/shard_map/scatter | solution.py:83
  14.2 1.7 %and_convert_fusion.mz_ref = f32[2,64,4096]{2,1,0:T(8,128)} fusion(s32[2,64]{1,0:T(2,128)S(1)} %convert_reduce_fusion, s32[64,4096]{1,0:T(8,128)S(1)} %iota_add_fusion, pred[4096]{0:T(1024)(128)(4,1)S(1)} %iota_compare_fusion), kind=kLoop, calls=%fused_computation.4 | loop fusion | flops 1572864 | bytes 3150336 | tf_op jit(solution)/shard_map/convert_element_type | solution.py:58
  16.1 2.9 %copy.62 = bf16[512,2048]{0,1:T(8,128)(2,1)S(1)} copy(bf16[512,2048]{1,0:T(8,128)(2,1)} %param.15) | data formatting | bytes 4194304 | tf_op args[6]
  19.0 1.3 %dynamic_slice.16.bias_ref = f32[16]{0:T(128)} dynamic-slice(f32[512]{0:T(512)} %param.12, s32[]{:T(128)S(6)} %select_n.37), dynamic_slice_sizes={16} | dynamic-slice | bytes 132 | tf_op jit(solution)/shard_map/dynamic_slice | solution.py:94
  20.3 0.8 %all-to-all-done = bf16[128,32,32]{0,2,1:T(8,128)(2,1)S(1)} async-done(((bf16[128,32,32]{0,2,1:T(8,128)(2,1)}), bf16[128,32,32]{0,2,1:T(8,128)(2,1)S(1)}, u32[]{:S(2)}, u32[]{:S(2)}) %all-to-all-start) | async-done | bytes 262176 | tf_op jit(solution)/shard_map/all_to_all | solution.py:91
  21.6 0.9 %copy.58.f_ref = bf16[16,1,4096]{2,1,0:T(2,128)(2,1)} copy(bf16[16,1,4096]{2,0,1:T(8,128)(2,1)S(1)} %get-tuple-element.11) | data formatting | bytes 262144 | tf_op jit(solution)/shard_map/reshape | solution.py:71
  22.6 0.6 gather_fusion
  23.2 0.8 %fusion.1.x_ref = bf16[16,64,64]{2,1,0:T(8,128)(2,1)} fusion(bf16[64,16,64]{2,1,0:T(8,128)(2,1)S(1)} %gather_fusion, pred[64]{0:T(512)(128)(4,1)S(1)} %get-tuple-element.13), kind=kLoop, calls=%fused_computation.13 | loop fusion | flops 65536 | bytes 262208 | tf_op jit(solution)/shard_map/jit(_take)/select_n | solution.py:86
  24.0 11.7 %shard_map.73 = bf16[16,64,64]{2,1,0:T(8,128)(2,1)} custom-call(f32[16]{0:T(128)} %dynamic_slice.16.bias_ref, bf16[16,1,4096]{2,1,0:T(2,128)(2,1)} %copy.58.f_ref, bf16[16,64,64]{2,1,0:T(8,128)(2,1)} %fusion.1.x_ref, s32[64,64]{1,0:T(8,128)} %copy-done.1, f32[2,64,4096]{2,1,0:T(8,128)} %and_convert_fusion.mz_ref), custom_call_target="tpu_custom_call" | custom-call | tf_op jit(solution)/shard_map/pallas_call | solution.py:59
  35.7 1.1 %copy.59 = bf16[16,64,64]{2,0,1:T(8,128)(2,1)S(1)} copy(bf16[16,64,64]{2,1,0:T(8,128)(2,1)} %shard_map.73) | data formatting | bytes 262144 | tf_op jit(solution)/shard_map/pallas_call | solution.py:59
  36.8 0.6 gather_fusion.1
  37.9 0.7 %copy_bitcast_fusion = bf16[32,128,16]{1,2,0:T(8,128)(2,1)} fusion(bf16[16,4096]{1,0:T(8,128)(2,1)S(1)} %reshape.60), kind=kLoop, calls=%fused_computation.17 | loop fusion | bytes 262144 | tf_op jit(solution)/shard_map/all_to_all | solution.py:98
  38.6 6.9 %all-to-all-start.1 = ((bf16[32,128,16]{1,2,0:T(8,128)(2,1)}), bf16[32,128,16]{1,2,0:T(8,128)(2,1)S(1)}, u32[]{:S(2)}, u32[]{:S(2)}) async-start(bf16[32,128,16]{1,2,0:T(8,128)(2,1)} %copy_bitcast_fusion), calls=%async_computation.1 | async-start | bytes 262144 | tf_op jit(solution)/shard_map/all_to_all | solution.py:98
  45.6 1.2 %constant_dynamic-slice_fusion = (bf16[512,2,1,512]{0,3,2,1:T(8,128)(2,1)S(1)}, bf16[512,2,1,512]{0,3,2,1:T(8,128)(2,1)}) fusion(bf16[512,2,2,512]{0,3,2,1:T(8,128)(2,1)S(1)} %bitcast.39, s32[]{:T(128)S(6)} %select_n.41, s32[]{:T(128)S(6)} %select_n.40), kind=kLoop, calls=%fused_computation.29 | loop fusion | bytes 4194312 | tf_op jit(solution)/shard_map/jit(dynamic_index_in_dim)/dynamic_slice | solution.py:104
  46.7 6.4 %all-to-all-done.1 = bf16[32,128,16]{1,2,0:T(8,128)(2,1)S(1)} async-done(((bf16[32,128,16]{1,2,0:T(8,128)(2,1)}), bf16[32,128,16]{1,2,0:T(8,128)(2,1)S(1)}, u32[]{:S(2)}, u32[]{:S(2)}) %all-to-all-start.1) | async-done | bytes 131104 | tf_op jit(solution)/shard_map/all_to_all | solution.py:98
  53.7 2.7 %collective-permute-start = (bf16[128,1024]{1,0:T(8,128)(2,1)S(1)}, bf16[128,1024]{1,0:T(8,128)(2,1)S(1)}, u32[]{:S(2)}, u32[]{:S(2)}) collective-permute-start(bf16[128,1024]{1,0:T(8,128)(2,1)S(1)} %convolution_convert_fusion), channel_id=1, source_target_pairs={{0,1},{1,0},{2,3},{3,2},{4,5},{5,4},{6,7},{7,6},{8,9},{9,8},{10,11... | collective-permute-start | bytes 786440 | tf_op jit(solution)/shard_map/ppermute | solution.py:108
  56.4 1.2 %collective-permute-done = bf16[128,1024]{1,0:T(8,128)(2,1)S(1)} collective-permute-done((bf16[128,1024]{1,0:T(8,128)(2,1)S(1)}, bf16[128,1024]{1,0:T(8,128)(2,1)S(1)}, u32[]{:S(2)}, u32[]{:S(2)}) %collective-permute-start) | collective-permute-done | bytes 262176 | tf_op jit(solution)/shard_map/ppermute | solution.py:108
  58.1 2.7 %collective-permute-start.1 = (bf16[128,512]{1,0:T(8,128)(2,1)S(1)}, bf16[128,512]{1,0:T(8,128)(2,1)S(1)}, u32[]{:S(2)}, u32[]{:S(2)}) collective-permute-start(bf16[128,512]{1,0:T(8,128)(2,1)S(1)} %dynamic-slice_convert_fusion), channel_id=1, source_target_pairs={{0,2},{1,3},{2,0},{3,1},{4,6},{5,7},{6,4},{7,5},{8,10},{9,11},{10,... | collective-permute-start | bytes 393224 | tf_op jit(solution)/shard_map/ppermute | solution.py:114
  60.8 3.6 %collective-permute-done.1 = bf16[128,512]{1,0:T(8,128)(2,1)S(1)} collective-permute-done((bf16[128,512]{1,0:T(8,128)(2,1)S(1)}, bf16[128,512]{1,0:T(8,128)(2,1)S(1)}, u32[]{:S(2)}, u32[]{:S(2)}) %collective-permute-start.1) | collective-permute-done | bytes 131104 | tf_op jit(solution)/shard_map/ppermute | solution.py:114
  64.3 0.7 %add_convert_fusion = bf16[128,512]{1,0:T(8,128)(2,1)} fusion(bf16[128,512]{1,0:T(8,128)(2,1)S(1)} %collective-permute-done.1, f32[128,1024]{1,0:T(8,128)S(1)} %convert_add_fusion, s32[]{:T(128)S(6)} %select_n.43), kind=kLoop, calls=%fused_computation.15 | loop fusion | flops 196608 | bytes 524292 | tf_op jit(solution)/shard_map/convert_element_type | solution.py:117
  (36 shorter events, 2.9 us)
Async XLA Ops:
  0.0 12.6 %copy-start.4 = (s32[64]{0:T(128)S(1)}, s32[64]{0:T(128)}, u32[]{:S(2)}) copy-start(s32[64]{0:T(128)} %param.14) | copy-start | bytes 772
  0.0 13.4 %copy-start.3 = (s32[4096]{0:T(1024)S(1)}, s32[4096]{0:T(1024)}, u32[]{:S(2)}) copy-start(s32[4096]{0:T(1024)} %param.13) | copy-start | bytes 49156
  2.8 18.3 %all-to-all-start = ((bf16[128,32,32]{0,2,1:T(8,128)(2,1)}), bf16[128,32,32]{0,2,1:T(8,128)(2,1)S(1)}, u32[]{:S(2)}, u32[]{:S(2)}) async-start(bf16[128,32,32]{0,2,1:T(8,128)(2,1)} %bitcast.2), calls=%async_computation | async-start | bytes 524288 | tf_op jit(solution)/shard_map/all_to_all | solution.py:91
  13.5 2.4 %copy-start.1 = (s32[64,64]{1,0:T(8,128)}, s32[64,64]{1,0:T(8,128)S(1)}, u32[]{:S(2)}) copy-start(s32[64,64]{1,0:T(8,128)S(1)} %reshape.59.doc_ref) | copy-start | bytes 49156
  14.1 1.9 %copy-start.2 = (bf16[128,512]{1,0:T(8,128)(2,1)S(1)}, bf16[128,512]{1,0:T(8,128)(2,1)}, u32[]{:S(2)}) copy-start(bf16[128,512]{1,0:T(8,128)(2,1)} %param.10) | copy-start | bytes 393220
  38.6 14.5 %all-to-all-start.1 = ((bf16[32,128,16]{1,2,0:T(8,128)(2,1)}), bf16[32,128,16]{1,2,0:T(8,128)(2,1)S(1)}, u32[]{:S(2)}, u32[]{:S(2)}) async-start(bf16[32,128,16]{1,2,0:T(8,128)(2,1)} %copy_bitcast_fusion), calls=%async_computation.1 | async-start | bytes 262144 | tf_op jit(solution)/shard_map/all_to_all | solution.py:98
  46.7 10.8 %copy-start = (bf16[512,2,1,512]{0,3,2,1:T(8,128)(2,1)S(1)}, bf16[512,2,1,512]{0,3,2,1:T(8,128)(2,1)}, u32[]{:S(2)}) copy-start(bf16[512,2,1,512]{0,3,2,1:T(8,128)(2,1)} %get-tuple-element.9) | copy-start | bytes 3145732
  53.7 3.9 %collective-permute-start = (bf16[128,1024]{1,0:T(8,128)(2,1)S(1)}, bf16[128,1024]{1,0:T(8,128)(2,1)S(1)}, u32[]{:S(2)}, u32[]{:S(2)}) collective-permute-start(bf16[128,1024]{1,0:T(8,128)(2,1)S(1)} %convolution_convert_fusion), channel_id=1, source_target_pairs={{0,1},{1,0},{2,3},{3,2},{4,5},{5,4},{6,7},{7,6},{8,9},{9,8},{10,11... | collective-permute-start | bytes 786440 | tf_op jit(solution)/shard_map/ppermute | solution.py:108
  58.1 6.3 %collective-permute-start.1 = (bf16[128,512]{1,0:T(8,128)(2,1)S(1)}, bf16[128,512]{1,0:T(8,128)(2,1)S(1)}, u32[]{:S(2)}, u32[]{:S(2)}) collective-permute-start(bf16[128,512]{1,0:T(8,128)(2,1)S(1)} %dynamic-slice_convert_fusion), channel_id=1, source_target_pairs={{0,2},{1,3},{2,0},{3,1},{4,6},{5,7},{6,4},{7,5},{8,10},{9,11},{10,... | collective-permute-start | bytes 393224 | tf_op jit(solution)/shard_map/ppermute | solution.py:114
where the time goes:
time: 65.5 us; the launch traced here: 65 us
  starting transfers between devices  22.1 us (34%)
  local copies, waits for them, and re-layouts  14.1 us (22%)
  waiting for transfers between devices  11.9 us (18%)
  Pallas kernels  11.7 us (18%)
  other arithmetic  3.95 us (6%)
  matrix products  0.95 us (1%)
    pallas_call x1, Pallas kernels, pallas_conv(): pl.pallas_call(conv_kernel, grid=(chans // step,), in_specs=[pl.BlockSpec...  11.7 us
    all_to_all x1, starting transfers between devices, body(): arrived = lax.all_to_all(packed, 'ctx', 1, 0, tiled=True).T  9.71 us
    all_to_all x1, starting transfers between devices, body(): pre_local = lax.all_to_all(pre_slots, 'ctx', 0, 1, tiled=True)  6.93 us
    all_to_all x1, waiting for transfers between devices, body(): pre_local = lax.all_to_all(pre_slots, 'ctx', 0, 1, tiled=True)  6.39 us
    unnamed x14, local copies, waits for them, and re-layouts  5.07 us
    ppermute x1, waiting for transfers between devices, body(): lax.ppermute(send_high.astype(jnp.bfloat16), 'tp', [(i, i ^ 2) for i in r...  3.55 us
    ppermute x1, starting transfers between devices, body(): lax.ppermute(p_other.astype(jnp.bfloat16), 'tp', [(i, i ^ 1) for i in ran...  2.74 us
    ppermute x1, starting transfers between devices, body(): lax.ppermute(send_high.astype(jnp.bfloat16), 'tp', [(i, i ^ 2) for i in r...  2.71 us
  transfers between devices with their start and end apart: 4, of which 4 were waited for; matrix products, arithmetic and copies ran while one was open for 13% of the time, Pallas kernels for 0%

commit v1 on v0

--- a/solution.py
+++ b/solution.py
@@ -9,7 +9,7 @@
 DOC_COUNT = 4
 
 
-CHANNELS_PER_STEP = 2
+CHANNELS_PER_STEP = 4
 
 
 def conv_kernel(bias_ref, f_ref, x_ref, doc_ref, mz_ref, y_ref):
@@ -99,22 +99,16 @@
     gated_local = (gate.astype(jnp.float32) * pre_local.astype(jnp.float32)).astype(jnp.bfloat16)
     tp_index = lax.axis_index("tp")
     n_tp = out_weight.shape[1] // chans
-    high, core = tp_index // 2, tp_index % 2
-    w_split = out_weight.reshape(chans, n_tp // 2, 2, chans)
-    w_other = lax.dynamic_index_in_dim(w_split, 1 - core, axis=2, keepdims=False)
-    p_other = jnp.dot(
-        gated_local, w_other.reshape(chans, -1), preferred_element_type=jnp.float32
-    )
-    recv_core = lax.ppermute(p_other.astype(jnp.bfloat16), "tp", [(i, i ^ 1) for i in range(n_tp)])
-    w_mine = lax.dynamic_index_in_dim(w_split, core, axis=2, keepdims=False)
-    p_mine = jnp.dot(gated_local, w_mine.reshape(chans, -1), preferred_element_type=jnp.float32)
-    p_mine = p_mine + recv_core.astype(jnp.float32)
-    send_high = lax.dynamic_slice_in_dim(p_mine, (1 - high) * chans, chans, axis=1)
-    keep_high = lax.dynamic_slice_in_dim(p_mine, high * chans, chans, axis=1)
-    recv_high = lax.ppermute(
-        send_high.astype(jnp.bfloat16), "tp", [(i, i ^ 2) for i in range(n_tp)]
-    )
-    return (keep_high + recv_high.astype(jnp.float32)).astype(jnp.bfloat16)
+    total = None
+    for offset in range(n_tp):
+        target = (tp_index + offset) % n_tp
+        w_cols = lax.dynamic_slice_in_dim(out_weight, target * chans, chans, axis=1)
+        part = jnp.dot(gated_local, w_cols, preferred_element_type=jnp.float32)
+        if offset:
+            pairs = [(i, (i + offset) % n_tp) for i in range(n_tp)]
+            part = lax.ppermute(part.astype(jnp.bfloat16), "tp", pairs).astype(jnp.float32)
+        total = part if total is None else total + part
+    return total.astype(jnp.bfloat16)
 
 
 def solution(mesh):

time: 65.5 us -> 64.1 us (0.979)
  waiting for transfers between devices: 11.9 us -> 17.2 us
  local copies, waits for them, and re-layouts: 14.1 us -> 10.2 us
  starting transfers between devices: 22.1 us -> 19.7 us
  matrix products: 0.95 us -> 1.68 us
  other arithmetic: 3.95 us -> 3.27 us
    all_to_all x1, starting transfers between devices: 6.93 us -> 3.87 us  [body(): pre_local = lax.all_to_all(pre_slots, 'ctx', 0, 1, tiled=True)]
    all_to_all x1, waiting for transfers between devices: 0.82 us -> 3.87 us  [body(): arrived = lax.all_to_all(packed, 'ctx', 1, 0, tiled=True).T]
    unnamed x14 -> x13, local copies, waits for them, and re-layouts: 5.07 us -> 2.33 us
    ppermute x2 -> x3, waiting for transfers between devices: 4.71 us -> 5.99 us  [body(): lax.ppermute(part.astype(jnp.bfloat16), 'tp', pairs).astype(jnp.float32)]
    dynamic_slice x1 -> x0, local copies, waits for them, and re-layouts: 1.17 us -> none  [body(): lax.dynamic_index_in_dim(w_split, 1 - core, axis=2, keepdims=False)]
    all_to_all x1, waiting for transfers between devices: 6.39 us -> 7.38 us  [body(): pre_local = lax.all_to_all(pre_slots, 'ctx', 0, 1, tiled=True)]
    dot_general x2 -> x4, matrix products: 0.95 us -> 1.68 us  [body(): part = jnp.dot(gated_local, w_cols, preferred_element_type=jnp.float32)]
    convert_element_type x1 -> x0, other arithmetic: 0.68 us -> none  [body(): return (keep_high + recv_high.astype(jnp.float32)).astype(jnp.bfloat16)]
  transfers between devices with their start and end apart: 4 -> 5, of which waited for: 4 -> 5; matrix products, arithmetic and copies ran while one was open for 13% -> 8% of each run, Pallas kernels for 0% -> 0%
where the time goes in v1:
time: 64.1 us; the launch traced here: 63.7 us
  starting transfers between devices  19.7 us (31%)
  waiting for transfers between devices  17.2 us (27%)
  Pallas kernels  11.3 us (18%)
  local copies, waits for them, and re-layouts  10.2 us (16%)
  other arithmetic  3.27 us (5%)
  matrix products  1.68 us (3%)
    pallas_call x1, Pallas kernels, pallas_conv(): pl.pallas_call(conv_kernel, grid=(chans // step,), in_specs=[pl.BlockSpec...  11.3 us
    all_to_all x1, starting transfers between devices, body(): arrived = lax.all_to_all(packed, 'ctx', 1, 0, tiled=True).T  9.71 us
    all_to_all x1, waiting for transfers between devices, body(): pre_local = lax.all_to_all(pre_slots, 'ctx', 0, 1, tiled=True)  7.38 us
    ppermute x3, starting transfers between devices, body(): lax.ppermute(part.astype(jnp.bfloat16), 'tp', pairs).astype(jnp.float32)  6.08 us
    ppermute x3, waiting for transfers between devices, body(): lax.ppermute(part.astype(jnp.bfloat16), 'tp', pairs).astype(jnp.float32)  5.99 us
    all_to_all x1, starting transfers between devices, body(): pre_local = lax.all_to_all(pre_slots, 'ctx', 0, 1, tiled=True)  3.87 us
    all_to_all x1, waiting for transfers between devices, body(): arrived = lax.all_to_all(packed, 'ctx', 1, 0, tiled=True).T  3.87 us
    unnamed x13, local copies, waits for them, and re-layouts  2.33 us
  transfers between devices with their start and end apart: 5, of which 5 were waited for; matrix products, arithmetic and copies ran while one was open for 8% of the time, Pallas kernels for 0%

profile of v1, /device:TPU:1, one launch (start us, length us, event | category | flops | bytes accessed | tf_op | source)
XLA Modules:
  0.0 63.7 jit_solution(1216667143586811360)
XLA Ops:
  0.0 1.2 %copy.49 = bf16[128,512]{0,1:T(8,128)(2,1)S(1)} copy(bf16[128,512]{1,0:T(8,128)(2,1)} %param.9) | data formatting | bytes 262144 | tf_op args[0]
  1.2 1.0 %copy.50 = bf16[128,512]{0,1:T(8,128)(2,1)S(1)} copy(bf16[128,512]{1,0:T(8,128)(2,1)} %param.11) | data formatting | bytes 262144 | tf_op args[2]
  2.3 0.7 %copy.51 = bf16[128,32,2,16]{0,3,2,1:T(8,128)(2,1)} copy(bf16[128,32,2,16]{0,3,1,2:T(8,128)(2,1)S(1)} %pad_maximum_fusion) | data formatting | bytes 524288 | tf_op jit(solution)/shard_map/stack | solution.py:88
  3.0 9.7 %all-to-all-start = ((bf16[128,32,32]{0,2,1:T(8,128)(2,1)}), bf16[128,32,32]{0,2,1:T(8,128)(2,1)S(1)}, u32[]{:S(2)}, u32[]{:S(2)}) async-start(bf16[128,32,32]{0,2,1:T(8,128)(2,1)} %bitcast.2), calls=%async_computation | async-start | bytes 524288 | tf_op jit(solution)/shard_map/all_to_all | solution.py:91
  12.8 0.8 %scatter_custom_fusion = s32[64]{0:T(128)S(1)} fusion(s32[64]{0:T(128)S(1)} %compare_select_fusion, s32[64]{0:T(128)S(1)} %iota.20, s32[]{:T(128)} %constant.51.clone.1), kind=kCustom, calls=%fused_computation.39 | custom fusion | bytes 260 | tf_op jit(solution)/shard_map/scatter | solution.py:83
  13.8 0.4 convert_reduce_fusion
  14.4 1.7 %and_convert_fusion.mz_ref = f32[2,64,4096]{2,1,0:T(8,128)} fusion(s32[2,64]{1,0:T(2,128)S(1)} %convert_reduce_fusion, s32[64,4096]{1,0:T(8,128)S(1)} %iota_add_fusion, pred[4096]{0:T(1024)(128)(4,1)S(1)} %iota_compare_fusion), kind=kLoop, calls=%fused_computation.4 | loop fusion | flops 1572864 | bytes 3150336 | tf_op jit(solution)/shard_map/convert_element_type | solution.py:58
  16.1 1.3 %dynamic_slice.15.bias_ref = f32[16]{0:T(128)} dynamic-slice(f32[512]{0:T(512)} %param.12, s32[]{:T(128)S(6)} %select_n.44), dynamic_slice_sizes={16} | dynamic-slice | bytes 132 | tf_op jit(solution)/shard_map/dynamic_slice | solution.py:94
  17.4 3.9 %all-to-all-done = bf16[128,32,32]{0,2,1:T(8,128)(2,1)S(1)} async-done(((bf16[128,32,32]{0,2,1:T(8,128)(2,1)}), bf16[128,32,32]{0,2,1:T(8,128)(2,1)S(1)}, u32[]{:S(2)}, u32[]{:S(2)}) %all-to-all-start) | async-done | bytes 262176 | tf_op jit(solution)/shard_map/all_to_all | solution.py:91
  21.7 0.9 %copy.55.f_ref = bf16[16,1,4096]{2,1,0:T(2,128)(2,1)} copy(bf16[16,1,4096]{2,0,1:T(8,128)(2,1)S(1)} %get-tuple-element.9) | data formatting | bytes 262144 | tf_op jit(solution)/shard_map/reshape | solution.py:71
  22.7 0.6 gather_fusion
  23.3 0.8 %fusion.6.x_ref = bf16[16,64,64]{2,1,0:T(8,128)(2,1)} fusion(bf16[64,16,64]{2,1,0:T(8,128)(2,1)S(1)} %gather_fusion, pred[64]{0:T(512)(128)(4,1)S(1)} %get-tuple-element.11), kind=kLoop, calls=%fused_computation.19 | loop fusion | flops 65536 | bytes 262208 | tf_op jit(solution)/shard_map/jit(_take)/select_n | solution.py:86
  24.1 11.3 %shard_map.73 = bf16[16,64,64]{2,1,0:T(8,128)(2,1)} custom-call(f32[16]{0:T(128)} %dynamic_slice.15.bias_ref, bf16[16,1,4096]{2,1,0:T(2,128)(2,1)} %copy.55.f_ref, bf16[16,64,64]{2,1,0:T(8,128)(2,1)} %fusion.6.x_ref, s32[64,64]{1,0:T(8,128)} %copy-done.1, f32[2,64,4096]{2,1,0:T(8,128)} %and_convert_fusion.mz_ref), custom_call_target="tpu_custom_call" | custom-call | tf_op jit(solution)/shard_map/pallas_call | solution.py:59
  35.5 1.2 %copy.56 = bf16[16,64,64]{2,0,1:T(8,128)(2,1)S(1)} copy(bf16[16,64,64]{2,1,0:T(8,128)(2,1)} %shard_map.73) | data formatting | bytes 262144 | tf_op jit(solution)/shard_map/pallas_call | solution.py:59
  36.6 0.6 gather_fusion.1
  37.8 0.7 %copy_bitcast_fusion = bf16[32,128,16]{1,2,0:T(8,128)(2,1)} fusion(bf16[16,4096]{1,0:T(8,128)(2,1)S(1)} %reshape.49), kind=kLoop, calls=%fused_computation.22 | loop fusion | bytes 262144 | tf_op jit(solution)/shard_map/all_to_all | solution.py:98
  38.4 3.9 %all-to-all-start.1 = ((bf16[32,128,16]{1,2,0:T(8,128)(2,1)}), bf16[32,128,16]{1,2,0:T(8,128)(2,1)S(1)}, u32[]{:S(2)}, u32[]{:S(2)}) async-start(bf16[32,128,16]{1,2,0:T(8,128)(2,1)} %copy_bitcast_fusion), calls=%async_computation.1 | async-start | bytes 262144 | tf_op jit(solution)/shard_map/all_to_all | solution.py:98
  42.5 7.4 %all-to-all-done.1 = bf16[32,128,16]{1,2,0:T(8,128)(2,1)S(1)} async-done(((bf16[32,128,16]{1,2,0:T(8,128)(2,1)}), bf16[32,128,16]{1,2,0:T(8,128)(2,1)S(1)}, u32[]{:S(2)}, u32[]{:S(2)}) %all-to-all-start.1) | async-done | bytes 131104 | tf_op jit(solution)/shard_map/all_to_all | solution.py:98
  50.2 5.5 %collective-permute-start = (bf16[128,512]{1,0:T(8,128)(2,1)S(1)}, bf16[128,512]{1,0:T(8,128)(2,1)S(1)}, u32[]{:S(2)}, u32[]{:S(2)}) collective-permute-start(bf16[128,512]{1,0:T(8,128)(2,1)S(1)} %convolution_convert_fusion.2), channel_id=1, source_target_pairs={{0,1},{1,2},{2,3},{3,0},{4,5},{5,6},{6,7},{7,4},{8,9},{9,10},{10,1... | collective-permute-start | bytes 393224 | tf_op jit(solution)/shard_map/ppermute | solution.py:109
  56.0 0.4 collective-permute-start.1
  56.8 1.3 %collective-permute-done = bf16[128,512]{1,0:T(8,128)(2,1)S(1)} collective-permute-done((bf16[128,512]{1,0:T(8,128)(2,1)S(1)}, bf16[128,512]{1,0:T(8,128)(2,1)S(1)}, u32[]{:S(2)}, u32[]{:S(2)}) %collective-permute-start) | collective-permute-done | bytes 131104 | tf_op jit(solution)/shard_map/ppermute | solution.py:109
  58.1 3.4 %collective-permute-done.1 = bf16[128,512]{1,0:T(8,128)(2,1)S(1)} collective-permute-done((bf16[128,512]{1,0:T(8,128)(2,1)S(1)}, bf16[128,512]{1,0:T(8,128)(2,1)S(1)}, u32[]{:S(2)}, u32[]{:S(2)}) %collective-permute-start.1) | collective-permute-done | bytes 131104 | tf_op jit(solution)/shard_map/ppermute | solution.py:109
  61.5 1.2 %collective-permute-done.2 = bf16[128,512]{1,0:T(8,128)(2,1)S(1)} collective-permute-done((bf16[128,512]{1,0:T(8,128)(2,1)S(1)}, bf16[128,512]{1,0:T(8,128)(2,1)S(1)}, u32[]{:S(2)}, u32[]{:S(2)}) %collective-permute-start.2) | collective-permute-done | bytes 131104 | tf_op jit(solution)/shard_map/ppermute | solution.py:109
  62.8 0.9 %add_convert_fusion = bf16[128,512]{1,0:T(8,128)(2,1)} fusion(bf16[128,512]{1,0:T(8,128)(2,1)S(1)} %collective-permute-done.2, bf16[128,512]{1,0:T(8,128)(2,1)S(1)} %collective-permute-done.1, bf16[128,512]{1,0:T(8,128)(2,1)S(1)} %collective-permute-done, bf16[128,512]{0,1:T(8,128)(2,1)S(1)} %fusion.5, bf16[512,2048]{1,0:T(8,128)(2,1)S(1)} %copy-done, ...), kind=kOutput, calls=%fused_computation.21 | convolution fusion | flops 67567616 | bytes 1179652 | tf_op jit(solution)/shard_map/dot_general | solution.py:106
  (36 shorter events, 2.4 us)
Async XLA Ops:
  0.0 49.9 %copy-start = (bf16[512,2048]{1,0:T(8,128)(2,1)S(1)}, bf16[512,2048]{1,0:T(8,128)(2,1)}, u32[]{:S(2)}) copy-start(bf16[512,2048]{1,0:T(8,128)(2,1)} %param.15) | copy-start | bytes 6291460
  0.0 12.7 %copy-start.4 = (s32[64]{0:T(128)S(1)}, s32[64]{0:T(128)}, u32[]{:S(2)}) copy-start(s32[64]{0:T(128)} %param.14) | copy-start | bytes 772
  0.0 13.6 %copy-start.3 = (s32[4096]{0:T(1024)S(1)}, s32[4096]{0:T(1024)}, u32[]{:S(2)}) copy-start(s32[4096]{0:T(1024)} %param.13) | copy-start | bytes 49156
  3.0 18.3 %all-to-all-start = ((bf16[128,32,32]{0,2,1:T(8,128)(2,1)}), bf16[128,32,32]{0,2,1:T(8,128)(2,1)S(1)}, u32[]{:S(2)}, u32[]{:S(2)}) async-start(bf16[128,32,32]{0,2,1:T(8,128)(2,1)} %bitcast.2), calls=%async_computation | async-start | bytes 524288 | tf_op jit(solution)/shard_map/all_to_all | solution.py:91
  13.6 2.4 %copy-start.1 = (s32[64,64]{1,0:T(8,128)}, s32[64,64]{1,0:T(8,128)S(1)}, u32[]{:S(2)}) copy-start(s32[64,64]{1,0:T(8,128)S(1)} %reshape.48.doc_ref) | copy-start | bytes 49156
  35.5 6.9 %copy-start.2 = (bf16[128,512]{1,0:T(8,128)(2,1)S(1)}, bf16[128,512]{1,0:T(8,128)(2,1)}, u32[]{:S(2)}) copy-start(bf16[128,512]{1,0:T(8,128)(2,1)} %param.10) | copy-start | bytes 393220
  38.4 11.4 %all-to-all-start.1 = ((bf16[32,128,16]{1,2,0:T(8,128)(2,1)}), bf16[32,128,16]{1,2,0:T(8,128)(2,1)S(1)}, u32[]{:S(2)}, u32[]{:S(2)}) async-start(bf16[32,128,16]{1,2,0:T(8,128)(2,1)} %copy_bitcast_fusion), calls=%async_computation.1 | async-start | bytes 262144 | tf_op jit(solution)/shard_map/all_to_all | solution.py:98
  50.2 7.9 %collective-permute-start = (bf16[128,512]{1,0:T(8,128)(2,1)S(1)}, bf16[128,512]{1,0:T(8,128)(2,1)S(1)}, u32[]{:S(2)}, u32[]{:S(2)}) collective-permute-start(bf16[128,512]{1,0:T(8,128)(2,1)S(1)} %convolution_convert_fusion.2), channel_id=1, source_target_pairs={{0,1},{1,2},{2,3},{3,0},{4,5},{5,6},{6,7},{7,4},{8,9},{9,10},{10,1... | collective-permute-start | bytes 393224 | tf_op jit(solution)/shard_map/ppermute | solution.py:109
  56.0 5.6 %collective-permute-start.1 = (bf16[128,512]{1,0:T(8,128)(2,1)S(1)}, bf16[128,512]{1,0:T(8,128)(2,1)S(1)}, u32[]{:S(2)}, u32[]{:S(2)}) collective-permute-start(bf16[128,512]{1,0:T(8,128)(2,1)S(1)} %convolution_convert_fusion.1), channel_id=1, source_target_pairs={{0,2},{1,3},{2,0},{3,1},{4,6},{5,7},{6,4},{7,5},{8,10},{9,11},{10,... | collective-permute-start | bytes 393224 | tf_op jit(solution)/shard_map/ppermute | solution.py:109
  56.7 6.1 %collective-permute-start.2 = (bf16[128,512]{1,0:T(8,128)(2,1)S(1)}, bf16[128,512]{1,0:T(8,128)(2,1)S(1)}, u32[]{:S(2)}, u32[]{:S(2)}) collective-permute-start(bf16[128,512]{1,0:T(8,128)(2,1)S(1)} %convolution_convert_fusion), channel_id=1, source_target_pairs={{0,3},{1,0},{2,1},{3,2},{4,7},{5,4},{6,5},{7,6},{8,11},{9,8},{10,9... | collective-permute-start | bytes 393224 | tf_op jit(solution)/shard_map/ppermute | solution.py:109

commit v2 on v1

--- a/solution.py
+++ b/solution.py
@@ -12,16 +12,15 @@
 CHANNELS_PER_STEP = 4
 
 
-def conv_kernel(bias_ref, f_ref, x_ref, doc_ref, mz_ref, y_ref):
+def conv_kernel(bias_ref, f_ref, x_ref, doc_ref, mask_ref, y_ref):
     blocks, span = x_ref.shape[1], x_ref.shape[2]
     seq = blocks * span
     lanes = 2 * span
     docs = doc_ref[...]
-    lead = docs[:, 0:1]
-    last = docs[:, span - 1 : span]
+    lead = docs[:, span - 1 : span]
     lead_rows = docs == lead
-    last_rows = (docs == last) & (docs != lead)
     doc_rows = [docs == doc for doc in range(DOC_COUNT)]
+    contract = (((1,), (1,)), ((), ()))
     for k in range(x_ref.shape[0]):
         channel = pl.program_id(0) * x_ref.shape[0] + k
         frow = f_ref[k].astype(jnp.float32)
@@ -29,19 +28,21 @@
         fb = jnp.broadcast_to(frow, (span, seq + lanes))
         tt = pltpu.roll(fb, 0, 1, stride=1, stride_axis=0)[:, :seq].astype(jnp.bfloat16)
         x = x_ref[k]
+        xf = x.astype(jnp.float32)
+        pair = jnp.concatenate([xf, pltpu.roll(xf, 1, 0)], axis=1)
+        src = jnp.concatenate(
+            [pair] + [pltpu.roll(pair, 2 * p, 0) for p in range(1, seq // lanes)], axis=1
+        )
+        src = (src * mask_ref[...]).astype(jnp.bfloat16)
+        y = lax.dot_general(src, tt, contract, preferred_element_type=jnp.float32)
+        y = jnp.where(lead_rows, y, 0.0)
         zero = jnp.zeros_like(x)
-        z_lead = jnp.dot(jnp.where(lead_rows, x, zero), tt, preferred_element_type=jnp.float32)
-        z_last = jnp.dot(jnp.where(last_rows, x, zero), tt, preferred_element_type=jnp.float32)
-        zm = z_lead * mz_ref[0] + z_last * mz_ref[1]
-        acc = zm[:, :lanes]
-        for pair in range(1, seq // lanes):
-            acc = acc + pltpu.roll(zm[:, pair * lanes : (pair + 1) * lanes], 2 * pair, 0)
-        y = acc[:, :span] + pltpu.roll(acc[:, span:], 1, 0)
         planes = jnp.concatenate([jnp.where(rows, x, zero) for rows in doc_rows], axis=0)
-        local = jnp.dot(planes, tt[:, :span], preferred_element_type=jnp.float32)
+        local = lax.dot_general(planes, tt[:, :span], contract, preferred_element_type=jnp.float32)
         for doc in range(DOC_COUNT):
-            y = y + jnp.where(doc_rows[doc], local[doc * blocks : (doc + 1) * blocks], 0.0)
-        y = y + bias_ref[channel] * x.astype(jnp.float32)
+            rows = doc_rows[doc] & (lead != doc)
+            y = y + jnp.where(rows, local[doc * blocks : (doc + 1) * blocks], 0.0)
+        y = y + bias_ref[channel] * xf
         y_ref[k] = y.astype(y_ref.dtype)
 
 
@@ -50,13 +51,15 @@
     span = SPAN
     blocks = seq // span
     step = CHANNELS_PER_STEP
-    xb = x_cm.reshape(chans, blocks, span)
+    xb = x_cm.reshape(chans, blocks, span)[:, :, ::-1]
     docb = doc_ids.reshape(blocks, span)
-    ends = jnp.sum(doc_ids[None, None, :] <= jnp.stack([docb[:, 0], docb[:, -1]])[:, :, None], axis=2)
-    rel = lax.broadcasted_iota(jnp.int32, (blocks, seq), 1)
-    pos = rel + span * lax.broadcasted_iota(jnp.int32, (blocks, seq), 0)
-    mz = ((rel >= span)[None] & (pos[None] < ends[:, :, None])).astype(jnp.float32)
-    return pl.pallas_call(
+    starts = jnp.sum(doc_ids[None, :] < docb[:, :1], axis=1)
+    lag = lax.broadcasted_iota(jnp.int32, (blocks, blocks, span), 1)
+    tgt = lax.broadcasted_iota(jnp.int32, (blocks, blocks, span), 0)
+    off = span - 1 - lax.broadcasted_iota(jnp.int32, (blocks, blocks, span), 2)
+    mask = (tgt >= lag) & (span * (tgt - lag) + off >= starts[:, None, None])
+    mask = mask.astype(jnp.float32).reshape(blocks, seq)
+    out = pl.pallas_call(
         conv_kernel,
         grid=(chans // step,),
         in_specs=[
@@ -64,11 +67,12 @@
             pl.BlockSpec((step, 1, seq), lambda c: (c, 0, 0)),
             pl.BlockSpec((step, blocks, span), lambda c: (c, 0, 0)),
             pl.BlockSpec((blocks, span), lambda c: (0, 0)),
-            pl.BlockSpec((2, blocks, seq), lambda c: (0, 0, 0)),
+            pl.BlockSpec((blocks, seq), lambda c: (0, 0)),
         ],
         out_specs=pl.BlockSpec((step, blocks, span), lambda c: (c, 0, 0)),
         out_shape=jax.ShapeDtypeStruct((chans, blocks, span), jnp.bfloat16),
-    )(bias_cm, f_cm.reshape(chans, 1, seq), xb, docb, mz)
+    )(bias_cm, f_cm.reshape(chans, 1, seq), xb, docb[:, ::-1], mask)
+    return out[:, :, ::-1]
 
 
 def body(signal, gate, filt, bias, doc_ids, block_perm, out_weight):

time: 64.1 us -> 60.3 us (0.941)
  Pallas kernels: 11.3 us -> 7.26 us
  local copies, waits for them, and re-layouts: 10.2 us -> 12 us
  other arithmetic: 3.27 us -> 1.9 us
    pallas_call x1, Pallas kernels: 11.3 us -> 7.26 us  [pallas_conv(): pl.pallas_call(conv_kernel, grid=(chans // step,), in_specs=[pl.BlockSpec...]
    rev x0 -> x4, local copies, waits for them, and re-layouts: none -> 2.86 us  [the longest x2 1.32 us: pallas_conv(): return out[:, :, ::-1]]
    pallas_call x1 -> x0, local copies, waits for them, and re-layouts: 1.16 us -> none  [pallas_conv(): pl.pallas_call(conv_kernel, grid=(chans // step,), in_specs=[pl.BlockSpec...]
    select_n x2, other arithmetic: 0.8 us -> 0.1 us  [slots_to_natural(): jnp.take(a.reshape(per_dev, blocks, span), inverse, axis=1)]
    unnamed x13 -> x11, local copies, waits for them, and re-layouts: 2.33 us -> 2.33 us
  transfers between devices with their start and end apart: 5 -> 5, of which waited for: 5 -> 5; matrix products, arithmetic and copies ran while one was open for 8% -> 9% of each run, Pallas kernels for 0% -> 0%
where the time goes in v2:
time: 60.3 us; the launch traced here: 59.9 us
  starting transfers between devices  19.7 us (33%)
  waiting for transfers between devices  17.2 us (29%)
  local copies, waits for them, and re-layouts  12 us (20%)
  Pallas kernels  7.26 us (12%)
  other arithmetic  1.9 us (3%)
  matrix products  1.68 us (3%)
    all_to_all x1, starting transfers between devices, body(): arrived = lax.all_to_all(packed, 'ctx', 1, 0, tiled=True).T  9.71 us
    all_to_all x1, waiting for transfers between devices, body(): pre_local = lax.all_to_all(pre_slots, 'ctx', 0, 1, tiled=True)  7.39 us
    pallas_call x1, Pallas kernels, pallas_conv(): pl.pallas_call(conv_kernel, grid=(chans // step,), in_specs=[pl.BlockSpec...  7.26 us
    ppermute x3, starting transfers between devices, body(): lax.ppermute(part.astype(jnp.bfloat16), 'tp', pairs).astype(jnp.float32)  6 us
    ppermute x3, waiting for transfers between devices, body(): lax.ppermute(part.astype(jnp.bfloat16), 'tp', pairs).astype(jnp.float32)  5.99 us
    all_to_all x1, starting transfers between devices, body(): pre_local = lax.all_to_all(pre_slots, 'ctx', 0, 1, tiled=True)  3.93 us
    all_to_all x1, waiting for transfers between devices, body(): arrived = lax.all_to_all(packed, 'ctx', 1, 0, tiled=True).T  3.81 us
    unnamed x11, local copies, waits for them, and re-layouts  2.33 us
  transfers between devices with their start and end apart: 5, of which 5 were waited for; matrix products, arithmetic and copies ran while one was open for 9% of the time, Pallas kernels for 0%

profile of v2, /device:TPU:1, one launch (start us, length us, event | category | flops | bytes accessed | tf_op | source)
XLA Modules:
  0.0 59.9 jit_solution(17907103806711240283)
XLA Ops:
  0.0 1.2 %copy.49 = bf16[128,512]{0,1:T(8,128)(2,1)S(1)} copy(bf16[128,512]{1,0:T(8,128)(2,1)} %param.9) | data formatting | bytes 262144 | tf_op args[0]
  1.2 1.0 %copy.50 = bf16[128,512]{0,1:T(8,128)(2,1)S(1)} copy(bf16[128,512]{1,0:T(8,128)(2,1)} %param.11) | data formatting | bytes 262144 | tf_op args[2]
  2.3 0.7 %copy.51 = bf16[128,32,2,16]{0,3,2,1:T(8,128)(2,1)} copy(bf16[128,32,2,16]{0,3,1,2:T(8,128)(2,1)S(1)} %pad_maximum_fusion) | data formatting | bytes 524288 | tf_op jit(solution)/shard_map/stack | solution.py:92
  3.0 9.7 %all-to-all-start = ((bf16[128,32,32]{0,2,1:T(8,128)(2,1)}), bf16[128,32,32]{0,2,1:T(8,128)(2,1)S(1)}, u32[]{:S(2)}, u32[]{:S(2)}) async-start(bf16[128,32,32]{0,2,1:T(8,128)(2,1)} %bitcast.2), calls=%async_computation | async-start | bytes 524288 | tf_op jit(solution)/shard_map/all_to_all | solution.py:95
  12.7 0.8 %scatter_custom_fusion = s32[64]{0:T(128)S(1)} fusion(s32[64]{0:T(128)S(1)} %compare_select_fusion, s32[64]{0:T(128)S(1)} %iota.40, s32[]{:T(128)} %constant.52.clone.1), kind=kCustom, calls=%fused_computation.38 | custom fusion | bytes 260 | tf_op jit(solution)/shard_map/scatter | solution.py:87
  14.2 1.3 %fusion.1.mask_ref = f32[64,4096]{1,0:T(8,128)} fusion(s32[64]{0:T(128)S(1)} %convert_reduce_fusion, s32[4096]{0:T(1024)S(1)} %iota.48, s32[4096]{0:T(1024)S(1)} %iota.43), kind=kLoop, calls=%fused_computation.10 | loop fusion | flops 1835008 | bytes 1081600 | tf_op jit(solution)/shard_map/convert_element_type | solution.py:61
  15.5 0.7 %rev.10.doc_ref = s32[64,64]{1,0:T(8,128)} reverse(s32[64,64]{1,0:T(8,128)S(1)} %reshape.36), dimensions={1} | reverse | bytes 32768 | tf_op jit(solution)/shard_map/rev | solution.py:74
  16.2 1.3 %dynamic_slice.15.bias_ref = f32[16]{0:T(128)} dynamic-slice(f32[512]{0:T(512)} %param.12, s32[]{:T(128)S(6)} %select_n.44), dynamic_slice_sizes={16} | dynamic-slice | bytes 132 | tf_op jit(solution)/shard_map/dynamic_slice | solution.py:98
  17.4 3.8 %all-to-all-done = bf16[128,32,32]{0,2,1:T(8,128)(2,1)S(1)} async-done(((bf16[128,32,32]{0,2,1:T(8,128)(2,1)}), bf16[128,32,32]{0,2,1:T(8,128)(2,1)S(1)}, u32[]{:S(2)}, u32[]{:S(2)}) %all-to-all-start) | async-done | bytes 262176 | tf_op jit(solution)/shard_map/all_to_all | solution.py:95
  21.7 0.6 %gather_fusion = bf16[64,16,64]{2,1,0:T(8,128)(2,1)S(1)} fusion(bf16[16,64,64]{2,0,1:T(8,128)(2,1)S(1)} %copy.53, s32[1024]{0:T(1024)S(1)} %pad_clamp_fusion.1), kind=kCustom, calls=%fused_computation.clone | custom fusion | bytes 262400 | tf_op jit(solution)/shard_map/jit(_take)/gather | solution.py:90
  22.5 0.9 %rev.9.x_ref = bf16[16,64,64]{2,1,0:T(8,128)(2,1)} reverse(bf16[16,64,64]{2,1,0:T(8,128)(2,1)S(1)} %fusion.8), dimensions={2} | reverse | bytes 262144 | tf_op jit(solution)/shard_map/rev | solution.py:54
  23.3 0.9 %copy.55.f_ref = bf16[16,1,4096]{2,1,0:T(2,128)(2,1)} copy(bf16[16,1,4096]{2,0,1:T(8,128)(2,1)S(1)} %get-tuple-element.7) | data formatting | bytes 262144 | tf_op jit(solution)/shard_map/reshape | solution.py:74
  24.2 7.3 %shard_map.73 = bf16[16,64,64]{2,1,0:T(8,128)(2,1)} custom-call(f32[16]{0:T(128)} %dynamic_slice.15.bias_ref, bf16[16,1,4096]{2,1,0:T(2,128)(2,1)} %copy.55.f_ref, bf16[16,64,64]{2,1,0:T(8,128)(2,1)} %rev.9.x_ref, s32[64,64]{1,0:T(8,128)} %rev.10.doc_ref, f32[64,4096]{1,0:T(8,128)} %fusion.1.mask_ref), custom_call_target="tpu_custom_call" | custom-call | tf_op jit(solution)/shard_map/pallas_call | solution.py:62
  31.5 1.1 %rev.11 = bf16[16,64,64]{2,1,0:T(8,128)(2,1)S(1)} reverse(bf16[16,64,64]{2,1,0:T(8,128)(2,1)} %shard_map.73), dimensions={2} | reverse | bytes 262144 | tf_op jit(solution)/shard_map/rev | solution.py:75
  32.8 0.6 %gather_fusion.1 = bf16[64,16,64]{2,1,0:T(8,128)(2,1)S(1)} fusion(bf16[16,64,64]{2,0,1:T(8,128)(2,1)S(1)} %copy.56, s32[1024]{0:T(1024)S(1)} %pad_clamp_fusion), kind=kCustom, calls=%fused_computation.1.clone | custom fusion | bytes 262400 | tf_op jit(solution)/shard_map/jit(_take)/gather | solution.py:100
  34.0 0.7 %copy_bitcast_fusion = bf16[32,128,16]{1,2,0:T(8,128)(2,1)} fusion(bf16[16,4096]{1,0:T(8,128)(2,1)S(1)} %reshape.37), kind=kLoop, calls=%fused_computation.24 | loop fusion | bytes 262144 | tf_op jit(solution)/shard_map/all_to_all | solution.py:102
  34.7 3.9 %all-to-all-start.1 = ((bf16[32,128,16]{1,2,0:T(8,128)(2,1)}), bf16[32,128,16]{1,2,0:T(8,128)(2,1)S(1)}, u32[]{:S(2)}, u32[]{:S(2)}) async-start(bf16[32,128,16]{1,2,0:T(8,128)(2,1)} %copy_bitcast_fusion), calls=%async_computation.1 | async-start | bytes 262144 | tf_op jit(solution)/shard_map/all_to_all | solution.py:102
  38.8 7.4 %all-to-all-done.1 = bf16[32,128,16]{1,2,0:T(8,128)(2,1)S(1)} async-done(((bf16[32,128,16]{1,2,0:T(8,128)(2,1)}), bf16[32,128,16]{1,2,0:T(8,128)(2,1)S(1)}, u32[]{:S(2)}, u32[]{:S(2)}) %all-to-all-start.1) | async-done | bytes 131104 | tf_op jit(solution)/shard_map/all_to_all | solution.py:102
  46.5 5.4 %collective-permute-start = (bf16[128,512]{1,0:T(8,128)(2,1)S(1)}, bf16[128,512]{1,0:T(8,128)(2,1)S(1)}, u32[]{:S(2)}, u32[]{:S(2)}) collective-permute-start(bf16[128,512]{1,0:T(8,128)(2,1)S(1)} %convolution_convert_fusion.2), channel_id=1, source_target_pairs={{0,1},{1,2},{2,3},{3,0},{4,5},{5,6},{6,7},{7,4},{8,9},{9,10},{10,1... | collective-permute-start | bytes 393224 | tf_op jit(solution)/shard_map/ppermute | solution.py:113
  52.2 0.4 collective-permute-start.1
  53.0 1.3 %collective-permute-done = bf16[128,512]{1,0:T(8,128)(2,1)S(1)} collective-permute-done((bf16[128,512]{1,0:T(8,128)(2,1)S(1)}, bf16[128,512]{1,0:T(8,128)(2,1)S(1)}, u32[]{:S(2)}, u32[]{:S(2)}) %collective-permute-start) | collective-permute-done | bytes 131104 | tf_op jit(solution)/shard_map/ppermute | solution.py:113
  54.3 3.4 %collective-permute-done.1 = bf16[128,512]{1,0:T(8,128)(2,1)S(1)} collective-permute-done((bf16[128,512]{1,0:T(8,128)(2,1)S(1)}, bf16[128,512]{1,0:T(8,128)(2,1)S(1)}, u32[]{:S(2)}, u32[]{:S(2)}) %collective-permute-start.1) | collective-permute-done | bytes 131104 | tf_op jit(solution)/shard_map/ppermute | solution.py:113
  57.7 1.2 %collective-permute-done.2 = bf16[128,512]{1,0:T(8,128)(2,1)S(1)} collective-permute-done((bf16[128,512]{1,0:T(8,128)(2,1)S(1)}, bf16[128,512]{1,0:T(8,128)(2,1)S(1)}, u32[]{:S(2)}, u32[]{:S(2)}) %collective-permute-start.2) | collective-permute-done | bytes 131104 | tf_op jit(solution)/shard_map/ppermute | solution.py:113
  59.0 0.9 %add_convert_fusion = bf16[128,512]{1,0:T(8,128)(2,1)} fusion(bf16[128,512]{1,0:T(8,128)(2,1)S(1)} %collective-permute-done.2, bf16[128,512]{1,0:T(8,128)(2,1)S(1)} %collective-permute-done.1, bf16[128,512]{1,0:T(8,128)(2,1)S(1)} %collective-permute-done, bf16[128,512]{0,1:T(8,128)(2,1)S(1)} %fusion.7, bf16[512,2048]{1,0:T(8,128)(2,1)S(1)} %copy-done, ...), kind=kOutput, calls=%fused_computation.23 | convolution fusion | flops 67567616 | bytes 1179652 | tf_op jit(solution)/shard_map/dot_general | solution.py:110
  (38 shorter events, 2.9 us)
Async XLA Ops:
  0.0 46.2 %copy-start = (bf16[512,2048]{1,0:T(8,128)(2,1)S(1)}, bf16[512,2048]{1,0:T(8,128)(2,1)}, u32[]{:S(2)}) copy-start(bf16[512,2048]{1,0:T(8,128)(2,1)} %param.15) | copy-start | bytes 6291460
  0.0 12.7 %copy-start.3 = (s32[64]{0:T(128)S(1)}, s32[64]{0:T(128)}, u32[]{:S(2)}) copy-start(s32[64]{0:T(128)} %param.14) | copy-start | bytes 772
  0.0 13.5 %copy-start.2 = (s32[4096]{0:T(1024)S(1)}, s32[4096]{0:T(1024)}, u32[]{:S(2)}) copy-start(s32[4096]{0:T(1024)} %param.13) | copy-start | bytes 49156
  3.0 18.3 %all-to-all-start = ((bf16[128,32,32]{0,2,1:T(8,128)(2,1)}), bf16[128,32,32]{0,2,1:T(8,128)(2,1)S(1)}, u32[]{:S(2)}, u32[]{:S(2)}) async-start(bf16[128,32,32]{0,2,1:T(8,128)(2,1)} %bitcast.2), calls=%async_computation | async-start | bytes 524288 | tf_op jit(solution)/shard_map/all_to_all | solution.py:95
  31.5 7.1 %copy-start.1 = (bf16[128,512]{1,0:T(8,128)(2,1)S(1)}, bf16[128,512]{1,0:T(8,128)(2,1)}, u32[]{:S(2)}) copy-start(bf16[128,512]{1,0:T(8,128)(2,1)} %param.10) | copy-start | bytes 393220
  34.7 11.5 %all-to-all-start.1 = ((bf16[32,128,16]{1,2,0:T(8,128)(2,1)}), bf16[32,128,16]{1,2,0:T(8,128)(2,1)S(1)}, u32[]{:S(2)}, u32[]{:S(2)}) async-start(bf16[32,128,16]{1,2,0:T(8,128)(2,1)} %copy_bitcast_fusion), calls=%async_computation.1 | async-start | bytes 262144 | tf_op jit(solution)/shard_map/all_to_all | solution.py:102
  46.5 7.8 %collective-permute-start = (bf16[128,512]{1,0:T(8,128)(2,1)S(1)}, bf16[128,512]{1,0:T(8,128)(2,1)S(1)}, u32[]{:S(2)}, u32[]{:S(2)}) collective-permute-start(bf16[128,512]{1,0:T(8,128)(2,1)S(1)} %convolution_convert_fusion.2), channel_id=1, source_target_pairs={{0,1},{1,2},{2,3},{3,0},{4,5},{5,6},{6,7},{7,4},{8,9},{9,10},{10,1... | collective-permute-start | bytes 393224 | tf_op jit(solution)/shard_map/ppermute | solution.py:113
  52.2 5.6 %collective-permute-start.1 = (bf16[128,512]{1,0:T(8,128)(2,1)S(1)}, bf16[128,512]{1,0:T(8,128)(2,1)S(1)}, u32[]{:S(2)}, u32[]{:S(2)}) collective-permute-start(bf16[128,512]{1,0:T(8,128)(2,1)S(1)} %convolution_convert_fusion.1), channel_id=1, source_target_pairs={{0,2},{1,3},{2,0},{3,1},{4,6},{5,7},{6,4},{7,5},{8,10},{9,11},{10,... | collective-permute-start | bytes 393224 | tf_op jit(solution)/shard_map/ppermute | solution.py:113
  52.9 6.1 %collective-permute-start.2 = (bf16[128,512]{1,0:T(8,128)(2,1)S(1)}, bf16[128,512]{1,0:T(8,128)(2,1)S(1)}, u32[]{:S(2)}, u32[]{:S(2)}) collective-permute-start(bf16[128,512]{1,0:T(8,128)(2,1)S(1)} %convolution_convert_fusion), channel_id=1, source_target_pairs={{0,3},{1,0},{2,1},{3,2},{4,7},{5,4},{6,5},{7,6},{8,11},{9,8},{10,9... | collective-permute-start | bytes 393224 | tf_op jit(solution)/shard_map/ppermute | solution.py:113

commit v3 on v2

--- a/solution.py
+++ b/solution.py
@@ -12,7 +12,11 @@
 CHANNELS_PER_STEP = 4
 
 
-def conv_kernel(bias_ref, f_ref, x_ref, doc_ref, mask_ref, y_ref):
+def exact_dot(a, b):
+    return jnp.dot(a, b, preferred_element_type=jnp.float32).astype(a.dtype)
+
+
+def conv_kernel(bias_ref, f_ref, x_ref, doc_ref, mask_ref, perm_ref, y_ref):
     blocks, span = x_ref.shape[1], x_ref.shape[2]
     seq = blocks * span
     lanes = 2 * span
@@ -27,7 +31,7 @@
         frow = jnp.concatenate([frow, jnp.zeros((1, lanes), jnp.float32)], axis=1)
         fb = jnp.broadcast_to(frow, (span, seq + lanes))
         tt = pltpu.roll(fb, 0, 1, stride=1, stride_axis=0)[:, :seq].astype(jnp.bfloat16)
-        x = x_ref[k]
+        x = exact_dot(perm_ref[0], exact_dot(x_ref[k], perm_ref[2]))
         xf = x.astype(jnp.float32)
         pair = jnp.concatenate([xf, pltpu.roll(xf, 1, 0)], axis=1)
         src = jnp.concatenate(
@@ -43,15 +47,19 @@
             rows = doc_rows[doc] & (lead != doc)
             y = y + jnp.where(rows, local[doc * blocks : (doc + 1) * blocks], 0.0)
         y = y + bias_ref[channel] * xf
-        y_ref[k] = y.astype(y_ref.dtype)
+        y = y.astype(y_ref.dtype)
+        y_ref[k] = exact_dot(perm_ref[1], exact_dot(y, perm_ref[2]))
 
 
-def pallas_conv(x_cm, f_cm, doc_ids, bias_cm):
-    chans, seq = x_cm.shape
+def pallas_conv(x_slots, f_cm, doc_ids, bias_cm, block_perm):
+    chans, seq = x_slots.shape
     span = SPAN
     blocks = seq // span
     step = CHANNELS_PER_STEP
-    xb = x_cm.reshape(chans, blocks, span)[:, :, ::-1]
+    xb = x_slots.reshape(chans, blocks, span)
+    to_seq = (block_perm[None, :] == jnp.arange(blocks, dtype=jnp.int32)[:, None]).astype(x_slots.dtype)
+    flip = jnp.eye(span, dtype=x_slots.dtype)[::-1]
+    perms = jnp.stack([to_seq, to_seq.T, flip])
     docb = doc_ids.reshape(blocks, span)
     starts = jnp.sum(doc_ids[None, :] < docb[:, :1], axis=1)
     lag = lax.broadcasted_iota(jnp.int32, (blocks, blocks, span), 1)
@@ -68,11 +76,12 @@
             pl.BlockSpec((step, blocks, span), lambda c: (c, 0, 0)),
             pl.BlockSpec((blocks, span), lambda c: (0, 0)),
             pl.BlockSpec((blocks, seq), lambda c: (0, 0)),
+            pl.BlockSpec((3, blocks, span), lambda c: (0, 0, 0)),
         ],
         out_specs=pl.BlockSpec((step, blocks, span), lambda c: (c, 0, 0)),
         out_shape=jax.ShapeDtypeStruct((chans, blocks, span), jnp.bfloat16),
-    )(bias_cm, f_cm.reshape(chans, 1, seq), xb, docb[:, ::-1], mask)
-    return out[:, :, ::-1]
+    )(bias_cm, f_cm.reshape(chans, 1, seq), xb, docb[:, ::-1], mask, perms)
+    return out
 
 
 def body(signal, gate, filt, bias, doc_ids, block_perm, out_weight):
@@ -84,20 +93,14 @@
     per_dev = chans // n_ctx
     ctx_index = lax.axis_index("ctx")
 
-    inverse = jnp.zeros((blocks,), jnp.int32).at[block_perm].set(jnp.arange(blocks, dtype=jnp.int32))
-
-    def slots_to_natural(a):
-        return jnp.take(a.reshape(per_dev, blocks, span), inverse, axis=1).reshape(per_dev, seq)
-
     packed = jnp.stack(
         [a.reshape(rows, n_ctx, per_dev) for a in (signal, filt)], axis=2
     ).reshape(rows, n_ctx * 2 * per_dev)
     arrived = lax.all_to_all(packed, "ctx", 1, 0, tiled=True).T
-    x_cm = slots_to_natural(arrived[:per_dev])
+    x_slots = arrived[:per_dev]
     f_cm = arrived[per_dev:]
     bias_cm = lax.dynamic_slice_in_dim(bias, ctx_index * per_dev, per_dev)
-    pre = pallas_conv(x_cm, f_cm, doc_ids, bias_cm)
-    pre_slots = jnp.take(pre, block_perm, axis=1)
+    pre_slots = pallas_conv(x_slots, f_cm, doc_ids, bias_cm, block_perm)
     pre_slots = pre_slots.reshape(per_dev, seq).T
     pre_local = lax.all_to_all(pre_slots, "ctx", 0, 1, tiled=True)
     gated_local = (gate.astype(jnp.float32) * pre_local.astype(jnp.float32)).astype(jnp.bfloat16)

time: 60.3 us -> 66.8 us (1.11)
  Pallas kernels: 7.26 us -> 16 us
  local copies, waits for them, and re-layouts: 12 us -> 9.22 us
    pallas_call x1, Pallas kernels: 7.26 us -> 16 us  [pallas_conv(): pl.pallas_call(conv_kernel, grid=(chans // step,), in_specs=[pl.BlockSpec...]
    rev x3 -> x1, local copies, waits for them, and re-layouts: 2.17 us -> 0.02 us  [pallas_conv(): flip = jnp.eye(span, dtype=x_slots.dtype)[::-1]]
    gather x2 -> x0, local copies, waits for them, and re-layouts: 1.27 us -> none  [the longest x1 0.63 us: slots_to_natural(): jnp.take(a.reshape(per_dev, blocks, span), inverse, axis=1)]
    reshape x1, local copies, waits for them, and re-layouts: 0.27 us -> 1.22 us  [body(): pre_slots = pre_slots.reshape(per_dev, seq).T]
    scatter x1 -> x0, local copies, waits for them, and re-layouts: 0.77 us -> none  [body(): jnp.zeros((blocks,), jnp.int32).at[block_perm]]
  transfers between devices with their start and end apart: 5 -> 5, of which waited for: 5 -> 5; matrix products, arithmetic and copies ran while one was open for 9% -> 8% of each run, Pallas kernels for 0% -> 0%
where the time goes in v3:
time: 66.8 us; the launch traced here: 66.4 us
  starting transfers between devices  19.7 us (29%)
  waiting for transfers between devices  17.3 us (26%)
  Pallas kernels  16 us (24%)
  local copies, waits for them, and re-layouts  9.22 us (14%)
  other arithmetic  2.34 us (4%)
  matrix products  1.68 us (3%)
    pallas_call x1, Pallas kernels, pallas_conv(): pl.pallas_call(conv_kernel, grid=(chans // step,), in_specs=[pl.BlockSpec...  16 us
    all_to_all x1, starting transfers between devices, body(): arrived = lax.all_to_all(packed, 'ctx', 1, 0, tiled=True).T  9.71 us
    all_to_all x1, waiting for transfers between devices, body(): pre_local = lax.all_to_all(pre_slots, 'ctx', 0, 1, tiled=True)  7.38 us
    ppermute x3, starting transfers between devices, body(): lax.ppermute(part.astype(jnp.bfloat16), 'tp', pairs).astype(jnp.float32)  6.09 us
    ppermute x3, waiting for transfers between devices, body(): lax.ppermute(part.astype(jnp.bfloat16), 'tp', pairs).astype(jnp.float32)  5.99 us
    all_to_all x1, waiting for transfers between devices, body(): arrived = lax.all_to_all(packed, 'ctx', 1, 0, tiled=True).T  3.9 us
    all_to_all x1, starting transfers between devices, body(): pre_local = lax.all_to_all(pre_slots, 'ctx', 0, 1, tiled=True)  3.86 us
    unnamed x11, local copies, waits for them, and re-layouts  2.33 us
  transfers between devices with their start and end apart: 5, of which 5 were waited for; matrix products, arithmetic and copies ran while one was open for 8% of the time, Pallas kernels for 0%

profile of v3, /device:TPU:1, one launch (start us, length us, event | category | flops | bytes accessed | tf_op | source)
XLA Modules:
  0.0 66.4 jit_solution(11407112628851815821)
XLA Ops:
  0.0 1.2 %copy.35 = bf16[128,512]{0,1:T(8,128)(2,1)S(1)} copy(bf16[128,512]{1,0:T(8,128)(2,1)} %param.7) | data formatting | bytes 262144 | tf_op args[0]
  1.2 1.0 %copy.36 = bf16[128,512]{0,1:T(8,128)(2,1)S(1)} copy(bf16[128,512]{1,0:T(8,128)(2,1)} %param.9) | data formatting | bytes 262144 | tf_op args[2]
  2.3 0.7 %copy.37 = bf16[128,32,2,16]{0,3,2,1:T(8,128)(2,1)} copy(bf16[128,32,2,16]{0,3,1,2:T(8,128)(2,1)S(1)} %pad_maximum_fusion) | data formatting | bytes 524288 | tf_op jit(solution)/shard_map/stack | solution.py:96
  3.0 9.7 %all-to-all-start = ((bf16[128,32,32]{0,2,1:T(8,128)(2,1)}), bf16[128,32,32]{0,2,1:T(8,128)(2,1)S(1)}, u32[]{:S(2)}, u32[]{:S(2)}) async-start(bf16[128,32,32]{0,2,1:T(8,128)(2,1)} %bitcast.2), calls=%async_computation | async-start | bytes 524288 | tf_op jit(solution)/shard_map/all_to_all | solution.py:99
  12.9 0.7 %rev.6.doc_ref = s32[64,64]{1,0:T(8,128)} reverse(s32[64,64]{1,0:T(8,128)S(1)} %reshape.94), dimensions={1} | reverse | bytes 32768 | tf_op jit(solution)/shard_map/rev | solution.py:83
  13.6 0.3 convert_reduce_fusion
  14.1 1.3 %dynamic_slice.15.bias_ref = f32[16]{0:T(128)} dynamic-slice(f32[512]{0:T(512)} %param.10, s32[]{:T(128)S(6)} %select_n.34), dynamic_slice_sizes={16} | dynamic-slice | bytes 132 | tf_op jit(solution)/shard_map/dynamic_slice | solution.py:102
  15.4 1.3 %fusion.1.mask_ref = f32[64,4096]{1,0:T(8,128)} fusion(s32[64]{0:T(128)S(1)} %convert_reduce_fusion, s32[4096]{0:T(1024)S(1)} %iota.64, s32[4096]{0:T(1024)S(1)} %iota.59), kind=kLoop, calls=%fused_computation.7 | loop fusion | flops 1835008 | bytes 1081600 | tf_op jit(solution)/shard_map/convert_element_type | solution.py:69
  16.7 0.6 pad_maximum_fusion.1.perm_ref
  17.4 3.9 %all-to-all-done = bf16[128,32,32]{0,2,1:T(8,128)(2,1)S(1)} async-done(((bf16[128,32,32]{0,2,1:T(8,128)(2,1)}), bf16[128,32,32]{0,2,1:T(8,128)(2,1)S(1)}, u32[]{:S(2)}, u32[]{:S(2)}) %all-to-all-start) | async-done | bytes 262176 | tf_op jit(solution)/shard_map/all_to_all | solution.py:99
  21.3 0.9 %copy.39.f_ref = bf16[16,1,4096]{2,1,0:T(2,128)(2,1)} copy(bf16[16,1,4096]{2,0,1:T(8,128)(2,1)S(1)} %get-tuple-element.6) | data formatting | bytes 262144 | tf_op jit(solution)/shard_map/reshape | solution.py:83
  22.3 1.0 %reshape.93.x_ref = bf16[16,64,64]{2,1,0:T(8,128)(2,1)} reshape(bf16[16,4096]{1,0:T(8,128)(2,1)S(1)} %get-tuple-element.5) | data formatting | bytes 262144 | tf_op jit(solution)/shard_map/reshape | solution.py:59
  23.2 16.0 %shard_map.73 = bf16[16,64,64]{2,1,0:T(8,128)(2,1)} custom-call(f32[16]{0:T(128)} %dynamic_slice.15.bias_ref, bf16[16,1,4096]{2,1,0:T(2,128)(2,1)} %copy.39.f_ref, bf16[16,64,64]{2,1,0:T(8,128)(2,1)} %reshape.93.x_ref, s32[64,64]{1,0:T(8,128)} %rev.6.doc_ref, f32[64,4096]{1,0:T(8,128)} %fusion.1.mask_ref, bf16[3,64,64]{2,1,0:T(8,128)(2,1)} %pad_maximum_fusion.1.perm_ref), custom_call_target="tpu_custom_call" | custom-call | tf_op jit(solution)/shard_map/pallas_call | solution.py:70
  39.2 1.2 %reshape.95 = bf16[16,4096]{1,0:T(8,128)(2,1)S(1)} reshape(bf16[16,64,64]{2,1,0:T(8,128)(2,1)} %shard_map.73) | data formatting | bytes 262144 | tf_op jit(solution)/shard_map/reshape | solution.py:104
  40.4 0.7 %copy_bitcast_fusion = bf16[32,128,16]{1,2,0:T(8,128)(2,1)} fusion(bf16[16,4096]{1,0:T(8,128)(2,1)S(1)} %reshape.95), kind=kLoop, calls=%fused_computation.18 | loop fusion | bytes 262144 | tf_op jit(solution)/shard_map/all_to_all | solution.py:105
  41.1 3.9 %all-to-all-start.1 = ((bf16[32,128,16]{1,2,0:T(8,128)(2,1)}), bf16[32,128,16]{1,2,0:T(8,128)(2,1)S(1)}, u32[]{:S(2)}, u32[]{:S(2)}) async-start(bf16[32,128,16]{1,2,0:T(8,128)(2,1)} %copy_bitcast_fusion), calls=%async_computation.1 | async-start | bytes 262144 | tf_op jit(solution)/shard_map/all_to_all | solution.py:105
  45.2 7.4 %all-to-all-done.1 = bf16[32,128,16]{1,2,0:T(8,128)(2,1)S(1)} async-done(((bf16[32,128,16]{1,2,0:T(8,128)(2,1)}), bf16[32,128,16]{1,2,0:T(8,128)(2,1)S(1)}, u32[]{:S(2)}, u32[]{:S(2)}) %all-to-all-start.1) | async-done | bytes 131104 | tf_op jit(solution)/shard_map/all_to_all | solution.py:105
  52.6 0.2 convolution_convert_fusion.2
  52.9 5.5 %collective-permute-start = (bf16[128,512]{1,0:T(8,128)(2,1)S(1)}, bf16[128,512]{1,0:T(8,128)(2,1)S(1)}, u32[]{:S(2)}, u32[]{:S(2)}) collective-permute-start(bf16[128,512]{1,0:T(8,128)(2,1)S(1)} %convolution_convert_fusion.2), channel_id=1, source_target_pairs={{0,1},{1,2},{2,3},{3,0},{4,5},{5,6},{6,7},{7,4},{8,9},{9,10},{10,1... | collective-permute-start | bytes 393224 | tf_op jit(solution)/shard_map/ppermute | solution.py:116
  58.7 0.4 collective-permute-start.1
  59.5 1.3 %collective-permute-done = bf16[128,512]{1,0:T(8,128)(2,1)S(1)} collective-permute-done((bf16[128,512]{1,0:T(8,128)(2,1)S(1)}, bf16[128,512]{1,0:T(8,128)(2,1)S(1)}, u32[]{:S(2)}, u32[]{:S(2)}) %collective-permute-start) | collective-permute-done | bytes 131104 | tf_op jit(solution)/shard_map/ppermute | solution.py:116
  60.8 3.4 %collective-permute-done.1 = bf16[128,512]{1,0:T(8,128)(2,1)S(1)} collective-permute-done((bf16[128,512]{1,0:T(8,128)(2,1)S(1)}, bf16[128,512]{1,0:T(8,128)(2,1)S(1)}, u32[]{:S(2)}, u32[]{:S(2)}) %collective-permute-start.1) | collective-permute-done | bytes 131104 | tf_op jit(solution)/shard_map/ppermute | solution.py:116
  64.2 1.2 %collective-permute-done.2 = bf16[128,512]{1,0:T(8,128)(2,1)S(1)} collective-permute-done((bf16[128,512]{1,0:T(8,128)(2,1)S(1)}, bf16[128,512]{1,0:T(8,128)(2,1)S(1)}, u32[]{:S(2)}, u32[]{:S(2)}) %collective-permute-start.2) | collective-permute-done | bytes 131104 | tf_op jit(solution)/shard_map/ppermute | solution.py:116
  65.5 0.9 %add_convert_fusion = bf16[128,512]{1,0:T(8,128)(2,1)} fusion(bf16[128,512]{1,0:T(8,128)(2,1)S(1)} %collective-permute-done.2, bf16[128,512]{1,0:T(8,128)(2,1)S(1)} %collective-permute-done.1, bf16[128,512]{1,0:T(8,128)(2,1)S(1)} %collective-permute-done, bf16[128,512]{0,1:T(8,128)(2,1)S(1)} %fusion.7, bf16[512,2048]{1,0:T(8,128)(2,1)S(1)} %copy-done, ...), kind=kOutput, calls=%fused_computation.17 | convolution fusion | flops 67567616 | bytes 1179652 | tf_op jit(solution)/shard_map/dot_general | solution.py:113
  (26 shorter events, 1.3 us)
Async XLA Ops:
  0.0 52.6 %copy-start = (bf16[512,2048]{1,0:T(8,128)(2,1)S(1)}, bf16[512,2048]{1,0:T(8,128)(2,1)}, u32[]{:S(2)}) copy-start(bf16[512,2048]{1,0:T(8,128)(2,1)} %param.13) | copy-start | bytes 6291460
  0.0 12.7 %copy-start.2 = (s32[4096]{0:T(1024)S(1)}, s32[4096]{0:T(1024)}, u32[]{:S(2)}) copy-start(s32[4096]{0:T(1024)} %param.11) | copy-start | bytes 49156
  0.0 16.6 %copy-start.3 = (s32[64]{0:T(128)S(1)}, s32[64]{0:T(128)}, u32[]{:S(2)}) copy-start(s32[64]{0:T(128)} %param.12) | copy-start | bytes 772
  3.0 18.3 %all-to-all-start = ((bf16[128,32,32]{0,2,1:T(8,128)(2,1)}), bf16[128,32,32]{0,2,1:T(8,128)(2,1)S(1)}, u32[]{:S(2)}, u32[]{:S(2)}) async-start(bf16[128,32,32]{0,2,1:T(8,128)(2,1)} %bitcast.2), calls=%async_computation | async-start | bytes 524288 | tf_op jit(solution)/shard_map/all_to_all | solution.py:99
  21.3 23.8 %copy-start.1 = (bf16[128,512]{1,0:T(8,128)(2,1)S(1)}, bf16[128,512]{1,0:T(8,128)(2,1)}, u32[]{:S(2)}) copy-start(bf16[128,512]{1,0:T(8,128)(2,1)} %param.8) | copy-start | bytes 393220
  41.1 11.4 %all-to-all-start.1 = ((bf16[32,128,16]{1,2,0:T(8,128)(2,1)}), bf16[32,128,16]{1,2,0:T(8,128)(2,1)S(1)}, u32[]{:S(2)}, u32[]{:S(2)}) async-start(bf16[32,128,16]{1,2,0:T(8,128)(2,1)} %copy_bitcast_fusion), calls=%async_computation.1 | async-start | bytes 262144 | tf_op jit(solution)/shard_map/all_to_all | solution.py:105
  52.9 7.9 %collective-permute-start = (bf16[128,512]{1,0:T(8,128)(2,1)S(1)}, bf16[128,512]{1,0:T(8,128)(2,1)S(1)}, u32[]{:S(2)}, u32[]{:S(2)}) collective-permute-start(bf16[128,512]{1,0:T(8,128)(2,1)S(1)} %convolution_convert_fusion.2), channel_id=1, source_target_pairs={{0,1},{1,2},{2,3},{3,0},{4,5},{5,6},{6,7},{7,4},{8,9},{9,10},{10,1... | collective-permute-start | bytes 393224 | tf_op jit(solution)/shard_map/ppermute | solution.py:116
  58.7 5.6 %collective-permute-start.1 = (bf16[128,512]{1,0:T(8,128)(2,1)S(1)}, bf16[128,512]{1,0:T(8,128)(2,1)S(1)}, u32[]{:S(2)}, u32[]{:S(2)}) collective-permute-start(bf16[128,512]{1,0:T(8,128)(2,1)S(1)} %convolution_convert_fusion.1), channel_id=1, source_target_pairs={{0,2},{1,3},{2,0},{3,1},{4,6},{5,7},{6,4},{7,5},{8,10},{9,11},{10,... | collective-permute-start | bytes 393224 | tf_op jit(solution)/shard_map/ppermute | solution.py:116
  59.3 6.1 %collective-permute-start.2 = (bf16[128,512]{1,0:T(8,128)(2,1)S(1)}, bf16[128,512]{1,0:T(8,128)(2,1)S(1)}, u32[]{:S(2)}, u32[]{:S(2)}) collective-permute-start(bf16[128,512]{1,0:T(8,128)(2,1)S(1)} %convolution_convert_fusion), channel_id=1, source_target_pairs={{0,3},{1,0},{2,1},{3,2},{4,7},{5,4},{6,5},{7,6},{8,11},{9,8},{10,9... | collective-permute-start | bytes 393224 | tf_op jit(solution)/shard_map/ppermute | solution.py:116

commit v4 on v2

--- a/solution.py
+++ b/solution.py
@@ -16,8 +16,9 @@
     blocks, span = x_ref.shape[1], x_ref.shape[2]
     seq = blocks * span
     lanes = 2 * span
+    width = seq + lanes
     docs = doc_ref[...]
-    lead = docs[:, span - 1 : span]
+    lead = docs[:, 0:1]
     lead_rows = docs == lead
     doc_rows = [docs == doc for doc in range(DOC_COUNT)]
     contract = (((1,), (1,)), ((), ()))
@@ -25,20 +26,23 @@
         channel = pl.program_id(0) * x_ref.shape[0] + k
         frow = f_ref[k].astype(jnp.float32)
         frow = jnp.concatenate([frow, jnp.zeros((1, lanes), jnp.float32)], axis=1)
-        fb = jnp.broadcast_to(frow, (span, seq + lanes))
-        tt = pltpu.roll(fb, 0, 1, stride=1, stride_axis=0)[:, :seq].astype(jnp.bfloat16)
+        fb = jnp.broadcast_to(frow, (span, width))
+        tt = pltpu.roll(fb, width - (span - 1), 1, stride=1, stride_axis=0)[:, :seq]
+        tt = tt.astype(jnp.bfloat16)
         x = x_ref[k]
         xf = x.astype(jnp.float32)
-        pair = jnp.concatenate([xf, pltpu.roll(xf, 1, 0)], axis=1)
+        pair = jnp.concatenate([pltpu.roll(xf, 1, 0), xf], axis=1)
         src = jnp.concatenate(
-            [pair] + [pltpu.roll(pair, 2 * p, 0) for p in range(1, seq // lanes)], axis=1
+            [pltpu.roll(pair, (blocks - 2 - 2 * p) % blocks, 0) for p in range(seq // lanes)], axis=1
         )
         src = (src * mask_ref[...]).astype(jnp.bfloat16)
         y = lax.dot_general(src, tt, contract, preferred_element_type=jnp.float32)
         y = jnp.where(lead_rows, y, 0.0)
         zero = jnp.zeros_like(x)
         planes = jnp.concatenate([jnp.where(rows, x, zero) for rows in doc_rows], axis=0)
-        local = lax.dot_general(planes, tt[:, :span], contract, preferred_element_type=jnp.float32)
+        local = lax.dot_general(
+            planes, tt[:, seq - span :], contract, preferred_element_type=jnp.float32
+        )
         for doc in range(DOC_COUNT):
             rows = doc_rows[doc] & (lead != doc)
             y = y + jnp.where(rows, local[doc * blocks : (doc + 1) * blocks], 0.0)
@@ -51,15 +55,15 @@
     span = SPAN
     blocks = seq // span
     step = CHANNELS_PER_STEP
-    xb = x_cm.reshape(chans, blocks, span)[:, :, ::-1]
+    xb = x_cm.reshape(chans, blocks, span)
     docb = doc_ids.reshape(blocks, span)
     starts = jnp.sum(doc_ids[None, :] < docb[:, :1], axis=1)
-    lag = lax.broadcasted_iota(jnp.int32, (blocks, blocks, span), 1)
     tgt = lax.broadcasted_iota(jnp.int32, (blocks, blocks, span), 0)
-    off = span - 1 - lax.broadcasted_iota(jnp.int32, (blocks, blocks, span), 2)
-    mask = (tgt >= lag) & (span * (tgt - lag) + off >= starts[:, None, None])
+    src_block = tgt - (blocks - 1) + lax.broadcasted_iota(jnp.int32, (blocks, blocks, span), 1)
+    off = lax.broadcasted_iota(jnp.int32, (blocks, blocks, span), 2)
+    mask = (src_block >= 0) & (span * src_block + off >= starts[:, None, None])
     mask = mask.astype(jnp.float32).reshape(blocks, seq)
-    out = pl.pallas_call(
+    return pl.pallas_call(
         conv_kernel,
         grid=(chans // step,),
         in_specs=[
@@ -71,8 +75,7 @@
         ],
         out_specs=pl.BlockSpec((step, blocks, span), lambda c: (c, 0, 0)),
         out_shape=jax.ShapeDtypeStruct((chans, blocks, span), jnp.bfloat16),
-    )(bias_cm, f_cm.reshape(chans, 1, seq), xb, docb[:, ::-1], mask)
-    return out[:, :, ::-1]
+    )(bias_cm, f_cm[:, ::-1].reshape(chans, 1, seq), xb, docb, mask)
 
 
 def body(signal, gate, filt, bias, doc_ids, block_perm, out_weight):

time: 60.3 us -> 62.7 us (1.040)
  local copies, waits for them, and re-layouts: 12 us -> 12.9 us
  other arithmetic: 1.9 us -> 2.6 us
    pallas_call x0 -> x1, local copies, waits for them, and re-layouts: none -> 1.12 us  [pallas_conv(): pl.pallas_call(conv_kernel, grid=(chans // step,), in_specs=[pl.BlockSpec...]
    select_n x2, other arithmetic: 0.1 us -> 0.8 us  [slots_to_natural(): jnp.take(a.reshape(per_dev, blocks, span), inverse, axis=1)]
    all_to_all x1, waiting for transfers between devices: 3.81 us -> 4.44 us  [body(): arrived = lax.all_to_all(packed, 'ctx', 1, 0, tiled=True).T]
    rev x4 -> x1, local copies, waits for them, and re-layouts: 2.86 us -> 2.59 us  [pallas_conv(): f_cm[:, ::-1].reshape(chans, 1, seq)]
    unnamed x11 -> x13, local copies, waits for them, and re-layouts: 2.33 us -> 2.33 us
  transfers between devices with their start and end apart: 5 -> 5, of which waited for: 5 -> 5; matrix products, arithmetic and copies ran while one was open for 9% -> 7% of each run, Pallas kernels for 0% -> 0%
where the time goes in v4:
time: 62.7 us; the launch traced here: 62.3 us
  starting transfers between devices  19.7 us (31%)
  waiting for transfers between devices  17.8 us (28%)
  local copies, waits for them, and re-layouts  12.9 us (21%)
  Pallas kernels  7.4 us (12%)
  other arithmetic  2.6 us (4%)
  matrix products  1.68 us (3%)
    all_to_all x1, starting transfers between devices, body(): arrived = lax.all_to_all(packed, 'ctx', 1, 0, tiled=True).T  9.71 us
    pallas_call x1, Pallas kernels, pallas_conv(): pl.pallas_call(conv_kernel, grid=(chans // step,), in_specs=[pl.BlockSpec...  7.4 us
    all_to_all x1, waiting for transfers between devices, body(): pre_local = lax.all_to_all(pre_slots, 'ctx', 0, 1, tiled=True)  7.38 us
    ppermute x3, starting transfers between devices, body(): lax.ppermute(part.astype(jnp.bfloat16), 'tp', pairs).astype(jnp.float32)  6.1 us
    ppermute x3, waiting for transfers between devices, body(): lax.ppermute(part.astype(jnp.bfloat16), 'tp', pairs).astype(jnp.float32)  5.99 us
    all_to_all x1, waiting for transfers between devices, body(): arrived = lax.all_to_all(packed, 'ctx', 1, 0, tiled=True).T  4.44 us
    all_to_all x1, starting transfers between devices, body(): pre_local = lax.all_to_all(pre_slots, 'ctx', 0, 1, tiled=True)  3.86 us
    rev x1, local copies, waits for them, and re-layouts, pallas_conv(): f_cm[:, ::-1].reshape(chans, 1, seq)  2.59 us
  transfers between devices with their start and end apart: 5, of which 5 were waited for; matrix products, arithmetic and copies ran while one was open for 7% of the time, Pallas kernels for 0%

profile of v4, /device:TPU:1, one launch (start us, length us, event | category | flops | bytes accessed | tf_op | source)
XLA Modules:
  0.0 62.3 jit_solution(11826217577283409816)
XLA Ops:
  0.0 1.2 %copy.49 = bf16[128,512]{0,1:T(8,128)(2,1)S(1)} copy(bf16[128,512]{1,0:T(8,128)(2,1)} %param.9) | data formatting | bytes 262144 | tf_op args[0]
  1.2 1.0 %copy.50 = bf16[128,512]{0,1:T(8,128)(2,1)S(1)} copy(bf16[128,512]{1,0:T(8,128)(2,1)} %param.11) | data formatting | bytes 262144 | tf_op args[2]
  2.3 0.7 %copy.51 = bf16[128,32,2,16]{0,3,2,1:T(8,128)(2,1)} copy(bf16[128,32,2,16]{0,3,1,2:T(8,128)(2,1)S(1)} %pad_maximum_fusion) | data formatting | bytes 524288 | tf_op jit(solution)/shard_map/stack | solution.py:95
  3.0 9.7 %all-to-all-start = ((bf16[128,32,32]{0,2,1:T(8,128)(2,1)}), bf16[128,32,32]{0,2,1:T(8,128)(2,1)S(1)}, u32[]{:S(2)}, u32[]{:S(2)}) async-start(bf16[128,32,32]{0,2,1:T(8,128)(2,1)} %bitcast.2), calls=%async_computation | async-start | bytes 524288 | tf_op jit(solution)/shard_map/all_to_all | solution.py:98
  12.8 0.8 %scatter_custom_fusion = s32[64]{0:T(128)S(1)} fusion(s32[64]{0:T(128)S(1)} %compare_select_fusion, s32[64]{0:T(128)S(1)} %iota.41, s32[]{:T(128)} %constant.54.clone.1), kind=kCustom, calls=%fused_computation.39 | custom fusion | bytes 260 | tf_op jit(solution)/shard_map/scatter | solution.py:90
  14.2 1.3 %fusion.3.mask_ref = f32[64,4096]{1,0:T(8,128)} fusion(s32[64]{0:T(128)S(1)} %convert_reduce_fusion, s32[4096]{0:T(1024)S(1)} %iota.48, s32[4096]{0:T(1024)S(1)} %iota.45, s32[64]{0:T(128)S(1)} %iota_add_fusion), kind=kLoop, calls=%fused_computation.12 | loop fusion | flops 1835008 | bytes 1081856 | tf_op jit(solution)/shard_map/convert_element_type | solution.py:65
  15.5 1.3 %dynamic_slice.15.bias_ref = f32[16]{0:T(128)} dynamic-slice(f32[512]{0:T(512)} %param.12, s32[]{:T(128)S(6)} %select_n.44), dynamic_slice_sizes={16} | dynamic-slice | bytes 132 | tf_op jit(solution)/shard_map/dynamic_slice | solution.py:101
  16.8 4.4 %all-to-all-done = bf16[128,32,32]{0,2,1:T(8,128)(2,1)S(1)} async-done(((bf16[128,32,32]{0,2,1:T(8,128)(2,1)}), bf16[128,32,32]{0,2,1:T(8,128)(2,1)S(1)}, u32[]{:S(2)}, u32[]{:S(2)}) %all-to-all-start) | async-done | bytes 262176 | tf_op jit(solution)/shard_map/all_to_all | solution.py:98
  21.7 2.6 %rev.3 = bf16[16,4096]{1,0:T(8,128)(2,1)S(1)} reverse(bf16[16,4096]{1,0:T(8,128)(2,1)S(1)} %get-tuple-element.7), dimensions={1} | reverse | bytes 262144 | tf_op jit(solution)/shard_map/rev | solution.py:78
  24.3 0.9 %copy.55.f_ref = bf16[16,1,4096]{2,1,0:T(2,128)(2,1)} copy(bf16[16,1,4096]{2,0,1:T(8,128)(2,1)S(1)} %bitcast.32) | data formatting | bytes 262144 | tf_op jit(solution)/shard_map/reshape | solution.py:78
  25.3 0.6 %gather_fusion = bf16[64,16,64]{2,1,0:T(8,128)(2,1)S(1)} fusion(bf16[16,64,64]{2,0,1:T(8,128)(2,1)S(1)} %copy.53, s32[1024]{0:T(1024)S(1)} %pad_clamp_fusion.1), kind=kCustom, calls=%fused_computation.clone | custom fusion | bytes 262400 | tf_op jit(solution)/shard_map/jit(_take)/gather | solution.py:93
  25.9 0.8 %fusion.10.x_ref = bf16[16,64,64]{2,1,0:T(8,128)(2,1)} fusion(bf16[64,16,64]{2,1,0:T(8,128)(2,1)S(1)} %gather_fusion, pred[64]{0:T(512)(128)(4,1)S(1)} %get-tuple-element.9), kind=kLoop, calls=%fused_computation.23 | loop fusion | flops 65536 | bytes 262208 | tf_op jit(solution)/shard_map/jit(_take)/select_n | solution.py:93
  26.7 7.4 %shard_map.73 = bf16[16,64,64]{2,1,0:T(8,128)(2,1)} custom-call(f32[16]{0:T(128)} %dynamic_slice.15.bias_ref, bf16[16,1,4096]{2,1,0:T(2,128)(2,1)} %copy.55.f_ref, bf16[16,64,64]{2,1,0:T(8,128)(2,1)} %fusion.10.x_ref, s32[64,64]{1,0:T(8,128)} %copy-done.1, f32[64,4096]{1,0:T(8,128)} %fusion.3.mask_ref), custom_call_target="tpu_custom_call" | custom-call | tf_op jit(solution)/shard_map/pallas_call | solution.py:66
  34.1 1.1 %copy.56 = bf16[16,64,64]{2,0,1:T(8,128)(2,1)S(1)} copy(bf16[16,64,64]{2,1,0:T(8,128)(2,1)} %shard_map.73) | data formatting | bytes 262144 | tf_op jit(solution)/shard_map/pallas_call | solution.py:66
  35.2 0.6 %gather_fusion.1 = bf16[64,16,64]{2,1,0:T(8,128)(2,1)S(1)} fusion(bf16[16,64,64]{2,0,1:T(8,128)(2,1)S(1)} %copy.56, s32[1024]{0:T(1024)S(1)} %pad_clamp_fusion), kind=kCustom, calls=%fused_computation.1.clone | custom fusion | bytes 262400 | tf_op jit(solution)/shard_map/jit(_take)/gather | solution.py:103
  36.4 0.7 %copy_bitcast_fusion = bf16[32,128,16]{1,2,0:T(8,128)(2,1)} fusion(bf16[16,4096]{1,0:T(8,128)(2,1)S(1)} %reshape.35), kind=kLoop, calls=%fused_computation.26 | loop fusion | bytes 262144 | tf_op jit(solution)/shard_map/all_to_all | solution.py:105
  37.1 3.9 %all-to-all-start.1 = ((bf16[32,128,16]{1,2,0:T(8,128)(2,1)}), bf16[32,128,16]{1,2,0:T(8,128)(2,1)S(1)}, u32[]{:S(2)}, u32[]{:S(2)}) async-start(bf16[32,128,16]{1,2,0:T(8,128)(2,1)} %copy_bitcast_fusion), calls=%async_computation.1 | async-start | bytes 262144 | tf_op jit(solution)/shard_map/all_to_all | solution.py:105
  41.1 7.4 %all-to-all-done.1 = bf16[32,128,16]{1,2,0:T(8,128)(2,1)S(1)} async-done(((bf16[32,128,16]{1,2,0:T(8,128)(2,1)}), bf16[32,128,16]{1,2,0:T(8,128)(2,1)S(1)}, u32[]{:S(2)}, u32[]{:S(2)}) %all-to-all-start.1) | async-done | bytes 131104 | tf_op jit(solution)/shard_map/all_to_all | solution.py:105
  48.8 5.5 %collective-permute-start = (bf16[128,512]{1,0:T(8,128)(2,1)S(1)}, bf16[128,512]{1,0:T(8,128)(2,1)S(1)}, u32[]{:S(2)}, u32[]{:S(2)}) collective-permute-start(bf16[128,512]{1,0:T(8,128)(2,1)S(1)} %convolution_convert_fusion.2), channel_id=1, source_target_pairs={{0,1},{1,2},{2,3},{3,0},{4,5},{5,6},{6,7},{7,4},{8,9},{9,10},{10,1... | collective-permute-start | bytes 393224 | tf_op jit(solution)/shard_map/ppermute | solution.py:116
  54.6 0.4 collective-permute-start.1
  55.4 1.3 %collective-permute-done = bf16[128,512]{1,0:T(8,128)(2,1)S(1)} collective-permute-done((bf16[128,512]{1,0:T(8,128)(2,1)S(1)}, bf16[128,512]{1,0:T(8,128)(2,1)S(1)}, u32[]{:S(2)}, u32[]{:S(2)}) %collective-permute-start) | collective-permute-done | bytes 131104 | tf_op jit(solution)/shard_map/ppermute | solution.py:116
  56.7 3.4 %collective-permute-done.1 = bf16[128,512]{1,0:T(8,128)(2,1)S(1)} collective-permute-done((bf16[128,512]{1,0:T(8,128)(2,1)S(1)}, bf16[128,512]{1,0:T(8,128)(2,1)S(1)}, u32[]{:S(2)}, u32[]{:S(2)}) %collective-permute-start.1) | collective-permute-done | bytes 131104 | tf_op jit(solution)/shard_map/ppermute | solution.py:116
  60.1 1.2 %collective-permute-done.2 = bf16[128,512]{1,0:T(8,128)(2,1)S(1)} collective-permute-done((bf16[128,512]{1,0:T(8,128)(2,1)S(1)}, bf16[128,512]{1,0:T(8,128)(2,1)S(1)}, u32[]{:S(2)}, u32[]{:S(2)}) %collective-permute-start.2) | collective-permute-done | bytes 131104 | tf_op jit(solution)/shard_map/ppermute | solution.py:116
  61.4 0.9 %add_convert_fusion = bf16[128,512]{1,0:T(8,128)(2,1)} fusion(bf16[128,512]{1,0:T(8,128)(2,1)S(1)} %collective-permute-done.2, bf16[128,512]{1,0:T(8,128)(2,1)S(1)} %collective-permute-done.1, bf16[128,512]{1,0:T(8,128)(2,1)S(1)} %collective-permute-done, bf16[128,512]{0,1:T(8,128)(2,1)S(1)} %fusion.9, bf16[512,2048]{1,0:T(8,128)(2,1)S(1)} %copy-done, ...), kind=kOutput, calls=%fused_computation.25 | convolution fusion | flops 67567616 | bytes 1179652 | tf_op jit(solution)/shard_map/dot_general | solution.py:113
  (38 shorter events, 2.7 us)
Async XLA Ops:
  0.0 48.5 %copy-start = (bf16[512,2048]{1,0:T(8,128)(2,1)S(1)}, bf16[512,2048]{1,0:T(8,128)(2,1)}, u32[]{:S(2)}) copy-start(bf16[512,2048]{1,0:T(8,128)(2,1)} %param.15) | copy-start | bytes 6291460
  0.0 12.7 %copy-start.4 = (s32[64]{0:T(128)S(1)}, s32[64]{0:T(128)}, u32[]{:S(2)}) copy-start(s32[64]{0:T(128)} %param.14) | copy-start | bytes 772
  0.0 13.5 %copy-start.3 = (s32[4096]{0:T(1024)S(1)}, s32[4096]{0:T(1024)}, u32[]{:S(2)}) copy-start(s32[4096]{0:T(1024)} %param.13) | copy-start | bytes 49156
  3.0 18.3 %all-to-all-start = ((bf16[128,32,32]{0,2,1:T(8,128)(2,1)}), bf16[128,32,32]{0,2,1:T(8,128)(2,1)S(1)}, u32[]{:S(2)}, u32[]{:S(2)}) async-start(bf16[128,32,32]{0,2,1:T(8,128)(2,1)} %bitcast.2), calls=%async_computation | async-start | bytes 524288 | tf_op jit(solution)/shard_map/all_to_all | solution.py:98
  13.6 12.3 %copy-start.1 = (s32[64,64]{1,0:T(8,128)}, s32[64,64]{1,0:T(8,128)S(1)}, u32[]{:S(2)}) copy-start(s32[64,64]{1,0:T(8,128)S(1)} %reshape.34.doc_ref) | copy-start | bytes 49156
  26.7 14.2 %copy-start.2 = (bf16[128,512]{1,0:T(8,128)(2,1)S(1)}, bf16[128,512]{1,0:T(8,128)(2,1)}, u32[]{:S(2)}) copy-start(bf16[128,512]{1,0:T(8,128)(2,1)} %param.10) | copy-start | bytes 393220
  37.1 11.4 %all-to-all-start.1 = ((bf16[32,128,16]{1,2,0:T(8,128)(2,1)}), bf16[32,128,16]{1,2,0:T(8,128)(2,1)S(1)}, u32[]{:S(2)}, u32[]{:S(2)}) async-start(bf16[32,128,16]{1,2,0:T(8,128)(2,1)} %copy_bitcast_fusion), calls=%async_computation.1 | async-start | bytes 262144 | tf_op jit(solution)/shard_map/all_to_all | solution.py:105
  48.8 7.9 %collective-permute-start = (bf16[128,512]{1,0:T(8,128)(2,1)S(1)}, bf16[128,512]{1,0:T(8,128)(2,1)S(1)}, u32[]{:S(2)}, u32[]{:S(2)}) collective-permute-start(bf16[128,512]{1,0:T(8,128)(2,1)S(1)} %convolution_convert_fusion.2), channel_id=1, source_target_pairs={{0,1},{1,2},{2,3},{3,0},{4,5},{5,6},{6,7},{7,4},{8,9},{9,10},{10,1... | collective-permute-start | bytes 393224 | tf_op jit(solution)/shard_map/ppermute | solution.py:116
  54.6 5.6 %collective-permute-start.1 = (bf16[128,512]{1,0:T(8,128)(2,1)S(1)}, bf16[128,512]{1,0:T(8,128)(2,1)S(1)}, u32[]{:S(2)}, u32[]{:S(2)}) collective-permute-start(bf16[128,512]{1,0:T(8,128)(2,1)S(1)} %convolution_convert_fusion.1), channel_id=1, source_target_pairs={{0,2},{1,3},{2,0},{3,1},{4,6},{5,7},{6,4},{7,5},{8,10},{9,11},{10,... | collective-permute-start | bytes 393224 | tf_op jit(solution)/shard_map/ppermute | solution.py:116
  55.3 6.1 %collective-permute-start.2 = (bf16[128,512]{1,0:T(8,128)(2,1)S(1)}, bf16[128,512]{1,0:T(8,128)(2,1)S(1)}, u32[]{:S(2)}, u32[]{:S(2)}) collective-permute-start(bf16[128,512]{1,0:T(8,128)(2,1)S(1)} %convolution_convert_fusion), channel_id=1, source_target_pairs={{0,3},{1,0},{2,1},{3,2},{4,7},{5,4},{6,5},{7,6},{8,11},{9,8},{10,9... | collective-permute-start | bytes 393224 | tf_op jit(solution)/shard_map/ppermute | solution.py:116

commit v5 on v2

--- a/solution.py
+++ b/solution.py
@@ -101,18 +101,12 @@
     pre_slots = pre_slots.reshape(per_dev, seq).T
     pre_local = lax.all_to_all(pre_slots, "ctx", 0, 1, tiled=True)
     gated_local = (gate.astype(jnp.float32) * pre_local.astype(jnp.float32)).astype(jnp.bfloat16)
-    tp_index = lax.axis_index("tp")
     n_tp = out_weight.shape[1] // chans
-    total = None
-    for offset in range(n_tp):
-        target = (tp_index + offset) % n_tp
-        w_cols = lax.dynamic_slice_in_dim(out_weight, target * chans, chans, axis=1)
-        part = jnp.dot(gated_local, w_cols, preferred_element_type=jnp.float32)
-        if offset:
-            pairs = [(i, (i + offset) % n_tp) for i in range(n_tp)]
-            part = lax.ppermute(part.astype(jnp.bfloat16), "tp", pairs).astype(jnp.float32)
-        total = part if total is None else total + part
-    return total.astype(jnp.bfloat16)
+    partial_value = jnp.dot(gated_local, out_weight, preferred_element_type=jnp.float32)
+    parts = lax.all_to_all(
+        partial_value.astype(jnp.bfloat16).reshape(rows, n_tp, chans), "tp", 1, 1, tiled=True
+    )
+    return jnp.sum(parts.astype(jnp.float32), axis=1).astype(jnp.bfloat16)
 
 
 def solution(mesh):

time: 60.3 us -> 64.1 us (1.063)
  blocking collectives: 0 us -> 16.1 us
  starting transfers between devices: 19.7 us -> 13.7 us
  waiting for transfers between devices: 17.2 us -> 11.3 us
  matrix products: 1.68 us -> 0.47 us
  other arithmetic: 1.9 us -> 2.67 us
    all_to_all x0 -> x1, blocking collectives: none -> 16.1 us  [body(): lax.all_to_all(partial_value.astype(jnp.bfloat16).reshape(rows, n_tp, cha...]
    ppermute x3 -> x0, starting transfers between devices: 6 us -> none  [body(): lax.ppermute(part.astype(jnp.bfloat16), 'tp', pairs).astype(jnp.float32)]
    ppermute x3 -> x0, waiting for transfers between devices: 5.99 us -> none  [body(): lax.ppermute(part.astype(jnp.bfloat16), 'tp', pairs).astype(jnp.float32)]
    dot_general x4 -> x1, matrix products: 1.68 us -> 0.47 us  [body(): jnp.dot(gated_local, out_weight, preferred_element_type=jnp.float32)]
    reduce_sum x0 -> x1, other arithmetic: none -> 0.75 us  [body(): return jnp.sum(parts.astype(jnp.float32), axis=1).astype(jnp.bfloat16)]
  transfers between devices with their start and end apart: 5 -> 2, of which waited for: 5 -> 2; matrix products, arithmetic and copies ran while one was open for 9% -> 8% of each run, Pallas kernels for 0% -> 0%
where the time goes in v5:
time: 64.1 us; the launch traced here: 63.7 us
  blocking collectives  16.1 us (25%)
  starting transfers between devices  13.7 us (21%)
  local copies, waits for them, and re-layouts  12.1 us (19%)
  waiting for transfers between devices  11.3 us (18%)
  Pallas kernels  7.27 us (11%)
  other arithmetic  2.67 us (4%)
    all_to_all x1, blocking collectives, body(): lax.all_to_all(partial_value.astype(jnp.bfloat16).reshape(rows, n_tp, cha...  16.1 us
    all_to_all x1, starting transfers between devices, body(): arrived = lax.all_to_all(packed, 'ctx', 1, 0, tiled=True).T  9.71 us
    all_to_all x1, waiting for transfers between devices, body(): pre_local = lax.all_to_all(pre_slots, 'ctx', 0, 1, tiled=True)  7.47 us
    pallas_call x1, Pallas kernels, pallas_conv(): pl.pallas_call(conv_kernel, grid=(chans // step,), in_specs=[pl.BlockSpec...  7.27 us
    all_to_all x1, starting transfers between devices, body(): pre_local = lax.all_to_all(pre_slots, 'ctx', 0, 1, tiled=True)  3.96 us
    all_to_all x1, waiting for transfers between devices, body(): arrived = lax.all_to_all(packed, 'ctx', 1, 0, tiled=True).T  3.78 us
    unnamed x11, local copies, waits for them, and re-layouts  2.33 us
    rev x2, local copies, waits for them, and re-layouts, pallas_conv(): return out[:, :, ::-1]  1.32 us
  transfers between devices with their start and end apart: 2, of which 2 were waited for; matrix products, arithmetic and copies ran while one was open for 8% of the time, Pallas kernels for 0%

profile of v5, /device:TPU:1, one launch (start us, length us, event | category | flops | bytes accessed | tf_op | source)
XLA Modules:
  0.0 63.7 jit_solution(11119659629076872418)
XLA Ops:
  0.0 1.2 %copy.50 = bf16[128,512]{0,1:T(8,128)(2,1)S(1)} copy(bf16[128,512]{1,0:T(8,128)(2,1)} %param.9) | data formatting | bytes 262144 | tf_op args[0]
  1.2 1.0 %copy.51 = bf16[128,512]{0,1:T(8,128)(2,1)S(1)} copy(bf16[128,512]{1,0:T(8,128)(2,1)} %param.11) | data formatting | bytes 262144 | tf_op args[2]
  2.3 0.7 %copy.52 = bf16[128,32,2,16]{0,3,2,1:T(8,128)(2,1)} copy(bf16[128,32,2,16]{0,3,1,2:T(8,128)(2,1)S(1)} %pad_maximum_fusion) | data formatting | bytes 524288 | tf_op jit(solution)/shard_map/stack | solution.py:92
  3.0 9.7 %all-to-all-start = ((bf16[128,32,32]{0,2,1:T(8,128)(2,1)}), bf16[128,32,32]{0,2,1:T(8,128)(2,1)S(1)}, u32[]{:S(2)}, u32[]{:S(2)}) async-start(bf16[128,32,32]{0,2,1:T(8,128)(2,1)} %bitcast.2), calls=%async_computation | async-start | bytes 524288 | tf_op jit(solution)/shard_map/all_to_all | solution.py:95
  12.7 0.8 %scatter_custom_fusion = s32[64]{0:T(128)S(1)} fusion(s32[64]{0:T(128)S(1)} %compare_select_fusion, s32[64]{0:T(128)S(1)} %iota.40, s32[]{:T(128)} %constant.6.clone.1), kind=kCustom, calls=%fused_computation.27 | custom fusion | bytes 260 | tf_op jit(solution)/shard_map/scatter | solution.py:87
  13.8 0.3 convert_reduce_fusion
  14.2 1.3 %fusion.1.mask_ref = f32[64,4096]{1,0:T(8,128)} fusion(s32[64]{0:T(128)S(1)} %convert_reduce_fusion, s32[4096]{0:T(1024)S(1)} %iota.48, s32[4096]{0:T(1024)S(1)} %iota.43), kind=kLoop, calls=%fused_computation.8 | loop fusion | flops 1835008 | bytes 1081600 | tf_op jit(solution)/shard_map/convert_element_type | solution.py:61
  15.5 0.7 %rev.10.doc_ref = s32[64,64]{1,0:T(8,128)} reverse(s32[64,64]{1,0:T(8,128)S(1)} %reshape.39), dimensions={1} | reverse | bytes 32768 | tf_op jit(solution)/shard_map/rev | solution.py:74
  16.2 1.3 %dynamic_slice.3.bias_ref = f32[16]{0:T(128)} dynamic-slice(f32[512]{0:T(512)} %param.12, s32[]{:T(128)S(6)} %select_n.13), dynamic_slice_sizes={16} | dynamic-slice | bytes 132 | tf_op jit(solution)/shard_map/dynamic_slice | solution.py:98
  17.5 3.8 %all-to-all-done = bf16[128,32,32]{0,2,1:T(8,128)(2,1)S(1)} async-done(((bf16[128,32,32]{0,2,1:T(8,128)(2,1)}), bf16[128,32,32]{0,2,1:T(8,128)(2,1)S(1)}, u32[]{:S(2)}, u32[]{:S(2)}) %all-to-all-start) | async-done | bytes 262176 | tf_op jit(solution)/shard_map/all_to_all | solution.py:95
  21.3 0.2 reshape.38
  21.8 0.6 gather_fusion
  22.5 0.9 %rev.9.x_ref = bf16[16,64,64]{2,1,0:T(8,128)(2,1)} reverse(bf16[16,64,64]{2,1,0:T(8,128)(2,1)S(1)} %fusion.3), dimensions={2} | reverse | bytes 262144 | tf_op jit(solution)/shard_map/rev | solution.py:54
  23.4 1.0 %copy.56.f_ref = bf16[16,1,4096]{2,1,0:T(2,128)(2,1)} copy(bf16[16,1,4096]{2,0,1:T(8,128)(2,1)S(1)} %get-tuple-element.7) | data formatting | bytes 262144 | tf_op jit(solution)/shard_map/reshape | solution.py:74
  24.3 7.3 %shard_map.73 = bf16[16,64,64]{2,1,0:T(8,128)(2,1)} custom-call(f32[16]{0:T(128)} %dynamic_slice.3.bias_ref, bf16[16,1,4096]{2,1,0:T(2,128)(2,1)} %copy.56.f_ref, bf16[16,64,64]{2,1,0:T(8,128)(2,1)} %rev.9.x_ref, s32[64,64]{1,0:T(8,128)} %rev.10.doc_ref, f32[64,4096]{1,0:T(8,128)} %fusion.1.mask_ref), custom_call_target="tpu_custom_call" | custom-call | tf_op jit(solution)/shard_map/pallas_call | solution.py:62
  31.6 1.1 %rev.11 = bf16[16,64,64]{2,1,0:T(8,128)(2,1)S(1)} reverse(bf16[16,64,64]{2,1,0:T(8,128)(2,1)} %shard_map.73), dimensions={2} | reverse | bytes 262144 | tf_op jit(solution)/shard_map/rev | solution.py:75
  32.9 0.6 gather_fusion.1
  33.8 0.3 reshape.40
  34.1 0.7 %copy_bitcast_fusion.1 = bf16[32,128,16]{1,2,0:T(8,128)(2,1)} fusion(bf16[16,4096]{1,0:T(8,128)(2,1)S(1)} %reshape.40), kind=kLoop, calls=%fused_computation.17 | loop fusion | bytes 262144 | tf_op jit(solution)/shard_map/all_to_all | solution.py:102
  34.7 4.0 %all-to-all-start.1 = ((bf16[32,128,16]{1,2,0:T(8,128)(2,1)}), bf16[32,128,16]{1,2,0:T(8,128)(2,1)S(1)}, u32[]{:S(2)}, u32[]{:S(2)}) async-start(bf16[32,128,16]{1,2,0:T(8,128)(2,1)} %copy_bitcast_fusion.1), calls=%async_computation.1 | async-start | bytes 262144 | tf_op jit(solution)/shard_map/all_to_all | solution.py:102
  38.8 7.5 %all-to-all-done.1 = bf16[32,128,16]{1,2,0:T(8,128)(2,1)S(1)} async-done(((bf16[32,128,16]{1,2,0:T(8,128)(2,1)}), bf16[32,128,16]{1,2,0:T(8,128)(2,1)S(1)}, u32[]{:S(2)}, u32[]{:S(2)}) %all-to-all-start.1) | async-done | bytes 131104 | tf_op jit(solution)/shard_map/all_to_all | solution.py:102
  46.4 0.5 convolution_convert_fusion
  46.9 16.1 %all_to_all.37 = bf16[128,4,512]{2,0,1:T(8,128)(2,1)S(1)} all-to-all(bf16[128,4,512]{2,0,1:T(8,128)(2,1)S(1)} %bitcast.35), channel_id=1, replica_groups=mesh['ctx'=32,'tp'=4] {'tp'}, dimensions={1} | all-to-all | bytes 1048576 | tf_op jit(solution)/shard_map/all_to_all | solution.py:106
  63.0 0.7 %reduce_sum.22 = bf16[128,512]{1,0:T(8,128)(2,1)} reduce(bf16[128,4,512]{2,0,1:T(8,128)(2,1)S(1)} %all_to_all.37, bf16[]{:T(256)} %constant.14.clone.1), dimensions={1}, to_apply=%region_2.4 | reduce | flops 196608 | bytes 655362 | tf_op jit(solution)/shard_map/reduce_sum | solution.py:109
  (33 shorter events, 1.3 us)
Async XLA Ops:
  0.0 46.3 %copy-start = (bf16[512,2048]{1,0:T(8,128)(2,1)S(1)}, bf16[512,2048]{1,0:T(8,128)(2,1)}, u32[]{:S(2)}) copy-start(bf16[512,2048]{1,0:T(8,128)(2,1)} %param.15) | copy-start | bytes 6291460
  0.0 12.7 %copy-start.3 = (s32[64]{0:T(128)S(1)}, s32[64]{0:T(128)}, u32[]{:S(2)}) copy-start(s32[64]{0:T(128)} %param.14) | copy-start | bytes 772
  0.0 13.6 %copy-start.2 = (s32[4096]{0:T(1024)S(1)}, s32[4096]{0:T(1024)}, u32[]{:S(2)}) copy-start(s32[4096]{0:T(1024)} %param.13) | copy-start | bytes 49156
  3.0 18.3 %all-to-all-start = ((bf16[128,32,32]{0,2,1:T(8,128)(2,1)}), bf16[128,32,32]{0,2,1:T(8,128)(2,1)S(1)}, u32[]{:S(2)}, u32[]{:S(2)}) async-start(bf16[128,32,32]{0,2,1:T(8,128)(2,1)} %bitcast.2), calls=%async_computation | async-start | bytes 524288 | tf_op jit(solution)/shard_map/all_to_all | solution.py:95
  31.6 7.1 %copy-start.1 = (bf16[128,512]{1,0:T(8,128)(2,1)S(1)}, bf16[128,512]{1,0:T(8,128)(2,1)}, u32[]{:S(2)}) copy-start(bf16[128,512]{1,0:T(8,128)(2,1)} %param.10) | copy-start | bytes 393220
  34.7 11.6 %all-to-all-start.1 = ((bf16[32,128,16]{1,2,0:T(8,128)(2,1)}), bf16[32,128,16]{1,2,0:T(8,128)(2,1)S(1)}, u32[]{:S(2)}, u32[]{:S(2)}) async-start(bf16[32,128,16]{1,2,0:T(8,128)(2,1)} %copy_bitcast_fusion.1), calls=%async_computation.1 | async-start | bytes 262144 | tf_op jit(solution)/shard_map/all_to_all | solution.py:102

commit v6 on v2

--- a/solution.py
+++ b/solution.py
@@ -9,10 +9,10 @@
 DOC_COUNT = 4
 
 
-CHANNELS_PER_STEP = 4
+CHANNELS_PER_STEP = 8
 
 
-def conv_kernel(bias_ref, f_ref, x_ref, doc_ref, mask_ref, y_ref):
+def conv_kernel(base_ref, bias_ref, f_ref, x_ref, doc_ref, mask_ref, y_ref):
     blocks, span = x_ref.shape[1], x_ref.shape[2]
     seq = blocks * span
     lanes = 2 * span
@@ -42,11 +42,11 @@
         for doc in range(DOC_COUNT):
             rows = doc_rows[doc] & (lead != doc)
             y = y + jnp.where(rows, local[doc * blocks : (doc + 1) * blocks], 0.0)
-        y = y + bias_ref[channel] * xf
+        y = y + bias_ref[base_ref[0] + channel] * xf
         y_ref[k] = y.astype(y_ref.dtype)
 
 
-def pallas_conv(x_cm, f_cm, doc_ids, bias_cm):
+def pallas_conv(x_cm, f_cm, doc_ids, bias, base):
     chans, seq = x_cm.shape
     span = SPAN
     blocks = seq // span
@@ -64,6 +64,7 @@
         grid=(chans // step,),
         in_specs=[
             pl.BlockSpec(memory_space=pltpu.SMEM),
+            pl.BlockSpec(memory_space=pltpu.SMEM),
             pl.BlockSpec((step, 1, seq), lambda c: (c, 0, 0)),
             pl.BlockSpec((step, blocks, span), lambda c: (c, 0, 0)),
             pl.BlockSpec((blocks, span), lambda c: (0, 0)),
@@ -71,7 +72,7 @@
         ],
         out_specs=pl.BlockSpec((step, blocks, span), lambda c: (c, 0, 0)),
         out_shape=jax.ShapeDtypeStruct((chans, blocks, span), jnp.bfloat16),
-    )(bias_cm, f_cm.reshape(chans, 1, seq), xb, docb[:, ::-1], mask)
+    )(base, bias, f_cm.reshape(chans, 1, seq), xb, docb[:, ::-1], mask)
     return out[:, :, ::-1]
 
 
@@ -95,8 +96,7 @@
     arrived = lax.all_to_all(packed, "ctx", 1, 0, tiled=True).T
     x_cm = slots_to_natural(arrived[:per_dev])
     f_cm = arrived[per_dev:]
-    bias_cm = lax.dynamic_slice_in_dim(bias, ctx_index * per_dev, per_dev)
-    pre = pallas_conv(x_cm, f_cm, doc_ids, bias_cm)
+    pre = pallas_conv(x_cm, f_cm, doc_ids, bias, (ctx_index * per_dev).reshape(1))
     pre_slots = jnp.take(pre, block_perm, axis=1)
     pre_slots = pre_slots.reshape(per_dev, seq).T
     pre_local = lax.all_to_all(pre_slots, "ctx", 0, 1, tiled=True)

time: 60.3 us -> 59.9 us (level)
  local copies, waits for them, and re-layouts: 12 us -> 10.7 us
  waiting for transfers between devices: 17.2 us -> 18.4 us
    all_to_all x1, waiting for transfers between devices: 3.81 us -> 5.08 us  [body(): arrived = lax.all_to_all(packed, 'ctx', 1, 0, tiled=True).T]
    dynamic_slice x1 -> x0, local copies, waits for them, and re-layouts: 1.27 us -> none  [body(): bias_cm = lax.dynamic_slice_in_dim(bias, ctx_index * per_dev, per_dev)]
  transfers between devices with their start and end apart: 5 -> 5, of which waited for: 5 -> 5; matrix products, arithmetic and copies ran while one was open for 9% -> 7% of each run, Pallas kernels for 0% -> 0%
where the time goes in v6:
time: 59.9 us; the launch traced here: 59.6 us
  starting transfers between devices  19.7 us (33%)
  waiting for transfers between devices  18.4 us (31%)
  local copies, waits for them, and re-layouts  10.7 us (18%)
  Pallas kernels  6.94 us (12%)
  other arithmetic  1.9 us (3%)
  matrix products  1.68 us (3%)
    all_to_all x1, starting transfers between devices, body(): arrived = lax.all_to_all(packed, 'ctx', 1, 0, tiled=True).T  9.71 us
    all_to_all x1, waiting for transfers between devices, body(): pre_local = lax.all_to_all(pre_slots, 'ctx', 0, 1, tiled=True)  7.38 us
    pallas_call x1, Pallas kernels, pallas_conv(): pl.pallas_call(conv_kernel, grid=(chans // step,), in_specs=[pl.BlockSpec...  6.94 us
    ppermute x3, starting transfers between devices, body(): lax.ppermute(part.astype(jnp.bfloat16), 'tp', pairs).astype(jnp.float32)  6.1 us
    ppermute x3, waiting for transfers between devices, body(): lax.ppermute(part.astype(jnp.bfloat16), 'tp', pairs).astype(jnp.float32)  5.99 us
    all_to_all x1, waiting for transfers between devices, body(): arrived = lax.all_to_all(packed, 'ctx', 1, 0, tiled=True).T  5.08 us
    all_to_all x1, starting transfers between devices, body(): pre_local = lax.all_to_all(pre_slots, 'ctx', 0, 1, tiled=True)  3.86 us
    unnamed x11, local copies, waits for them, and re-layouts  2.33 us
  transfers between devices with their start and end apart: 5, of which 5 were waited for; matrix products, arithmetic and copies ran while one was open for 7% of the time, Pallas kernels for 0%

profile of v6, /device:TPU:1, one launch (start us, length us, event | category | flops | bytes accessed | tf_op | source)
XLA Modules:
  0.0 59.6 jit_solution(5809567611639420161)
XLA Ops:
  0.0 1.2 %copy.49 = bf16[128,512]{0,1:T(8,128)(2,1)S(1)} copy(bf16[128,512]{1,0:T(8,128)(2,1)} %param.9) | data formatting | bytes 262144 | tf_op args[0]
  1.2 1.0 %copy.50 = bf16[128,512]{0,1:T(8,128)(2,1)S(1)} copy(bf16[128,512]{1,0:T(8,128)(2,1)} %param.11) | data formatting | bytes 262144 | tf_op args[2]
  2.3 0.7 %copy.51 = bf16[128,32,2,16]{0,3,2,1:T(8,128)(2,1)} copy(bf16[128,32,2,16]{0,3,1,2:T(8,128)(2,1)S(1)} %pad_maximum_fusion) | data formatting | bytes 524288 | tf_op jit(solution)/shard_map/stack | solution.py:93
  3.0 9.7 %all-to-all-start = ((bf16[128,32,32]{0,2,1:T(8,128)(2,1)}), bf16[128,32,32]{0,2,1:T(8,128)(2,1)S(1)}, u32[]{:S(2)}, u32[]{:S(2)}) async-start(bf16[128,32,32]{0,2,1:T(8,128)(2,1)} %bitcast.3), calls=%async_computation | async-start | bytes 524288 | tf_op jit(solution)/shard_map/all_to_all | solution.py:96
  12.7 0.8 %scatter_custom_fusion = s32[64]{0:T(128)S(1)} fusion(s32[64]{0:T(128)S(1)} %compare_select_fusion, s32[64]{0:T(128)S(1)} %iota.40, s32[]{:T(128)} %constant.52.clone.1), kind=kCustom, calls=%fused_computation.38 | custom fusion | bytes 260 | tf_op jit(solution)/shard_map/scatter | solution.py:88
  13.7 0.3 convert_reduce_fusion
  14.2 1.3 %fusion.1.mask_ref = f32[64,4096]{1,0:T(8,128)} fusion(s32[64]{0:T(128)S(1)} %convert_reduce_fusion, s32[4096]{0:T(1024)S(1)} %iota.48, s32[4096]{0:T(1024)S(1)} %iota.43), kind=kLoop, calls=%fused_computation.10 | loop fusion | flops 1835008 | bytes 1081600 | tf_op jit(solution)/shard_map/convert_element_type | solution.py:61
  15.5 0.7 %rev.10.doc_ref = s32[64,64]{1,0:T(8,128)} reverse(s32[64,64]{1,0:T(8,128)S(1)} %reshape.40), dimensions={1} | reverse | bytes 32768 | tf_op jit(solution)/shard_map/rev | solution.py:75
  16.2 5.1 %all-to-all-done = bf16[128,32,32]{0,2,1:T(8,128)(2,1)S(1)} async-done(((bf16[128,32,32]{0,2,1:T(8,128)(2,1)}), bf16[128,32,32]{0,2,1:T(8,128)(2,1)S(1)}, u32[]{:S(2)}, u32[]{:S(2)}) %all-to-all-start) | async-done | bytes 262176 | tf_op jit(solution)/shard_map/all_to_all | solution.py:96
  21.7 0.6 %gather_fusion = bf16[64,16,64]{2,1,0:T(8,128)(2,1)S(1)} fusion(bf16[16,64,64]{2,0,1:T(8,128)(2,1)S(1)} %copy.53, s32[1024]{0:T(1024)S(1)} %pad_clamp_fusion.1), kind=kCustom, calls=%fused_computation.clone | custom fusion | bytes 262400 | tf_op jit(solution)/shard_map/jit(_take)/gather | solution.py:91
  22.5 0.9 %rev.9.x_ref = bf16[16,64,64]{2,1,0:T(8,128)(2,1)} reverse(bf16[16,64,64]{2,1,0:T(8,128)(2,1)S(1)} %fusion.8), dimensions={2} | reverse | bytes 262144 | tf_op jit(solution)/shard_map/rev | solution.py:54
  23.3 0.9 %copy.55.f_ref = bf16[16,1,4096]{2,1,0:T(2,128)(2,1)} copy(bf16[16,1,4096]{2,0,1:T(8,128)(2,1)S(1)} %get-tuple-element.7) | data formatting | bytes 262144 | tf_op jit(solution)/shard_map/reshape | solution.py:75
  24.2 6.9 %shard_map.73 = bf16[16,64,64]{2,1,0:T(8,128)(2,1)} custom-call(s32[1]{0:T(128)} %bitcast.base_ref, f32[512]{0:T(512)} %bias_ref.1, bf16[16,1,4096]{2,1,0:T(2,128)(2,1)} %copy.55.f_ref, bf16[16,64,64]{2,1,0:T(8,128)(2,1)} %rev.9.x_ref, s32[64,64]{1,0:T(8,128)} %rev.10.doc_ref, f32[64,4096]{1,0:T(8,128)} %fusion.1.mask_ref), custom_call_target="tpu_custom_call" | custom-call | tf_op jit(solution)/shard_map/pallas_call | solution.py:62
  31.2 1.1 %rev.11 = bf16[16,64,64]{2,1,0:T(8,128)(2,1)S(1)} reverse(bf16[16,64,64]{2,1,0:T(8,128)(2,1)} %shard_map.73), dimensions={2} | reverse | bytes 262144 | tf_op jit(solution)/shard_map/rev | solution.py:76
  32.5 0.6 %gather_fusion.1 = bf16[64,16,64]{2,1,0:T(8,128)(2,1)S(1)} fusion(bf16[16,64,64]{2,0,1:T(8,128)(2,1)S(1)} %copy.56, s32[1024]{0:T(1024)S(1)} %pad_clamp_fusion), kind=kCustom, calls=%fused_computation.1.clone | custom fusion | bytes 262400 | tf_op jit(solution)/shard_map/jit(_take)/gather | solution.py:100
  33.6 0.7 %copy_bitcast_fusion = bf16[32,128,16]{1,2,0:T(8,128)(2,1)} fusion(bf16[16,4096]{1,0:T(8,128)(2,1)S(1)} %reshape.41), kind=kLoop, calls=%fused_computation.24 | loop fusion | bytes 262144 | tf_op jit(solution)/shard_map/all_to_all | solution.py:102
  34.3 3.9 %all-to-all-start.1 = ((bf16[32,128,16]{1,2,0:T(8,128)(2,1)}), bf16[32,128,16]{1,2,0:T(8,128)(2,1)S(1)}, u32[]{:S(2)}, u32[]{:S(2)}) async-start(bf16[32,128,16]{1,2,0:T(8,128)(2,1)} %copy_bitcast_fusion), calls=%async_computation.1 | async-start | bytes 262144 | tf_op jit(solution)/shard_map/all_to_all | solution.py:102
  38.4 7.4 %all-to-all-done.1 = bf16[32,128,16]{1,2,0:T(8,128)(2,1)S(1)} async-done(((bf16[32,128,16]{1,2,0:T(8,128)(2,1)}), bf16[32,128,16]{1,2,0:T(8,128)(2,1)S(1)}, u32[]{:S(2)}, u32[]{:S(2)}) %all-to-all-start.1) | async-done | bytes 131104 | tf_op jit(solution)/shard_map/all_to_all | solution.py:102
  46.1 5.5 %collective-permute-start = (bf16[128,512]{1,0:T(8,128)(2,1)S(1)}, bf16[128,512]{1,0:T(8,128)(2,1)S(1)}, u32[]{:S(2)}, u32[]{:S(2)}) collective-permute-start(bf16[128,512]{1,0:T(8,128)(2,1)S(1)} %convolution_convert_fusion.2), channel_id=1, source_target_pairs={{0,1},{1,2},{2,3},{3,0},{4,5},{5,6},{6,7},{7,4},{8,9},{9,10},{10,1... | collective-permute-start | bytes 393224 | tf_op jit(solution)/shard_map/ppermute | solution.py:113
  51.9 0.4 collective-permute-start.1
  52.7 1.3 %collective-permute-done = bf16[128,512]{1,0:T(8,128)(2,1)S(1)} collective-permute-done((bf16[128,512]{1,0:T(8,128)(2,1)S(1)}, bf16[128,512]{1,0:T(8,128)(2,1)S(1)}, u32[]{:S(2)}, u32[]{:S(2)}) %collective-permute-start) | collective-permute-done | bytes 131104 | tf_op jit(solution)/shard_map/ppermute | solution.py:113
  54.0 3.4 %collective-permute-done.1 = bf16[128,512]{1,0:T(8,128)(2,1)S(1)} collective-permute-done((bf16[128,512]{1,0:T(8,128)(2,1)S(1)}, bf16[128,512]{1,0:T(8,128)(2,1)S(1)}, u32[]{:S(2)}, u32[]{:S(2)}) %collective-permute-start.1) | collective-permute-done | bytes 131104 | tf_op jit(solution)/shard_map/ppermute | solution.py:113
  57.4 1.2 %collective-permute-done.2 = bf16[128,512]{1,0:T(8,128)(2,1)S(1)} collective-permute-done((bf16[128,512]{1,0:T(8,128)(2,1)S(1)}, bf16[128,512]{1,0:T(8,128)(2,1)S(1)}, u32[]{:S(2)}, u32[]{:S(2)}) %collective-permute-start.2) | collective-permute-done | bytes 131104 | tf_op jit(solution)/shard_map/ppermute | solution.py:113
  58.7 0.9 %add_convert_fusion = bf16[128,512]{1,0:T(8,128)(2,1)} fusion(bf16[128,512]{1,0:T(8,128)(2,1)S(1)} %collective-permute-done.2, bf16[128,512]{1,0:T(8,128)(2,1)S(1)} %collective-permute-done.1, bf16[128,512]{1,0:T(8,128)(2,1)S(1)} %collective-permute-done, bf16[128,512]{0,1:T(8,128)(2,1)S(1)} %fusion.7, bf16[512,2048]{1,0:T(8,128)(2,1)S(1)} %copy-done, ...), kind=kOutput, calls=%fused_computation.23 | convolution fusion | flops 67567616 | bytes 1179652 | tf_op jit(solution)/shard_map/dot_general | solution.py:110
  (37 shorter events, 2.6 us)
Async XLA Ops:
  0.0 45.8 %copy-start = (bf16[512,2048]{1,0:T(8,128)(2,1)S(1)}, bf16[512,2048]{1,0:T(8,128)(2,1)}, u32[]{:S(2)}) copy-start(bf16[512,2048]{1,0:T(8,128)(2,1)} %param.15) | copy-start | bytes 6291460
  0.0 12.7 %copy-start.3 = (s32[64]{0:T(128)S(1)}, s32[64]{0:T(128)}, u32[]{:S(2)}) copy-start(s32[64]{0:T(128)} %param.14) | copy-start | bytes 772
  0.0 13.5 %copy-start.2 = (s32[4096]{0:T(1024)S(1)}, s32[4096]{0:T(1024)}, u32[]{:S(2)}) copy-start(s32[4096]{0:T(1024)} %param.13) | copy-start | bytes 49156
  3.0 18.3 %all-to-all-start = ((bf16[128,32,32]{0,2,1:T(8,128)(2,1)}), bf16[128,32,32]{0,2,1:T(8,128)(2,1)S(1)}, u32[]{:S(2)}, u32[]{:S(2)}) async-start(bf16[128,32,32]{0,2,1:T(8,128)(2,1)} %bitcast.3), calls=%async_computation | async-start | bytes 524288 | tf_op jit(solution)/shard_map/all_to_all | solution.py:96
  31.2 7.1 %copy-start.1 = (bf16[128,512]{1,0:T(8,128)(2,1)S(1)}, bf16[128,512]{1,0:T(8,128)(2,1)}, u32[]{:S(2)}) copy-start(bf16[128,512]{1,0:T(8,128)(2,1)} %param.10) | copy-start | bytes 393220
  34.3 11.4 %all-to-all-start.1 = ((bf16[32,128,16]{1,2,0:T(8,128)(2,1)}), bf16[32,128,16]{1,2,0:T(8,128)(2,1)S(1)}, u32[]{:S(2)}, u32[]{:S(2)}) async-start(bf16[32,128,16]{1,2,0:T(8,128)(2,1)} %copy_bitcast_fusion), calls=%async_computation.1 | async-start | bytes 262144 | tf_op jit(solution)/shard_map/all_to_all | solution.py:102
  46.1 7.9 %collective-permute-start = (bf16[128,512]{1,0:T(8,128)(2,1)S(1)}, bf16[128,512]{1,0:T(8,128)(2,1)S(1)}, u32[]{:S(2)}, u32[]{:S(2)}) collective-permute-start(bf16[128,512]{1,0:T(8,128)(2,1)S(1)} %convolution_convert_fusion.2), channel_id=1, source_target_pairs={{0,1},{1,2},{2,3},{3,0},{4,5},{5,6},{6,7},{7,4},{8,9},{9,10},{10,1... | collective-permute-start | bytes 393224 | tf_op jit(solution)/shard_map/ppermute | solution.py:113
  51.9 5.6 %collective-permute-start.1 = (bf16[128,512]{1,0:T(8,128)(2,1)S(1)}, bf16[128,512]{1,0:T(8,128)(2,1)S(1)}, u32[]{:S(2)}, u32[]{:S(2)}) collective-permute-start(bf16[128,512]{1,0:T(8,128)(2,1)S(1)} %convolution_convert_fusion.1), channel_id=1, source_target_pairs={{0,2},{1,3},{2,0},{3,1},{4,6},{5,7},{6,4},{7,5},{8,10},{9,11},{10,... | collective-permute-start | bytes 393224 | tf_op jit(solution)/shard_map/ppermute | solution.py:113
  52.6 6.1 %collective-permute-start.2 = (bf16[128,512]{1,0:T(8,128)(2,1)S(1)}, bf16[128,512]{1,0:T(8,128)(2,1)S(1)}, u32[]{:S(2)}, u32[]{:S(2)}) collective-permute-start(bf16[128,512]{1,0:T(8,128)(2,1)S(1)} %convolution_convert_fusion), channel_id=1, source_target_pairs={{0,3},{1,0},{2,1},{3,2},{4,7},{5,4},{6,5},{7,6},{8,11},{9,8},{10,9... | collective-permute-start | bytes 393224 | tf_op jit(solution)/shard_map/ppermute | solution.py:113

commit v7 on v6

--- a/solution.py
+++ b/solution.py
@@ -46,12 +46,11 @@
         y_ref[k] = y.astype(y_ref.dtype)
 
 
-def pallas_conv(x_cm, f_cm, doc_ids, bias, base):
-    chans, seq = x_cm.shape
-    span = SPAN
-    blocks = seq // span
+def pallas_conv(x_rev, f_cm, doc_ids, bias, base):
+    chans, blocks, span = x_rev.shape
+    seq = blocks * span
     step = CHANNELS_PER_STEP
-    xb = x_cm.reshape(chans, blocks, span)[:, :, ::-1]
+    xb = x_rev
     docb = doc_ids.reshape(blocks, span)
     starts = jnp.sum(doc_ids[None, :] < docb[:, :1], axis=1)
     lag = lax.broadcasted_iota(jnp.int32, (blocks, blocks, span), 1)
@@ -73,7 +72,7 @@
         out_specs=pl.BlockSpec((step, blocks, span), lambda c: (c, 0, 0)),
         out_shape=jax.ShapeDtypeStruct((chans, blocks, span), jnp.bfloat16),
     )(base, bias, f_cm.reshape(chans, 1, seq), xb, docb[:, ::-1], mask)
-    return out[:, :, ::-1]
+    return out
 
 
 def body(signal, gate, filt, bias, doc_ids, block_perm, out_weight):
@@ -85,19 +84,20 @@
     per_dev = chans // n_ctx
     ctx_index = lax.axis_index("ctx")
 
-    inverse = jnp.zeros((blocks,), jnp.int32).at[block_perm].set(jnp.arange(blocks, dtype=jnp.int32))
+    to_seq = (block_perm[None, :] == jnp.arange(blocks, dtype=jnp.int32)[:, None]).astype(jnp.bfloat16)
+    flip = jnp.eye(span, dtype=jnp.bfloat16)[::-1]
 
-    def slots_to_natural(a):
-        return jnp.take(a.reshape(per_dev, blocks, span), inverse, axis=1).reshape(per_dev, seq)
+    def one_hot(spec, *ops):
+        return jnp.einsum(spec, *ops, preferred_element_type=jnp.float32).astype(jnp.bfloat16)
 
     packed = jnp.stack(
         [a.reshape(rows, n_ctx, per_dev) for a in (signal, filt)], axis=2
     ).reshape(rows, n_ctx * 2 * per_dev)
     arrived = lax.all_to_all(packed, "ctx", 1, 0, tiled=True).T
-    x_cm = slots_to_natural(arrived[:per_dev])
+    x_rev = one_hot("tk,ckm->ctm", to_seq, one_hot("ckj,jm->ckm", arrived[:per_dev].reshape(per_dev, blocks, span), flip))
     f_cm = arrived[per_dev:]
-    pre = pallas_conv(x_cm, f_cm, doc_ids, bias, (ctx_index * per_dev).reshape(1))
-    pre_slots = jnp.take(pre, block_perm, axis=1)
+    pre = pallas_conv(x_rev, f_cm, doc_ids, bias, (ctx_index * per_dev).reshape(1))
+    pre_slots = one_hot("tk,ctm->ckm", to_seq, one_hot("ctj,jm->ctm", pre, flip))
     pre_slots = pre_slots.reshape(per_dev, seq).T
     pre_local = lax.all_to_all(pre_slots, "ctx", 0, 1, tiled=True)
     gated_local = (gate.astype(jnp.float32) * pre_local.astype(jnp.float32)).astype(jnp.bfloat16)

time: 59.9 us -> 58.7 us (0.980)
  local copies, waits for them, and re-layouts: 10.7 us -> 6.48 us
  matrix products: 1.68 us -> 4.14 us
  waiting for transfers between devices: 18.4 us -> 19.3 us
    dot_general x0 -> x2, matrix products: none -> 2.47 us  [one_hot(): jnp.einsum(spec, *ops, preferred_element_type=jnp.float32)]
    rev x3 -> x1, local copies, waits for them, and re-layouts: 2.17 us -> 0.03 us  [body(): flip = jnp.eye(span, dtype=jnp.bfloat16)[::-1]]
    gather x2 -> x0, local copies, waits for them, and re-layouts: 1.27 us -> none  [the longest x1 0.63 us: slots_to_natural(): jnp.take(a.reshape(per_dev, blocks, span), inverse, axis=1)]
    all_to_all x1, waiting for transfers between devices: 5.08 us -> 5.9 us  [body(): arrived = lax.all_to_all(packed, 'ctx', 1, 0, tiled=True).T]
    scatter x1 -> x0, local copies, waits for them, and re-layouts: 0.77 us -> none  [body(): jnp.zeros((blocks,), jnp.int32).at[block_perm]]
  transfers between devices with their start and end apart: 5 -> 5, of which waited for: 5 -> 5; matrix products, arithmetic and copies ran while one was open for 7% -> 6% of each run, Pallas kernels for 0% -> 0%
where the time goes in v7:
time: 58.7 us; the launch traced here: 58.4 us
  starting transfers between devices  19.7 us (34%)
  waiting for transfers between devices  19.3 us (33%)
  Pallas kernels  6.97 us (12%)
  local copies, waits for them, and re-layouts  6.48 us (11%)
  matrix products  4.14 us (7%)
  other arithmetic  1.65 us (3%)
    all_to_all x1, starting transfers between devices, body(): arrived = lax.all_to_all(packed, 'ctx', 1, 0, tiled=True).T  9.71 us
    all_to_all x1, waiting for transfers between devices, body(): pre_local = lax.all_to_all(pre_slots, 'ctx', 0, 1, tiled=True)  7.38 us
    pallas_call x1, Pallas kernels, pallas_conv(): pl.pallas_call(conv_kernel, grid=(chans // step,), in_specs=[pl.BlockSpec...  6.97 us
    ppermute x3, starting transfers between devices, body(): lax.ppermute(part.astype(jnp.bfloat16), 'tp', pairs).astype(jnp.float32)  6.1 us
    ppermute x3, waiting for transfers between devices, body(): lax.ppermute(part.astype(jnp.bfloat16), 'tp', pairs).astype(jnp.float32)  5.99 us
    all_to_all x1, waiting for transfers between devices, body(): arrived = lax.all_to_all(packed, 'ctx', 1, 0, tiled=True).T  5.9 us
    all_to_all x1, starting transfers between devices, body(): pre_local = lax.all_to_all(pre_slots, 'ctx', 0, 1, tiled=True)  3.86 us
    dot_general x2, matrix products, one_hot(): jnp.einsum(spec, *ops, preferred_element_type=jnp.float32)  2.47 us
  transfers between devices with their start and end apart: 5, of which 5 were waited for; matrix products, arithmetic and copies ran while one was open for 6% of the time, Pallas kernels for 0%

profile of v7, /device:TPU:1, one launch (start us, length us, event | category | flops | bytes accessed | tf_op | source)
XLA Modules:
  0.0 58.4 jit_solution(12889958149508984186)
XLA Ops:
  0.0 1.2 %copy.48 = bf16[128,512]{0,1:T(8,128)(2,1)S(1)} copy(bf16[128,512]{1,0:T(8,128)(2,1)} %param.7) | data formatting | bytes 262144 | tf_op args[0]
  1.2 1.0 %copy.49 = bf16[128,512]{0,1:T(8,128)(2,1)S(1)} copy(bf16[128,512]{1,0:T(8,128)(2,1)} %param.9) | data formatting | bytes 262144 | tf_op args[2]
  2.3 0.7 %copy.50 = bf16[128,32,2,16]{0,3,2,1:T(8,128)(2,1)} copy(bf16[128,32,2,16]{0,3,1,2:T(8,128)(2,1)S(1)} %pad_maximum_fusion) | data formatting | bytes 524288 | tf_op jit(solution)/shard_map/stack | solution.py:93
  3.0 9.7 %all-to-all-start = ((bf16[128,32,32]{0,2,1:T(8,128)(2,1)}), bf16[128,32,32]{0,2,1:T(8,128)(2,1)S(1)}, u32[]{:S(2)}, u32[]{:S(2)}) async-start(bf16[128,32,32]{0,2,1:T(8,128)(2,1)} %bitcast.3), calls=%async_computation | async-start | bytes 524288 | tf_op jit(solution)/shard_map/all_to_all | solution.py:96
  12.9 0.3 convert_reduce_fusion
  13.4 1.3 %fusion.3.mask_ref = f32[64,4096]{1,0:T(8,128)} fusion(s32[64]{0:T(128)S(1)} %convert_reduce_fusion, s32[4096]{0:T(1024)S(1)} %iota.60, s32[4096]{0:T(1024)S(1)} %iota.55), kind=kLoop, calls=%fused_computation.13 | loop fusion | flops 1835008 | bytes 1081600 | tf_op jit(solution)/shard_map/convert_element_type | solution.py:60
  14.7 0.7 %rev.7.doc_ref = s32[64,64]{1,0:T(8,128)} reverse(s32[64,64]{1,0:T(8,128)S(1)} %reshape.36), dimensions={1} | reverse | bytes 32768 | tf_op jit(solution)/shard_map/rev | solution.py:74
  15.4 5.9 %all-to-all-done = bf16[128,32,32]{0,2,1:T(8,128)(2,1)S(1)} async-done(((bf16[128,32,32]{0,2,1:T(8,128)(2,1)}), bf16[128,32,32]{0,2,1:T(8,128)(2,1)S(1)}, u32[]{:S(2)}, u32[]{:S(2)}) %all-to-all-start) | async-done | bytes 262176 | tf_op jit(solution)/shard_map/all_to_all | solution.py:96
  21.6 1.0 %copy.54.f_ref = bf16[16,1,4096]{2,1,0:T(2,128)(2,1)} copy(bf16[16,1,4096]{2,0,1:T(8,128)(2,1)S(1)} %get-tuple-element.6) | data formatting | bytes 262144 | tf_op jit(solution)/shard_map/reshape | solution.py:74
  22.5 1.1 %fusion.x_ref = bf16[16,64,64]{2,1,0:T(8,128)(2,1)} fusion(bf16[16,64,64]{2,1,0:T(8,128)(2,1)S(1)} %reshape.35, bf16[64,64]{1,0:T(8,128)(2,1)S(1)} %rev.6, s32[64]{0:T(128)S(1)} %copy-done.3), kind=kOutput, calls=%fused_computation.4 | convolution fusion | flops 16912384 | bytes 270592 | tf_op jit(solution)/shard_map/tk,ckm->ctm/dot_general | solution.py:91
  23.6 7.0 %shard_map.73 = bf16[16,64,64]{2,1,0:T(8,128)(2,1)} custom-call(s32[1]{0:T(128)} %bitcast.base_ref, f32[512]{0:T(512)} %bias_ref.1, bf16[16,1,4096]{2,1,0:T(2,128)(2,1)} %copy.54.f_ref, bf16[16,64,64]{2,1,0:T(8,128)(2,1)} %fusion.x_ref, s32[64,64]{1,0:T(8,128)} %rev.7.doc_ref, f32[64,4096]{1,0:T(8,128)} %fusion.3.mask_ref), custom_call_target="tpu_custom_call" | custom-call | tf_op jit(solution)/shard_map/pallas_call | solution.py:61
  30.6 1.4 %fusion.1 = bf16[16,64,64]{1,2,0:T(8,128)(2,1)S(1)} fusion(bf16[16,64,64]{2,1,0:T(8,128)(2,1)} %shard_map.73, bf16[64,64]{1,0:T(8,128)(2,1)S(1)} %rev.6, s32[64]{0:T(128)S(1)} %copy-done.3), kind=kOutput, calls=%fused_computation.5 | convolution fusion | flops 16912384 | bytes 270592 | tf_op jit(solution)/shard_map/tk,ctm->ckm/dot_general | solution.py:91
  32.2 0.3 reshape.37
  32.4 0.7 %copy_bitcast_fusion = bf16[32,128,16]{1,2,0:T(8,128)(2,1)} fusion(bf16[16,4096]{1,0:T(8,128)(2,1)S(1)} %reshape.37), kind=kLoop, calls=%fused_computation.24 | loop fusion | bytes 262144 | tf_op jit(solution)/shard_map/all_to_all | solution.py:102
  33.1 3.9 %all-to-all-start.1 = ((bf16[32,128,16]{1,2,0:T(8,128)(2,1)}), bf16[32,128,16]{1,2,0:T(8,128)(2,1)S(1)}, u32[]{:S(2)}, u32[]{:S(2)}) async-start(bf16[32,128,16]{1,2,0:T(8,128)(2,1)} %copy_bitcast_fusion), calls=%async_computation.1 | async-start | bytes 262144 | tf_op jit(solution)/shard_map/all_to_all | solution.py:102
  37.2 7.4 %all-to-all-done.1 = bf16[32,128,16]{1,2,0:T(8,128)(2,1)S(1)} async-done(((bf16[32,128,16]{1,2,0:T(8,128)(2,1)}), bf16[32,128,16]{1,2,0:T(8,128)(2,1)S(1)}, u32[]{:S(2)}, u32[]{:S(2)}) %all-to-all-start.1) | async-done | bytes 131104 | tf_op jit(solution)/shard_map/all_to_all | solution.py:102
  44.6 0.3 convolution_convert_fusion.6
  44.9 5.5 %collective-permute-start = (bf16[128,512]{1,0:T(8,128)(2,1)S(1)}, bf16[128,512]{1,0:T(8,128)(2,1)S(1)}, u32[]{:S(2)}, u32[]{:S(2)}) collective-permute-start(bf16[128,512]{1,0:T(8,128)(2,1)S(1)} %convolution_convert_fusion.6), channel_id=1, source_target_pairs={{0,1},{1,2},{2,3},{3,0},{4,5},{5,6},{6,7},{7,4},{8,9},{9,10},{10,1... | collective-permute-start | bytes 393224 | tf_op jit(solution)/shard_map/ppermute | solution.py:113
  50.4 0.2 convolution_convert_fusion.5
  50.7 0.4 collective-permute-start.1
  51.5 1.3 %collective-permute-done = bf16[128,512]{1,0:T(8,128)(2,1)S(1)} collective-permute-done((bf16[128,512]{1,0:T(8,128)(2,1)S(1)}, bf16[128,512]{1,0:T(8,128)(2,1)S(1)}, u32[]{:S(2)}, u32[]{:S(2)}) %collective-permute-start) | collective-permute-done | bytes 131104 | tf_op jit(solution)/shard_map/ppermute | solution.py:113
  52.8 3.4 %collective-permute-done.1 = bf16[128,512]{1,0:T(8,128)(2,1)S(1)} collective-permute-done((bf16[128,512]{1,0:T(8,128)(2,1)S(1)}, bf16[128,512]{1,0:T(8,128)(2,1)S(1)}, u32[]{:S(2)}, u32[]{:S(2)}) %collective-permute-start.1) | collective-permute-done | bytes 131104 | tf_op jit(solution)/shard_map/ppermute | solution.py:113
  56.2 1.2 %collective-permute-done.2 = bf16[128,512]{1,0:T(8,128)(2,1)S(1)} collective-permute-done((bf16[128,512]{1,0:T(8,128)(2,1)S(1)}, bf16[128,512]{1,0:T(8,128)(2,1)S(1)}, u32[]{:S(2)}, u32[]{:S(2)}) %collective-permute-start.2) | collective-permute-done | bytes 131104 | tf_op jit(solution)/shard_map/ppermute | solution.py:113
  57.5 0.9 %add_convert_fusion = bf16[128,512]{1,0:T(8,128)(2,1)} fusion(bf16[128,512]{1,0:T(8,128)(2,1)S(1)} %collective-permute-done.2, bf16[128,512]{1,0:T(8,128)(2,1)S(1)} %collective-permute-done.1, bf16[128,512]{1,0:T(8,128)(2,1)S(1)} %collective-permute-done, bf16[128,512]{0,1:T(8,128)(2,1)S(1)} %fusion.9, bf16[512,2048]{1,0:T(8,128)(2,1)S(1)} %copy-done, ...), kind=kOutput, calls=%fused_computation.23 | convolution fusion | flops 67567616 | bytes 1179652 | tf_op jit(solution)/shard_map/dot_general | solution.py:110
  (26 shorter events, 1.4 us)
Async XLA Ops:
  0.0 44.6 %copy-start = (bf16[512,2048]{1,0:T(8,128)(2,1)S(1)}, bf16[512,2048]{1,0:T(8,128)(2,1)}, u32[]{:S(2)}) copy-start(bf16[512,2048]{1,0:T(8,128)(2,1)} %param.13) | copy-start | bytes 6291460
  0.0 12.7 %copy-start.2 = (s32[4096]{0:T(1024)S(1)}, s32[4096]{0:T(1024)}, u32[]{:S(2)}) copy-start(s32[4096]{0:T(1024)} %param.11) | copy-start | bytes 49156
  2.3 20.3 %copy-start.3 = (s32[64]{0:T(128)S(1)}, s32[64]{0:T(128)}, u32[]{:S(2)}) copy-start(s32[64]{0:T(128)} %param.12) | copy-start | bytes 772
  3.0 18.3 %all-to-all-start = ((bf16[128,32,32]{0,2,1:T(8,128)(2,1)}), bf16[128,32,32]{0,2,1:T(8,128)(2,1)S(1)}, u32[]{:S(2)}, u32[]{:S(2)}) async-start(bf16[128,32,32]{0,2,1:T(8,128)(2,1)} %bitcast.3), calls=%async_computation | async-start | bytes 524288 | tf_op jit(solution)/shard_map/all_to_all | solution.py:96
  23.6 13.4 %copy-start.1 = (bf16[128,512]{1,0:T(8,128)(2,1)S(1)}, bf16[128,512]{1,0:T(8,128)(2,1)}, u32[]{:S(2)}) copy-start(bf16[128,512]{1,0:T(8,128)(2,1)} %param.8) | copy-start | bytes 393220
  33.1 11.4 %all-to-all-start.1 = ((bf16[32,128,16]{1,2,0:T(8,128)(2,1)}), bf16[32,128,16]{1,2,0:T(8,128)(2,1)S(1)}, u32[]{:S(2)}, u32[]{:S(2)}) async-start(bf16[32,128,16]{1,2,0:T(8,128)(2,1)} %copy_bitcast_fusion), calls=%async_computation.1 | async-start | bytes 262144 | tf_op jit(solution)/shard_map/all_to_all | solution.py:102
  44.9 7.9 %collective-permute-start = (bf16[128,512]{1,0:T(8,128)(2,1)S(1)}, bf16[128,512]{1,0:T(8,128)(2,1)S(1)}, u32[]{:S(2)}, u32[]{:S(2)}) collective-permute-start(bf16[128,512]{1,0:T(8,128)(2,1)S(1)} %convolution_convert_fusion.6), channel_id=1, source_target_pairs={{0,1},{1,2},{2,3},{3,0},{4,5},{5,6},{6,7},{7,4},{8,9},{9,10},{10,1... | collective-permute-start | bytes 393224 | tf_op jit(solution)/shard_map/ppermute | solution.py:113
  50.7 5.6 %collective-permute-start.1 = (bf16[128,512]{1,0:T(8,128)(2,1)S(1)}, bf16[128,512]{1,0:T(8,128)(2,1)S(1)}, u32[]{:S(2)}, u32[]{:S(2)}) collective-permute-start(bf16[128,512]{1,0:T(8,128)(2,1)S(1)} %convolution_convert_fusion.5), channel_id=1, source_target_pairs={{0,2},{1,3},{2,0},{3,1},{4,6},{5,7},{6,4},{7,5},{8,10},{9,11},{10,... | collective-permute-start | bytes 393224 | tf_op jit(solution)/shard_map/ppermute | solution.py:113
  51.3 6.1 %collective-permute-start.2 = (bf16[128,512]{1,0:T(8,128)(2,1)S(1)}, bf16[128,512]{1,0:T(8,128)(2,1)S(1)}, u32[]{:S(2)}, u32[]{:S(2)}) collective-permute-start(bf16[128,512]{1,0:T(8,128)(2,1)S(1)} %convolution_convert_fusion.4), channel_id=1, source_target_pairs={{0,3},{1,0},{2,1},{3,2},{4,7},{5,4},{6,5},{7,6},{8,11},{9,8},{10,9... | collective-permute-start | bytes 393224 | tf_op jit(solution)/shard_map/ppermute | solution.py:113

commit v8 on v7

--- a/solution.py
+++ b/solution.py
@@ -103,16 +103,22 @@
     gated_local = (gate.astype(jnp.float32) * pre_local.astype(jnp.float32)).astype(jnp.bfloat16)
     tp_index = lax.axis_index("tp")
     n_tp = out_weight.shape[1] // chans
-    total = None
-    for offset in range(n_tp):
-        target = (tp_index + offset) % n_tp
-        w_cols = lax.dynamic_slice_in_dim(out_weight, target * chans, chans, axis=1)
-        part = jnp.dot(gated_local, w_cols, preferred_element_type=jnp.float32)
-        if offset:
-            pairs = [(i, (i + offset) % n_tp) for i in range(n_tp)]
-            part = lax.ppermute(part.astype(jnp.bfloat16), "tp", pairs).astype(jnp.float32)
-        total = part if total is None else total + part
-    return total.astype(jnp.bfloat16)
+    high, core = tp_index // 2, tp_index % 2
+    w_split = out_weight.reshape(chans, n_tp // 2, 2, chans)
+    w_other = lax.dynamic_index_in_dim(w_split, 1 - core, axis=2, keepdims=False)
+    p_other = jnp.dot(
+        gated_local, w_other.reshape(chans, -1), preferred_element_type=jnp.float32
+    )
+    recv_core = lax.ppermute(p_other.astype(jnp.bfloat16), "tp", [(i, i ^ 1) for i in range(n_tp)])
+    w_mine = lax.dynamic_index_in_dim(w_split, core, axis=2, keepdims=False)
+    p_mine = jnp.dot(gated_local, w_mine.reshape(chans, -1), preferred_element_type=jnp.float32)
+    p_mine = p_mine + recv_core.astype(jnp.float32)
+    send_high = lax.dynamic_slice_in_dim(p_mine, (1 - high) * chans, chans, axis=1)
+    keep_high = lax.dynamic_slice_in_dim(p_mine, high * chans, chans, axis=1)
+    recv_high = lax.ppermute(
+        send_high.astype(jnp.bfloat16), "tp", [(i, i ^ 2) for i in range(n_tp)]
+    )
+    return (keep_high + recv_high.astype(jnp.float32)).astype(jnp.bfloat16)
 
 
 def solution(mesh):

time: 58.7 us -> 57.7 us (0.983)
  waiting for transfers between devices: 19.3 us -> 13.9 us
  local copies, waits for them, and re-layouts: 6.48 us -> 10.4 us
  matrix products: 4.14 us -> 3.43 us
  other arithmetic: 1.65 us -> 2.33 us
    all_to_all x1, waiting for transfers between devices: 5.9 us -> 2.83 us  [body(): arrived = lax.all_to_all(packed, 'ctx', 1, 0, tiled=True).T]
    unnamed x11 -> x12, local copies, waits for them, and re-layouts: 2.34 us -> 5.09 us
    ppermute x3 -> x2, waiting for transfers between devices: 5.99 us -> 4.72 us  [the longest x1 3.56 us: body(): lax.ppermute(send_high.astype(jnp.bfloat16), 'tp', [(i, i ^ 2) for i in r...]
    dynamic_slice x0 -> x1, local copies, waits for them, and re-layouts: none -> 1.18 us  [body(): lax.dynamic_index_in_dim(w_split, 1 - core, axis=2, keepdims=False)]
    all_to_all x1, starting transfers between devices: 3.86 us -> 4.91 us  [body(): pre_local = lax.all_to_all(pre_slots, 'ctx', 0, 1, tiled=True)]
    all_to_all x1, waiting for transfers between devices: 7.38 us -> 6.39 us  [body(): pre_local = lax.all_to_all(pre_slots, 'ctx', 0, 1, tiled=True)]
    dot_general x4 -> x2, matrix products: 1.68 us -> 0.96 us  [the longest x1 0.48 us: body(): jnp.dot(gated_local, w_other.reshape(chans, -1), preferred_element_type=j...]
    convert_element_type x0 -> x1, other arithmetic: none -> 0.68 us  [body(): return (keep_high + recv_high.astype(jnp.float32)).astype(jnp.bfloat16)]
  transfers between devices with their start and end apart: 5 -> 4, of which waited for: 5 -> 4; matrix products, arithmetic and copies ran while one was open for 6% -> 12% of each run, Pallas kernels for 0% -> 0%
where the time goes in v8:
time: 57.7 us; the launch traced here: 57.3 us
  starting transfers between devices  20.1 us (35%)
  waiting for transfers between devices  13.9 us (24%)
  local copies, waits for them, and re-layouts  10.4 us (18%)
  Pallas kernels  6.94 us (12%)
  matrix products  3.43 us (6%)
  other arithmetic  2.33 us (4%)
    all_to_all x1, starting transfers between devices, body(): arrived = lax.all_to_all(packed, 'ctx', 1, 0, tiled=True).T  9.71 us
    pallas_call x1, Pallas kernels, pallas_conv(): pl.pallas_call(conv_kernel, grid=(chans // step,), in_specs=[pl.BlockSpec...  6.94 us
    all_to_all x1, waiting for transfers between devices, body(): pre_local = lax.all_to_all(pre_slots, 'ctx', 0, 1, tiled=True)  6.39 us
    unnamed x12, local copies, waits for them, and re-layouts  5.09 us
    all_to_all x1, starting transfers between devices, body(): pre_local = lax.all_to_all(pre_slots, 'ctx', 0, 1, tiled=True)  4.91 us
    ppermute x1, waiting for transfers between devices, body(): lax.ppermute(send_high.astype(jnp.bfloat16), 'tp', [(i, i ^ 2) for i in r...  3.56 us
    all_to_all x1, waiting for transfers between devices, body(): arrived = lax.all_to_all(packed, 'ctx', 1, 0, tiled=True).T  2.83 us
    ppermute x1, starting transfers between devices, body(): lax.ppermute(p_other.astype(jnp.bfloat16), 'tp', [(i, i ^ 1) for i in ran...  2.73 us
  transfers between devices with their start and end apart: 4, of which 4 were waited for; matrix products, arithmetic and copies ran while one was open for 12% of the time, Pallas kernels for 0%

profile of v8, /device:TPU:1, one launch (start us, length us, event | category | flops | bytes accessed | tf_op | source)
XLA Modules:
  0.0 57.3 jit_solution(2961583515657600463)
XLA Ops:
  0.0 1.0 %copy.51 = bf16[128,512]{0,1:T(8,128)(2,1)S(1)} copy(bf16[128,512]{1,0:T(8,128)(2,1)} %param.7) | data formatting | bytes 262144 | tf_op args[0]
  1.0 1.0 %copy.52 = bf16[128,512]{0,1:T(8,128)(2,1)S(1)} copy(bf16[128,512]{1,0:T(8,128)(2,1)} %param.9) | data formatting | bytes 262144 | tf_op args[2]
  2.1 0.7 %copy.53 = bf16[128,32,2,16]{0,3,2,1:T(8,128)(2,1)} copy(bf16[128,32,2,16]{0,3,1,2:T(8,128)(2,1)S(1)} %pad_maximum_fusion) | data formatting | bytes 524288 | tf_op jit(solution)/shard_map/stack | solution.py:93
  2.8 9.7 %all-to-all-start = ((bf16[128,32,32]{0,2,1:T(8,128)(2,1)}), bf16[128,32,32]{0,2,1:T(8,128)(2,1)S(1)}, u32[]{:S(2)}, u32[]{:S(2)}) async-start(bf16[128,32,32]{0,2,1:T(8,128)(2,1)} %bitcast.3), calls=%async_computation | async-start | bytes 524288 | tf_op jit(solution)/shard_map/all_to_all | solution.py:96
  12.8 0.3 convert_reduce_fusion
  13.2 1.3 %fusion.3.mask_ref = f32[64,4096]{1,0:T(8,128)} fusion(s32[64]{0:T(128)S(1)} %convert_reduce_fusion, s32[4096]{0:T(1024)S(1)} %iota.60, s32[4096]{0:T(1024)S(1)} %iota.55), kind=kLoop, calls=%fused_computation.11 | loop fusion | flops 1835008 | bytes 1081600 | tf_op jit(solution)/shard_map/convert_element_type | solution.py:60
  14.5 0.7 %rev.7.doc_ref = s32[64,64]{1,0:T(8,128)} reverse(s32[64,64]{1,0:T(8,128)S(1)} %reshape.47), dimensions={1} | reverse | bytes 32768 | tf_op jit(solution)/shard_map/rev | solution.py:74
  15.2 2.9 %copy.61 = bf16[512,2048]{0,1:T(8,128)(2,1)S(1)} copy(bf16[512,2048]{1,0:T(8,128)(2,1)} %param.13) | data formatting | bytes 4194304 | tf_op args[6]
  18.3 2.8 %all-to-all-done = bf16[128,32,32]{0,2,1:T(8,128)(2,1)S(1)} async-done(((bf16[128,32,32]{0,2,1:T(8,128)(2,1)}), bf16[128,32,32]{0,2,1:T(8,128)(2,1)S(1)}, u32[]{:S(2)}, u32[]{:S(2)}) %all-to-all-start) | async-done | bytes 262176 | tf_op jit(solution)/shard_map/all_to_all | solution.py:96
  21.4 1.0 %copy.57.f_ref = bf16[16,1,4096]{2,1,0:T(2,128)(2,1)} copy(bf16[16,1,4096]{2,0,1:T(8,128)(2,1)S(1)} %get-tuple-element.8) | data formatting | bytes 262144 | tf_op jit(solution)/shard_map/reshape | solution.py:74
  22.4 1.1 %fusion.x_ref = bf16[16,64,64]{2,1,0:T(8,128)(2,1)} fusion(bf16[16,64,64]{2,1,0:T(8,128)(2,1)S(1)} %reshape.46, bf16[64,64]{1,0:T(8,128)(2,1)S(1)} %rev.6, s32[64]{0:T(128)S(1)} %copy-done.3), kind=kOutput, calls=%fused_computation.5 | convolution fusion | flops 16912384 | bytes 270592 | tf_op jit(solution)/shard_map/tk,ckm->ctm/dot_general | solution.py:91
  23.5 6.9 %shard_map.73 = bf16[16,64,64]{2,1,0:T(8,128)(2,1)} custom-call(s32[1]{0:T(128)} %bitcast.base_ref, f32[512]{0:T(512)} %bias_ref.1, bf16[16,1,4096]{2,1,0:T(2,128)(2,1)} %copy.57.f_ref, bf16[16,64,64]{2,1,0:T(8,128)(2,1)} %fusion.x_ref, s32[64,64]{1,0:T(8,128)} %rev.7.doc_ref, f32[64,4096]{1,0:T(8,128)} %fusion.3.mask_ref), custom_call_target="tpu_custom_call" | custom-call | tf_op jit(solution)/shard_map/pallas_call | solution.py:61
  30.4 1.4 %fusion.1 = bf16[16,64,64]{1,2,0:T(8,128)(2,1)S(1)} fusion(bf16[16,64,64]{2,1,0:T(8,128)(2,1)} %shard_map.73, bf16[64,64]{1,0:T(8,128)(2,1)S(1)} %rev.6, s32[64]{0:T(128)S(1)} %copy-done.3), kind=kOutput, calls=%fused_computation.6 | convolution fusion | flops 16912384 | bytes 270592 | tf_op jit(solution)/shard_map/tk,ctm->ckm/dot_general | solution.py:91
  32.2 0.7 %copy_bitcast_fusion = bf16[32,128,16]{1,2,0:T(8,128)(2,1)} fusion(bf16[16,4096]{1,0:T(8,128)(2,1)S(1)} %reshape.48), kind=kLoop, calls=%fused_computation.19 | loop fusion | bytes 262144 | tf_op jit(solution)/shard_map/all_to_all | solution.py:102
  32.9 4.9 %all-to-all-start.1 = ((bf16[32,128,16]{1,2,0:T(8,128)(2,1)}), bf16[32,128,16]{1,2,0:T(8,128)(2,1)S(1)}, u32[]{:S(2)}, u32[]{:S(2)}) async-start(bf16[32,128,16]{1,2,0:T(8,128)(2,1)} %copy_bitcast_fusion), calls=%async_computation.1 | async-start | bytes 262144 | tf_op jit(solution)/shard_map/all_to_all | solution.py:102
  37.8 1.2 %constant_dynamic-slice_fusion = (bf16[512,2,1,512]{0,3,2,1:T(8,128)(2,1)S(1)}, bf16[512,2,1,512]{0,3,2,1:T(8,128)(2,1)}) fusion(bf16[512,2,2,512]{0,3,2,1:T(8,128)(2,1)S(1)} %bitcast.50, s32[]{:T(128)S(6)} %select_n.26, s32[]{:T(128)S(6)} %select_n.25), kind=kLoop, calls=%fused_computation.30 | loop fusion | bytes 4194312 | tf_op jit(solution)/shard_map/jit(dynamic_index_in_dim)/dynamic_slice | solution.py:108
  39.0 6.4 %all-to-all-done.1 = bf16[32,128,16]{1,2,0:T(8,128)(2,1)S(1)} async-done(((bf16[32,128,16]{1,2,0:T(8,128)(2,1)}), bf16[32,128,16]{1,2,0:T(8,128)(2,1)S(1)}, u32[]{:S(2)}, u32[]{:S(2)}) %all-to-all-start.1) | async-done | bytes 131104 | tf_op jit(solution)/shard_map/all_to_all | solution.py:102
  45.5 0.5 convolution_convert_fusion
  45.9 2.7 %collective-permute-start = (bf16[128,1024]{1,0:T(8,128)(2,1)S(1)}, bf16[128,1024]{1,0:T(8,128)(2,1)S(1)}, u32[]{:S(2)}, u32[]{:S(2)}) collective-permute-start(bf16[128,1024]{1,0:T(8,128)(2,1)S(1)} %convolution_convert_fusion), channel_id=1, source_target_pairs={{0,1},{1,0},{2,3},{3,2},{4,5},{5,4},{6,7},{7,6},{8,9},{9,8},{10,11... | collective-permute-start | bytes 786440 | tf_op jit(solution)/shard_map/ppermute | solution.py:112
  48.7 1.2 %collective-permute-done = bf16[128,1024]{1,0:T(8,128)(2,1)S(1)} collective-permute-done((bf16[128,1024]{1,0:T(8,128)(2,1)S(1)}, bf16[128,1024]{1,0:T(8,128)(2,1)S(1)}, u32[]{:S(2)}, u32[]{:S(2)}) %collective-permute-start) | collective-permute-done | bytes 262176 | tf_op jit(solution)/shard_map/ppermute | solution.py:112
  49.8 0.5 convert_add_fusion
  50.4 2.7 %collective-permute-start.1 = (bf16[128,512]{1,0:T(8,128)(2,1)S(1)}, bf16[128,512]{1,0:T(8,128)(2,1)S(1)}, u32[]{:S(2)}, u32[]{:S(2)}) collective-permute-start(bf16[128,512]{1,0:T(8,128)(2,1)S(1)} %dynamic-slice_convert_fusion), channel_id=1, source_target_pairs={{0,2},{1,3},{2,0},{3,1},{4,6},{5,7},{6,4},{7,5},{8,10},{9,11},{10,... | collective-permute-start | bytes 393224 | tf_op jit(solution)/shard_map/ppermute | solution.py:118
  53.1 3.6 %collective-permute-done.1 = bf16[128,512]{1,0:T(8,128)(2,1)S(1)} collective-permute-done((bf16[128,512]{1,0:T(8,128)(2,1)S(1)}, bf16[128,512]{1,0:T(8,128)(2,1)S(1)}, u32[]{:S(2)}, u32[]{:S(2)}) %collective-permute-start.1) | collective-permute-done | bytes 131104 | tf_op jit(solution)/shard_map/ppermute | solution.py:118
  56.6 0.7 %add_convert_fusion = bf16[128,512]{1,0:T(8,128)(2,1)} fusion(bf16[128,512]{1,0:T(8,128)(2,1)S(1)} %collective-permute-done.1, f32[128,1024]{1,0:T(8,128)S(1)} %convert_add_fusion, s32[]{:T(128)S(6)} %select_n.28), kind=kLoop, calls=%fused_computation.17 | loop fusion | flops 196608 | bytes 524292 | tf_op jit(solution)/shard_map/convert_element_type | solution.py:121
  (26 shorter events, 1.3 us)
Async XLA Ops:
  0.0 12.6 %copy-start.2 = (s32[4096]{0:T(1024)S(1)}, s32[4096]{0:T(1024)}, u32[]{:S(2)}) copy-start(s32[4096]{0:T(1024)} %param.11) | copy-start | bytes 49156
  2.8 18.3 %all-to-all-start = ((bf16[128,32,32]{0,2,1:T(8,128)(2,1)}), bf16[128,32,32]{0,2,1:T(8,128)(2,1)S(1)}, u32[]{:S(2)}, u32[]{:S(2)}) async-start(bf16[128,32,32]{0,2,1:T(8,128)(2,1)} %bitcast.3), calls=%async_computation | async-start | bytes 524288 | tf_op jit(solution)/shard_map/all_to_all | solution.py:96
  15.2 3.0 %copy-start.1 = (bf16[128,512]{1,0:T(8,128)(2,1)S(1)}, bf16[128,512]{1,0:T(8,128)(2,1)}, u32[]{:S(2)}) copy-start(bf16[128,512]{1,0:T(8,128)(2,1)} %param.8) | copy-start | bytes 393220
  18.1 4.3 %copy-start.3 = (s32[64]{0:T(128)S(1)}, s32[64]{0:T(128)}, u32[]{:S(2)}) copy-start(s32[64]{0:T(128)} %param.12) | copy-start | bytes 772
  32.9 12.5 %all-to-all-start.1 = ((bf16[32,128,16]{1,2,0:T(8,128)(2,1)}), bf16[32,128,16]{1,2,0:T(8,128)(2,1)S(1)}, u32[]{:S(2)}, u32[]{:S(2)}) async-start(bf16[32,128,16]{1,2,0:T(8,128)(2,1)} %copy_bitcast_fusion), calls=%async_computation.1 | async-start | bytes 262144 | tf_op jit(solution)/shard_map/all_to_all | solution.py:102
  39.0 10.8 %copy-start = (bf16[512,2,1,512]{0,3,2,1:T(8,128)(2,1)S(1)}, bf16[512,2,1,512]{0,3,2,1:T(8,128)(2,1)}, u32[]{:S(2)}) copy-start(bf16[512,2,1,512]{0,3,2,1:T(8,128)(2,1)} %get-tuple-element.6) | copy-start | bytes 3145732
  45.9 3.9 %collective-permute-start = (bf16[128,1024]{1,0:T(8,128)(2,1)S(1)}, bf16[128,1024]{1,0:T(8,128)(2,1)S(1)}, u32[]{:S(2)}, u32[]{:S(2)}) collective-permute-start(bf16[128,1024]{1,0:T(8,128)(2,1)S(1)} %convolution_convert_fusion), channel_id=1, source_target_pairs={{0,1},{1,0},{2,3},{3,2},{4,5},{5,4},{6,7},{7,6},{8,9},{9,8},{10,11... | collective-permute-start | bytes 786440 | tf_op jit(solution)/shard_map/ppermute | solution.py:112
  50.4 6.3 %collective-permute-start.1 = (bf16[128,512]{1,0:T(8,128)(2,1)S(1)}, bf16[128,512]{1,0:T(8,128)(2,1)S(1)}, u32[]{:S(2)}, u32[]{:S(2)}) collective-permute-start(bf16[128,512]{1,0:T(8,128)(2,1)S(1)} %dynamic-slice_convert_fusion), channel_id=1, source_target_pairs={{0,2},{1,3},{2,0},{3,1},{4,6},{5,7},{6,4},{7,5},{8,10},{9,11},{10,... | collective-permute-start | bytes 393224 | tf_op jit(solution)/shard_map/ppermute | solution.py:118

commit v9 on v8

--- a/solution.py
+++ b/solution.py
@@ -23,7 +23,7 @@
     contract = (((1,), (1,)), ((), ()))
     for k in range(x_ref.shape[0]):
         channel = pl.program_id(0) * x_ref.shape[0] + k
-        frow = f_ref[k].astype(jnp.float32)
+        frow = f_ref[k : k + 1, :].astype(jnp.float32)
         frow = jnp.concatenate([frow, jnp.zeros((1, lanes), jnp.float32)], axis=1)
         fb = jnp.broadcast_to(frow, (span, seq + lanes))
         tt = pltpu.roll(fb, 0, 1, stride=1, stride_axis=0)[:, :seq].astype(jnp.bfloat16)
@@ -64,14 +64,14 @@
         in_specs=[
             pl.BlockSpec(memory_space=pltpu.SMEM),
             pl.BlockSpec(memory_space=pltpu.SMEM),
-            pl.BlockSpec((step, 1, seq), lambda c: (c, 0, 0)),
+            pl.BlockSpec((step, seq), lambda c: (c, 0)),
             pl.BlockSpec((step, blocks, span), lambda c: (c, 0, 0)),
             pl.BlockSpec((blocks, span), lambda c: (0, 0)),
             pl.BlockSpec((blocks, seq), lambda c: (0, 0)),
         ],
         out_specs=pl.BlockSpec((step, blocks, span), lambda c: (c, 0, 0)),
         out_shape=jax.ShapeDtypeStruct((chans, blocks, span), jnp.bfloat16),
-    )(base, bias, f_cm.reshape(chans, 1, seq), xb, docb[:, ::-1], mask)
+    )(base, bias, f_cm, xb, docb[:, ::-1], mask)
     return out
 
 

time: 57.7 us -> 57.3 us (level)
    reshape x1 -> x0, local copies, waits for them, and re-layouts: 0.95 us -> none  [pallas_conv(): f_cm.reshape(chans, 1, seq)]
    slice x1, local copies, waits for them, and re-layouts: 0.02 us -> 0.67 us  [body(): arrived[:per_dev].reshape(per_dev, blocks, span)]
where the time goes in v9:
time: 57.3 us; the launch traced here: 56.9 us
  starting transfers between devices  20 us (35%)
  waiting for transfers between devices  14 us (24%)
  local copies, waits for them, and re-layouts  10.1 us (18%)
  Pallas kernels  6.85 us (12%)
  matrix products  3.43 us (6%)
  other arithmetic  2.33 us (4%)
    all_to_all x1, starting transfers between devices, body(): arrived = lax.all_to_all(packed, 'ctx', 1, 0, tiled=True).T  9.71 us
    pallas_call x1, Pallas kernels, pallas_conv(): pl.pallas_call(conv_kernel, grid=(chans // step,), in_specs=[pl.BlockSpec...  6.85 us
    all_to_all x1, waiting for transfers between devices, body(): pre_local = lax.all_to_all(pre_slots, 'ctx', 0, 1, tiled=True)  6.39 us
    unnamed x12, local copies, waits for them, and re-layouts  5.08 us
    all_to_all x1, starting transfers between devices, body(): pre_local = lax.all_to_all(pre_slots, 'ctx', 0, 1, tiled=True)  4.89 us
    ppermute x1, waiting for transfers between devices, body(): lax.ppermute(send_high.astype(jnp.bfloat16), 'tp', [(i, i ^ 2) for i in r...  3.56 us
    all_to_all x1, waiting for transfers between devices, body(): arrived = lax.all_to_all(packed, 'ctx', 1, 0, tiled=True).T  2.85 us
    ppermute x1, starting transfers between devices, body(): lax.ppermute(p_other.astype(jnp.bfloat16), 'tp', [(i, i ^ 1) for i in ran...  2.74 us
  transfers between devices with their start and end apart: 4, of which 4 were waited for; matrix products, arithmetic and copies ran while one was open for 12% of the time, Pallas kernels for 0%

profile of v9, /device:TPU:1, one launch (start us, length us, event | category | flops | bytes accessed | tf_op | source)
XLA Modules:
  0.0 56.9 jit_solution(17698662189460011197)
XLA Ops:
  0.0 1.0 %copy.37 = bf16[128,512]{0,1:T(8,128)(2,1)S(1)} copy(bf16[128,512]{1,0:T(8,128)(2,1)} %param.7) | data formatting | bytes 262144 | tf_op args[0]
  1.0 1.0 %copy.38 = bf16[128,512]{0,1:T(8,128)(2,1)S(1)} copy(bf16[128,512]{1,0:T(8,128)(2,1)} %param.9) | data formatting | bytes 262144 | tf_op args[2]
  2.1 0.7 %copy.39 = bf16[128,32,2,16]{0,3,2,1:T(8,128)(2,1)} copy(bf16[128,32,2,16]{0,3,1,2:T(8,128)(2,1)S(1)} %pad_maximum_fusion) | data formatting | bytes 524288 | tf_op jit(solution)/shard_map/stack | solution.py:93
  2.8 9.7 %all-to-all-start = ((bf16[128,32,32]{0,2,1:T(8,128)(2,1)}), bf16[128,32,32]{0,2,1:T(8,128)(2,1)S(1)}, u32[]{:S(2)}, u32[]{:S(2)}) async-start(bf16[128,32,32]{0,2,1:T(8,128)(2,1)} %bitcast.3), calls=%async_computation | async-start | bytes 524288 | tf_op jit(solution)/shard_map/all_to_all | solution.py:96
  12.8 0.3 convert_reduce_fusion
  13.2 1.3 %fusion.3.mask_ref = f32[64,4096]{1,0:T(8,128)} fusion(s32[64]{0:T(128)S(1)} %convert_reduce_fusion, s32[4096]{0:T(1024)S(1)} %iota.60, s32[4096]{0:T(1024)S(1)} %iota.55), kind=kLoop, calls=%fused_computation.11 | loop fusion | flops 1835008 | bytes 1081600 | tf_op jit(solution)/shard_map/convert_element_type | solution.py:60
  14.5 0.7 %rev.7.doc_ref = s32[64,64]{1,0:T(8,128)} reverse(s32[64,64]{1,0:T(8,128)S(1)} %reshape.43), dimensions={1} | reverse | bytes 32768 | tf_op jit(solution)/shard_map/rev | solution.py:74
  15.2 2.9 %copy.46 = bf16[512,2048]{0,1:T(8,128)(2,1)S(1)} copy(bf16[512,2048]{1,0:T(8,128)(2,1)} %param.13) | data formatting | bytes 4194304 | tf_op args[6]
  18.3 2.8 %all-to-all-done = bf16[128,32,32]{0,2,1:T(8,128)(2,1)S(1)} async-done(((bf16[128,32,32]{0,2,1:T(8,128)(2,1)}), bf16[128,32,32]{0,2,1:T(8,128)(2,1)S(1)}, u32[]{:S(2)}, u32[]{:S(2)}) %all-to-all-start) | async-done | bytes 262176 | tf_op jit(solution)/shard_map/all_to_all | solution.py:96
  21.1 0.7 %fusion.15 = (bf16[16,4096]{1,0:T(8,128)(2,1)S(1)}, bf16[16,4096]{1,0:T(8,128)(2,1)}) fusion(bf16[32,4096]{1,0:T(8,128)(2,1)S(1)} %bitcast_bitcast_fusion), kind=kLoop, calls=%fused_computation.32 | loop fusion | bytes 524288 | tf_op jit(solution)/shard_map/slice | solution.py:97
  22.1 1.1 %fusion.x_ref = bf16[16,64,64]{2,1,0:T(8,128)(2,1)} fusion(bf16[16,64,64]{2,1,0:T(8,128)(2,1)S(1)} %reshape.42, bf16[64,64]{1,0:T(8,128)(2,1)S(1)} %rev.6, s32[64]{0:T(128)S(1)} %copy-done.3), kind=kOutput, calls=%fused_computation.5 | convolution fusion | flops 16912384 | bytes 270592 | tf_op jit(solution)/shard_map/tk,ckm->ctm/dot_general | solution.py:91
  23.2 6.8 %shard_map.73 = bf16[16,64,64]{2,1,0:T(8,128)(2,1)} custom-call(s32[1]{0:T(128)} %bitcast.base_ref, f32[512]{0:T(512)} %bias_ref.1, bf16[16,4096]{1,0:T(8,128)(2,1)} %get-tuple-element.8.f_ref, bf16[16,64,64]{2,1,0:T(8,128)(2,1)} %fusion.x_ref, s32[64,64]{1,0:T(8,128)} %rev.7.doc_ref, f32[64,4096]{1,0:T(8,128)} %fusion.3.mask_ref), custom_call_target="tpu_custom_call" | custom-call | tf_op jit(solution)/shard_map/pallas_call | solution.py:61
  30.0 1.4 %fusion.1 = bf16[16,64,64]{1,2,0:T(8,128)(2,1)S(1)} fusion(bf16[16,64,64]{2,1,0:T(8,128)(2,1)} %shard_map.73, bf16[64,64]{1,0:T(8,128)(2,1)S(1)} %rev.6, s32[64]{0:T(128)S(1)} %copy-done.3), kind=kOutput, calls=%fused_computation.6 | convolution fusion | flops 16912384 | bytes 270592 | tf_op jit(solution)/shard_map/tk,ctm->ckm/dot_general | solution.py:91
  31.9 0.7 %copy_bitcast_fusion = bf16[32,128,16]{1,2,0:T(8,128)(2,1)} fusion(bf16[16,4096]{1,0:T(8,128)(2,1)S(1)} %reshape.44), kind=kLoop, calls=%fused_computation.19 | loop fusion | bytes 262144 | tf_op jit(solution)/shard_map/all_to_all | solution.py:102
  32.5 4.9 %all-to-all-start.1 = ((bf16[32,128,16]{1,2,0:T(8,128)(2,1)}), bf16[32,128,16]{1,2,0:T(8,128)(2,1)S(1)}, u32[]{:S(2)}, u32[]{:S(2)}) async-start(bf16[32,128,16]{1,2,0:T(8,128)(2,1)} %copy_bitcast_fusion), calls=%async_computation.1 | async-start | bytes 262144 | tf_op jit(solution)/shard_map/all_to_all | solution.py:102
  37.4 1.2 %constant_dynamic-slice_fusion = (bf16[512,2,1,512]{0,3,2,1:T(8,128)(2,1)S(1)}, bf16[512,2,1,512]{0,3,2,1:T(8,128)(2,1)}) fusion(bf16[512,2,2,512]{0,3,2,1:T(8,128)(2,1)S(1)} %bitcast.48, s32[]{:T(128)S(6)} %select_n.26, s32[]{:T(128)S(6)} %select_n.25), kind=kLoop, calls=%fused_computation.29 | loop fusion | bytes 4194312 | tf_op jit(solution)/shard_map/jit(dynamic_index_in_dim)/dynamic_slice | solution.py:108
  38.6 6.4 %all-to-all-done.1 = bf16[32,128,16]{1,2,0:T(8,128)(2,1)S(1)} async-done(((bf16[32,128,16]{1,2,0:T(8,128)(2,1)}), bf16[32,128,16]{1,2,0:T(8,128)(2,1)S(1)}, u32[]{:S(2)}, u32[]{:S(2)}) %all-to-all-start.1) | async-done | bytes 131104 | tf_op jit(solution)/shard_map/all_to_all | solution.py:102
  45.1 0.5 convolution_convert_fusion
  45.5 2.7 %collective-permute-start = (bf16[128,1024]{1,0:T(8,128)(2,1)S(1)}, bf16[128,1024]{1,0:T(8,128)(2,1)S(1)}, u32[]{:S(2)}, u32[]{:S(2)}) collective-permute-start(bf16[128,1024]{1,0:T(8,128)(2,1)S(1)} %convolution_convert_fusion), channel_id=1, source_target_pairs={{0,1},{1,0},{2,3},{3,2},{4,5},{5,4},{6,7},{7,6},{8,9},{9,8},{10,11... | collective-permute-start | bytes 786440 | tf_op jit(solution)/shard_map/ppermute | solution.py:112
  48.3 1.2 %collective-permute-done = bf16[128,1024]{1,0:T(8,128)(2,1)S(1)} collective-permute-done((bf16[128,1024]{1,0:T(8,128)(2,1)S(1)}, bf16[128,1024]{1,0:T(8,128)(2,1)S(1)}, u32[]{:S(2)}, u32[]{:S(2)}) %collective-permute-start) | collective-permute-done | bytes 262176 | tf_op jit(solution)/shard_map/ppermute | solution.py:112
  49.4 0.5 convert_add_fusion
  50.0 2.7 %collective-permute-start.1 = (bf16[128,512]{1,0:T(8,128)(2,1)S(1)}, bf16[128,512]{1,0:T(8,128)(2,1)S(1)}, u32[]{:S(2)}, u32[]{:S(2)}) collective-permute-start(bf16[128,512]{1,0:T(8,128)(2,1)S(1)} %dynamic-slice_convert_fusion), channel_id=1, source_target_pairs={{0,2},{1,3},{2,0},{3,1},{4,6},{5,7},{6,4},{7,5},{8,10},{9,11},{10,... | collective-permute-start | bytes 393224 | tf_op jit(solution)/shard_map/ppermute | solution.py:118
  52.7 3.6 %collective-permute-done.1 = bf16[128,512]{1,0:T(8,128)(2,1)S(1)} collective-permute-done((bf16[128,512]{1,0:T(8,128)(2,1)S(1)}, bf16[128,512]{1,0:T(8,128)(2,1)S(1)}, u32[]{:S(2)}, u32[]{:S(2)}) %collective-permute-start.1) | collective-permute-done | bytes 131104 | tf_op jit(solution)/shard_map/ppermute | solution.py:118
  56.2 0.7 %add_convert_fusion = bf16[128,512]{1,0:T(8,128)(2,1)} fusion(bf16[128,512]{1,0:T(8,128)(2,1)S(1)} %collective-permute-done.1, f32[128,1024]{1,0:T(8,128)S(1)} %convert_add_fusion, s32[]{:T(128)S(6)} %select_n.28), kind=kLoop, calls=%fused_computation.17 | loop fusion | flops 196608 | bytes 524292 | tf_op jit(solution)/shard_map/convert_element_type | solution.py:121
  (25 shorter events, 1.3 us)
Async XLA Ops:
  0.0 12.6 %copy-start.2 = (s32[4096]{0:T(1024)S(1)}, s32[4096]{0:T(1024)}, u32[]{:S(2)}) copy-start(s32[4096]{0:T(1024)} %param.11) | copy-start | bytes 49156
  2.8 18.3 %all-to-all-start = ((bf16[128,32,32]{0,2,1:T(8,128)(2,1)}), bf16[128,32,32]{0,2,1:T(8,128)(2,1)S(1)}, u32[]{:S(2)}, u32[]{:S(2)}) async-start(bf16[128,32,32]{0,2,1:T(8,128)(2,1)} %bitcast.3), calls=%async_computation | async-start | bytes 524288 | tf_op jit(solution)/shard_map/all_to_all | solution.py:96
  15.2 3.0 %copy-start.1 = (bf16[128,512]{1,0:T(8,128)(2,1)S(1)}, bf16[128,512]{1,0:T(8,128)(2,1)}, u32[]{:S(2)}) copy-start(bf16[128,512]{1,0:T(8,128)(2,1)} %param.8) | copy-start | bytes 393220
  15.2 6.9 %copy-start.3 = (s32[64]{0:T(128)S(1)}, s32[64]{0:T(128)}, u32[]{:S(2)}) copy-start(s32[64]{0:T(128)} %param.12) | copy-start | bytes 772
  32.5 12.5 %all-to-all-start.1 = ((bf16[32,128,16]{1,2,0:T(8,128)(2,1)}), bf16[32,128,16]{1,2,0:T(8,128)(2,1)S(1)}, u32[]{:S(2)}, u32[]{:S(2)}) async-start(bf16[32,128,16]{1,2,0:T(8,128)(2,1)} %copy_bitcast_fusion), calls=%async_computation.1 | async-start | bytes 262144 | tf_op jit(solution)/shard_map/all_to_all | solution.py:102
  38.6 10.8 %copy-start = (bf16[512,2,1,512]{0,3,2,1:T(8,128)(2,1)S(1)}, bf16[512,2,1,512]{0,3,2,1:T(8,128)(2,1)}, u32[]{:S(2)}) copy-start(bf16[512,2,1,512]{0,3,2,1:T(8,128)(2,1)} %get-tuple-element.6) | copy-start | bytes 3145732
  45.5 3.9 %collective-permute-start = (bf16[128,1024]{1,0:T(8,128)(2,1)S(1)}, bf16[128,1024]{1,0:T(8,128)(2,1)S(1)}, u32[]{:S(2)}, u32[]{:S(2)}) collective-permute-start(bf16[128,1024]{1,0:T(8,128)(2,1)S(1)} %convolution_convert_fusion), channel_id=1, source_target_pairs={{0,1},{1,0},{2,3},{3,2},{4,5},{5,4},{6,7},{7,6},{8,9},{9,8},{10,11... | collective-permute-start | bytes 786440 | tf_op jit(solution)/shard_map/ppermute | solution.py:112
  50.0 6.3 %collective-permute-start.1 = (bf16[128,512]{1,0:T(8,128)(2,1)S(1)}, bf16[128,512]{1,0:T(8,128)(2,1)S(1)}, u32[]{:S(2)}, u32[]{:S(2)}) collective-permute-start(bf16[128,512]{1,0:T(8,128)(2,1)S(1)} %dynamic-slice_convert_fusion), channel_id=1, source_target_pairs={{0,2},{1,3},{2,0},{3,1},{4,6},{5,7},{6,4},{7,5},{8,10},{9,11},{10,... | collective-permute-start | bytes 393224 | tf_op jit(solution)/shard_map/ppermute | solution.py:118

commit v10 on v9

--- a/solution.py
+++ b/solution.py
@@ -29,11 +29,11 @@
         tt = pltpu.roll(fb, 0, 1, stride=1, stride_axis=0)[:, :seq].astype(jnp.bfloat16)
         x = x_ref[k]
         xf = x.astype(jnp.float32)
-        pair = jnp.concatenate([xf, pltpu.roll(xf, 1, 0)], axis=1)
+        pair = jnp.concatenate([xf, pltpu.roll(xf, 1, 0)], axis=1).astype(jnp.bfloat16)
         src = jnp.concatenate(
             [pair] + [pltpu.roll(pair, 2 * p, 0) for p in range(1, seq // lanes)], axis=1
         )
-        src = (src * mask_ref[...]).astype(jnp.bfloat16)
+        src = src * mask_ref[...]
         y = lax.dot_general(src, tt, contract, preferred_element_type=jnp.float32)
         y = jnp.where(lead_rows, y, 0.0)
         zero = jnp.zeros_like(x)
@@ -57,7 +57,7 @@
     tgt = lax.broadcasted_iota(jnp.int32, (blocks, blocks, span), 0)
     off = span - 1 - lax.broadcasted_iota(jnp.int32, (blocks, blocks, span), 2)
     mask = (tgt >= lag) & (span * (tgt - lag) + off >= starts[:, None, None])
-    mask = mask.astype(jnp.float32).reshape(blocks, seq)
+    mask = mask.astype(jnp.bfloat16).reshape(blocks, seq)
     out = pl.pallas_call(
         conv_kernel,
         grid=(chans // step,),

time: 57.3 us -> 57.8 us (level)
  other arithmetic: 2.33 us -> 3.07 us
    convert_element_type x1, other arithmetic: 0.04 us -> 0.94 us  [body(): (gate.astype(jnp.float32) * pre_local.astype(jnp.float32)).astype(jnp.bfl...]
where the time goes in v10:
time: 57.8 us; the launch traced here: 57.3 us
  starting transfers between devices  20 us (35%)
  waiting for transfers between devices  14.1 us (24%)
  local copies, waits for them, and re-layouts  10.1 us (17%)
  Pallas kernels  6.41 us (11%)
  matrix products  3.43 us (6%)
  other arithmetic  3.07 us (5%)
    all_to_all x1, starting transfers between devices, body(): arrived = lax.all_to_all(packed, 'ctx', 1, 0, tiled=True).T  9.71 us
    pallas_call x1, Pallas kernels, pallas_conv(): pl.pallas_call(conv_kernel, grid=(chans // step,), in_specs=[pl.BlockSpec...  6.41 us
    all_to_all x1, waiting for transfers between devices, body(): pre_local = lax.all_to_all(pre_slots, 'ctx', 0, 1, tiled=True)  6.36 us
    unnamed x12, local copies, waits for them, and re-layouts  5.08 us
    all_to_all x1, starting transfers between devices, body(): pre_local = lax.all_to_all(pre_slots, 'ctx', 0, 1, tiled=True)  4.86 us
    ppermute x1, waiting for transfers between devices, body(): lax.ppermute(send_high.astype(jnp.bfloat16), 'tp', [(i, i ^ 2) for i in r...  3.58 us
    all_to_all x1, waiting for transfers between devices, body(): arrived = lax.all_to_all(packed, 'ctx', 1, 0, tiled=True).T  3.01 us
    ppermute x1, starting transfers between devices, body(): lax.ppermute(p_other.astype(jnp.bfloat16), 'tp', [(i, i ^ 1) for i in ran...  2.77 us
  transfers between devices with their start and end apart: 4, of which 4 were waited for; matrix products, arithmetic and copies ran while one was open for 12% of the time, Pallas kernels for 0%

profile of v10, /device:TPU:1, one launch (start us, length us, event | category | flops | bytes accessed | tf_op | source)
XLA Modules:
  0.0 57.3 jit_solution(10932034199496162984)
XLA Ops:
  0.0 1.0 %copy.37 = bf16[128,512]{0,1:T(8,128)(2,1)S(1)} copy(bf16[128,512]{1,0:T(8,128)(2,1)} %param.7) | data formatting | bytes 262144 | tf_op args[0]
  1.0 1.0 %copy.38 = bf16[128,512]{0,1:T(8,128)(2,1)S(1)} copy(bf16[128,512]{1,0:T(8,128)(2,1)} %param.9) | data formatting | bytes 262144 | tf_op args[2]
  2.1 0.7 %copy.39 = bf16[128,32,2,16]{0,3,2,1:T(8,128)(2,1)} copy(bf16[128,32,2,16]{0,3,1,2:T(8,128)(2,1)S(1)} %pad_maximum_fusion) | data formatting | bytes 524288 | tf_op jit(solution)/shard_map/stack | solution.py:93
  2.8 9.7 %all-to-all-start = ((bf16[128,32,32]{0,2,1:T(8,128)(2,1)}), bf16[128,32,32]{0,2,1:T(8,128)(2,1)S(1)}, u32[]{:S(2)}, u32[]{:S(2)}) async-start(bf16[128,32,32]{0,2,1:T(8,128)(2,1)} %bitcast.3), calls=%async_computation | async-start | bytes 524288 | tf_op jit(solution)/shard_map/all_to_all | solution.py:96
  13.2 1.1 %fusion.3.mask_ref = bf16[64,4096]{1,0:T(8,128)(2,1)} fusion(s32[64]{0:T(128)S(1)} %convert_reduce_fusion, s32[4096]{0:T(1024)S(1)} %iota.60, s32[4096]{0:T(1024)S(1)} %iota.55), kind=kLoop, calls=%fused_computation.11 | loop fusion | flops 1835008 | bytes 557312 | tf_op jit(solution)/shard_map/convert_element_type | solution.py:60
  14.3 0.7 %rev.7.doc_ref = s32[64,64]{1,0:T(8,128)} reverse(s32[64,64]{1,0:T(8,128)S(1)} %reshape.43), dimensions={1} | reverse | bytes 32768 | tf_op jit(solution)/shard_map/rev | solution.py:74
  15.0 2.9 %copy.46 = bf16[512,2048]{0,1:T(8,128)(2,1)S(1)} copy(bf16[512,2048]{1,0:T(8,128)(2,1)} %param.13) | data formatting | bytes 4194304 | tf_op args[6]
  18.1 3.0 %all-to-all-done = bf16[128,32,32]{0,2,1:T(8,128)(2,1)S(1)} async-done(((bf16[128,32,32]{0,2,1:T(8,128)(2,1)}), bf16[128,32,32]{0,2,1:T(8,128)(2,1)S(1)}, u32[]{:S(2)}, u32[]{:S(2)}) %all-to-all-start) | async-done | bytes 262176 | tf_op jit(solution)/shard_map/all_to_all | solution.py:96
  21.1 0.7 %fusion.15 = (bf16[16,4096]{1,0:T(8,128)(2,1)S(1)}, bf16[16,4096]{1,0:T(8,128)(2,1)}) fusion(bf16[32,4096]{1,0:T(8,128)(2,1)S(1)} %bitcast_bitcast_fusion), kind=kLoop, calls=%fused_computation.32 | loop fusion | bytes 524288 | tf_op jit(solution)/shard_map/slice | solution.py:97
  22.1 1.1 %fusion.x_ref = bf16[16,64,64]{2,1,0:T(8,128)(2,1)} fusion(bf16[16,64,64]{2,1,0:T(8,128)(2,1)S(1)} %reshape.42, bf16[64,64]{1,0:T(8,128)(2,1)S(1)} %rev.6, s32[64]{0:T(128)S(1)} %copy-done.3), kind=kOutput, calls=%fused_computation.5 | convolution fusion | flops 16912384 | bytes 270592 | tf_op jit(solution)/shard_map/tk,ckm->ctm/dot_general | solution.py:91
  23.2 6.4 %shard_map.73 = bf16[16,64,64]{2,1,0:T(8,128)(2,1)} custom-call(s32[1]{0:T(128)} %bitcast.base_ref, f32[512]{0:T(512)} %bias_ref.1, bf16[16,4096]{1,0:T(8,128)(2,1)} %get-tuple-element.8.f_ref, bf16[16,64,64]{2,1,0:T(8,128)(2,1)} %fusion.x_ref, s32[64,64]{1,0:T(8,128)} %rev.7.doc_ref, bf16[64,4096]{1,0:T(8,128)(2,1)} %fusion.3.mask_ref), custom_call_target="tpu_custom_call" | custom-call | tf_op jit(solution)/shard_map/pallas_call | solution.py:61
  29.6 1.4 %fusion.1 = bf16[16,64,64]{1,2,0:T(8,128)(2,1)S(1)} fusion(bf16[16,64,64]{2,1,0:T(8,128)(2,1)} %shard_map.73, bf16[64,64]{1,0:T(8,128)(2,1)S(1)} %rev.6, s32[64]{0:T(128)S(1)} %copy-done.3), kind=kOutput, calls=%fused_computation.6 | convolution fusion | flops 16912384 | bytes 270592 | tf_op jit(solution)/shard_map/tk,ctm->ckm/dot_general | solution.py:91
  31.4 0.7 %copy_bitcast_fusion = bf16[32,128,16]{1,2,0:T(8,128)(2,1)} fusion(bf16[16,4096]{1,0:T(8,128)(2,1)S(1)} %reshape.44), kind=kLoop, calls=%fused_computation.19 | loop fusion | bytes 262144 | tf_op jit(solution)/shard_map/all_to_all | solution.py:102
  32.1 4.9 %all-to-all-start.1 = ((bf16[32,128,16]{1,2,0:T(8,128)(2,1)}), bf16[32,128,16]{1,2,0:T(8,128)(2,1)}, u32[]{:S(2)}, u32[]{:S(2)}) async-start(bf16[32,128,16]{1,2,0:T(8,128)(2,1)} %copy_bitcast_fusion), calls=%async_computation.1 | async-start | bytes 262144 | tf_op jit(solution)/shard_map/all_to_all | solution.py:102
  37.0 1.2 %constant_dynamic-slice_fusion = (bf16[512,2,1,512]{0,3,2,1:T(8,128)(2,1)S(1)}, bf16[512,2,1,512]{0,3,2,1:T(8,128)(2,1)}) fusion(bf16[512,2,2,512]{0,3,2,1:T(8,128)(2,1)S(1)} %bitcast.48, s32[]{:T(128)S(6)} %select_n.26, s32[]{:T(128)S(6)} %select_n.25), kind=kLoop, calls=%fused_computation.29 | loop fusion | bytes 4194312 | tf_op jit(solution)/shard_map/jit(dynamic_index_in_dim)/dynamic_slice | solution.py:108
  38.1 6.4 %all-to-all-done.1 = bf16[32,128,16]{1,2,0:T(8,128)(2,1)} async-done(((bf16[32,128,16]{1,2,0:T(8,128)(2,1)}), bf16[32,128,16]{1,2,0:T(8,128)(2,1)}, u32[]{:S(2)}, u32[]{:S(2)}) %all-to-all-start.1) | async-done | bytes 131104 | tf_op jit(solution)/shard_map/all_to_all | solution.py:102
  44.5 0.9 %fusion.4 = bf16[128,512]{0,1:T(8,128)(2,1)S(1)} fusion(bf16[128,512]{0,1:T(8,128)(2,1)S(1)} %copy.36, bf16[32,128,16]{1,2,0:T(8,128)(2,1)} %all-to-all-done.1), kind=kLoop, calls=%fused_computation.16 | loop fusion | flops 262144 | bytes 393216 | tf_op jit(solution)/shard_map/convert_element_type | solution.py:103
  45.5 0.5 convolution_convert_fusion
  45.9 2.8 %collective-permute-start = (bf16[128,1024]{1,0:T(8,128)(2,1)S(1)}, bf16[128,1024]{1,0:T(8,128)(2,1)S(1)}, u32[]{:S(2)}, u32[]{:S(2)}) collective-permute-start(bf16[128,1024]{1,0:T(8,128)(2,1)S(1)} %convolution_convert_fusion), channel_id=1, source_target_pairs={{0,1},{1,0},{2,3},{3,2},{4,5},{5,4},{6,7},{7,6},{8,9},{9,8},{10,11... | collective-permute-start | bytes 786440 | tf_op jit(solution)/shard_map/ppermute | solution.py:112
  48.7 1.2 %collective-permute-done = bf16[128,1024]{1,0:T(8,128)(2,1)S(1)} collective-permute-done((bf16[128,1024]{1,0:T(8,128)(2,1)S(1)}, bf16[128,1024]{1,0:T(8,128)(2,1)S(1)}, u32[]{:S(2)}, u32[]{:S(2)}) %collective-permute-start) | collective-permute-done | bytes 262176 | tf_op jit(solution)/shard_map/ppermute | solution.py:112
  49.9 0.5 convert_add_fusion
  50.4 2.7 %collective-permute-start.1 = (bf16[128,512]{1,0:T(8,128)(2,1)S(1)}, bf16[128,512]{1,0:T(8,128)(2,1)S(1)}, u32[]{:S(2)}, u32[]{:S(2)}) collective-permute-start(bf16[128,512]{1,0:T(8,128)(2,1)S(1)} %dynamic-slice_convert_fusion), channel_id=1, source_target_pairs={{0,2},{1,3},{2,0},{3,1},{4,6},{5,7},{6,4},{7,5},{8,10},{9,11},{10,... | collective-permute-start | bytes 393224 | tf_op jit(solution)/shard_map/ppermute | solution.py:118
  53.1 3.6 %collective-permute-done.1 = bf16[128,512]{1,0:T(8,128)(2,1)S(1)} collective-permute-done((bf16[128,512]{1,0:T(8,128)(2,1)S(1)}, bf16[128,512]{1,0:T(8,128)(2,1)S(1)}, u32[]{:S(2)}, u32[]{:S(2)}) %collective-permute-start.1) | collective-permute-done | bytes 131104 | tf_op jit(solution)/shard_map/ppermute | solution.py:118
  56.7 0.7 %add_convert_fusion = bf16[128,512]{1,0:T(8,128)(2,1)} fusion(bf16[128,512]{1,0:T(8,128)(2,1)S(1)} %collective-permute-done.1, f32[128,1024]{1,0:T(8,128)S(1)} %convert_add_fusion, s32[]{:T(128)S(6)} %select_n.28), kind=kLoop, calls=%fused_computation.17 | loop fusion | flops 196608 | bytes 524292 | tf_op jit(solution)/shard_map/convert_element_type | solution.py:121
  (25 shorter events, 1.5 us)
Async XLA Ops:
  0.0 12.6 %copy-start.2 = (s32[4096]{0:T(1024)S(1)}, s32[4096]{0:T(1024)}, u32[]{:S(2)}) copy-start(s32[4096]{0:T(1024)} %param.11) | copy-start | bytes 49156
  2.8 18.3 %all-to-all-start = ((bf16[128,32,32]{0,2,1:T(8,128)(2,1)}), bf16[128,32,32]{0,2,1:T(8,128)(2,1)S(1)}, u32[]{:S(2)}, u32[]{:S(2)}) async-start(bf16[128,32,32]{0,2,1:T(8,128)(2,1)} %bitcast.3), calls=%async_computation | async-start | bytes 524288 | tf_op jit(solution)/shard_map/all_to_all | solution.py:96
  15.0 3.0 %copy-start.1 = (bf16[128,512]{1,0:T(8,128)(2,1)S(1)}, bf16[128,512]{1,0:T(8,128)(2,1)}, u32[]{:S(2)}) copy-start(bf16[128,512]{1,0:T(8,128)(2,1)} %param.8) | copy-start | bytes 393220
  15.0 7.0 %copy-start.3 = (s32[64]{0:T(128)S(1)}, s32[64]{0:T(128)}, u32[]{:S(2)}) copy-start(s32[64]{0:T(128)} %param.12) | copy-start | bytes 772
  32.1 12.4 %all-to-all-start.1 = ((bf16[32,128,16]{1,2,0:T(8,128)(2,1)}), bf16[32,128,16]{1,2,0:T(8,128)(2,1)}, u32[]{:S(2)}, u32[]{:S(2)}) async-start(bf16[32,128,16]{1,2,0:T(8,128)(2,1)} %copy_bitcast_fusion), calls=%async_computation.1 | async-start | bytes 262144 | tf_op jit(solution)/shard_map/all_to_all | solution.py:102
  38.1 11.7 %copy-start = (bf16[512,2,1,512]{0,3,2,1:T(8,128)(2,1)S(1)}, bf16[512,2,1,512]{0,3,2,1:T(8,128)(2,1)}, u32[]{:S(2)}) copy-start(bf16[512,2,1,512]{0,3,2,1:T(8,128)(2,1)} %get-tuple-element.6) | copy-start | bytes 3145732
  45.9 3.9 %collective-permute-start = (bf16[128,1024]{1,0:T(8,128)(2,1)S(1)}, bf16[128,1024]{1,0:T(8,128)(2,1)S(1)}, u32[]{:S(2)}, u32[]{:S(2)}) collective-permute-start(bf16[128,1024]{1,0:T(8,128)(2,1)S(1)} %convolution_convert_fusion), channel_id=1, source_target_pairs={{0,1},{1,0},{2,3},{3,2},{4,5},{5,4},{6,7},{7,6},{8,9},{9,8},{10,11... | collective-permute-start | bytes 786440 | tf_op jit(solution)/shard_map/ppermute | solution.py:112
  50.4 6.3 %collective-permute-start.1 = (bf16[128,512]{1,0:T(8,128)(2,1)S(1)}, bf16[128,512]{1,0:T(8,128)(2,1)S(1)}, u32[]{:S(2)}, u32[]{:S(2)}) collective-permute-start(bf16[128,512]{1,0:T(8,128)(2,1)S(1)} %dynamic-slice_convert_fusion), channel_id=1, source_target_pairs={{0,2},{1,3},{2,0},{3,1},{4,6},{5,7},{6,4},{7,5},{8,10},{9,11},{10,... | collective-permute-start | bytes 393224 | tf_op jit(solution)/shard_map/ppermute | solution.py:118

commit v11 on v9

--- a/solution.py
+++ b/solution.py
@@ -9,7 +9,7 @@
 DOC_COUNT = 4
 
 
-CHANNELS_PER_STEP = 8
+CHANNELS_PER_STEP = 16
 
 
 def conv_kernel(base_ref, bias_ref, f_ref, x_ref, doc_ref, mask_ref, y_ref):

time: 57.3 us -> 57.1 us (level)
  no operation moved by 1% of the time
where the time goes in v11:
time: 57.1 us; the launch traced here: 56.6 us
  starting transfers between devices  20 us (35%)
  waiting for transfers between devices  14 us (25%)
  local copies, waits for them, and re-layouts  10.1 us (18%)
  Pallas kernels  6.58 us (12%)
  matrix products  3.43 us (6%)
  other arithmetic  2.33 us (4%)
    all_to_all x1, starting transfers between devices, body(): arrived = lax.all_to_all(packed, 'ctx', 1, 0, tiled=True).T  9.71 us
    pallas_call x1, Pallas kernels, pallas_conv(): pl.pallas_call(conv_kernel, grid=(chans // step,), in_specs=[pl.BlockSpec...  6.58 us
    all_to_all x1, waiting for transfers between devices, body(): pre_local = lax.all_to_all(pre_slots, 'ctx', 0, 1, tiled=True)  6.39 us
    unnamed x12, local copies, waits for them, and re-layouts  5.08 us
    all_to_all x1, starting transfers between devices, body(): pre_local = lax.all_to_all(pre_slots, 'ctx', 0, 1, tiled=True)  4.89 us
    ppermute x1, waiting for transfers between devices, body(): lax.ppermute(send_high.astype(jnp.bfloat16), 'tp', [(i, i ^ 2) for i in r...  3.56 us
    all_to_all x1, waiting for transfers between devices, body(): arrived = lax.all_to_all(packed, 'ctx', 1, 0, tiled=True).T  2.85 us
    ppermute x1, starting transfers between devices, body(): lax.ppermute(p_other.astype(jnp.bfloat16), 'tp', [(i, i ^ 1) for i in ran...  2.74 us
  transfers between devices with their start and end apart: 4, of which 4 were waited for; matrix products, arithmetic and copies ran while one was open for 12% of the time, Pallas kernels for 0%

profile of v11, /device:TPU:1, one launch (start us, length us, event | category | flops | bytes accessed | tf_op | source)
XLA Modules:
  0.0 56.6 jit_solution(14409746545191980975)
XLA Ops:
  0.0 1.0 %copy.37 = bf16[128,512]{0,1:T(8,128)(2,1)S(1)} copy(bf16[128,512]{1,0:T(8,128)(2,1)} %param.7) | data formatting | bytes 262144 | tf_op args[0]
  1.0 1.0 %copy.38 = bf16[128,512]{0,1:T(8,128)(2,1)S(1)} copy(bf16[128,512]{1,0:T(8,128)(2,1)} %param.9) | data formatting | bytes 262144 | tf_op args[2]
  2.1 0.7 %copy.39 = bf16[128,32,2,16]{0,3,2,1:T(8,128)(2,1)} copy(bf16[128,32,2,16]{0,3,1,2:T(8,128)(2,1)S(1)} %pad_maximum_fusion) | data formatting | bytes 524288 | tf_op jit(solution)/shard_map/stack | solution.py:93
  2.8 9.7 %all-to-all-start = ((bf16[128,32,32]{0,2,1:T(8,128)(2,1)}), bf16[128,32,32]{0,2,1:T(8,128)(2,1)S(1)}, u32[]{:S(2)}, u32[]{:S(2)}) async-start(bf16[128,32,32]{0,2,1:T(8,128)(2,1)} %bitcast.3), calls=%async_computation | async-start | bytes 524288 | tf_op jit(solution)/shard_map/all_to_all | solution.py:96
  12.8 0.3 convert_reduce_fusion
  13.2 1.3 %fusion.3.mask_ref = f32[64,4096]{1,0:T(8,128)} fusion(s32[64]{0:T(128)S(1)} %convert_reduce_fusion, s32[4096]{0:T(1024)S(1)} %iota.60, s32[4096]{0:T(1024)S(1)} %iota.55), kind=kLoop, calls=%fused_computation.11 | loop fusion | flops 1835008 | bytes 1081600 | tf_op jit(solution)/shard_map/convert_element_type | solution.py:60
  14.5 0.7 %rev.7.doc_ref = s32[64,64]{1,0:T(8,128)} reverse(s32[64,64]{1,0:T(8,128)S(1)} %reshape.43), dimensions={1} | reverse | bytes 32768 | tf_op jit(solution)/shard_map/rev | solution.py:74
  15.2 2.9 %copy.46 = bf16[512,2048]{0,1:T(8,128)(2,1)S(1)} copy(bf16[512,2048]{1,0:T(8,128)(2,1)} %param.13) | data formatting | bytes 4194304 | tf_op args[6]
  18.3 2.8 %all-to-all-done = bf16[128,32,32]{0,2,1:T(8,128)(2,1)S(1)} async-done(((bf16[128,32,32]{0,2,1:T(8,128)(2,1)}), bf16[128,32,32]{0,2,1:T(8,128)(2,1)S(1)}, u32[]{:S(2)}, u32[]{:S(2)}) %all-to-all-start) | async-done | bytes 262176 | tf_op jit(solution)/shard_map/all_to_all | solution.py:96
  21.1 0.7 %fusion.15 = (bf16[16,4096]{1,0:T(8,128)(2,1)S(1)}, bf16[16,4096]{1,0:T(8,128)(2,1)}) fusion(bf16[32,4096]{1,0:T(8,128)(2,1)S(1)} %bitcast_bitcast_fusion), kind=kLoop, calls=%fused_computation.32 | loop fusion | bytes 524288 | tf_op jit(solution)/shard_map/slice | solution.py:97
  22.1 1.1 %fusion.x_ref = bf16[16,64,64]{2,1,0:T(8,128)(2,1)} fusion(bf16[16,64,64]{2,1,0:T(8,128)(2,1)S(1)} %reshape.42, bf16[64,64]{1,0:T(8,128)(2,1)S(1)} %rev.6, s32[64]{0:T(128)S(1)} %copy-done.3), kind=kOutput, calls=%fused_computation.5 | convolution fusion | flops 16912384 | bytes 270592 | tf_op jit(solution)/shard_map/tk,ckm->ctm/dot_general | solution.py:91
  23.2 6.6 %shard_map.73 = bf16[16,64,64]{2,1,0:T(8,128)(2,1)} custom-call(s32[1]{0:T(128)} %bitcast.base_ref, f32[512]{0:T(512)} %bias_ref.1, bf16[16,4096]{1,0:T(8,128)(2,1)} %get-tuple-element.8.f_ref, bf16[16,64,64]{2,1,0:T(8,128)(2,1)} %fusion.x_ref, s32[64,64]{1,0:T(8,128)} %rev.7.doc_ref, f32[64,4096]{1,0:T(8,128)} %fusion.3.mask_ref), custom_call_target="tpu_custom_call" | custom-call | tf_op jit(solution)/shard_map/pallas_call | solution.py:61
  29.8 1.4 %fusion.1 = bf16[16,64,64]{1,2,0:T(8,128)(2,1)S(1)} fusion(bf16[16,64,64]{2,1,0:T(8,128)(2,1)} %shard_map.73, bf16[64,64]{1,0:T(8,128)(2,1)S(1)} %rev.6, s32[64]{0:T(128)S(1)} %copy-done.3), kind=kOutput, calls=%fused_computation.6 | convolution fusion | flops 16912384 | bytes 270592 | tf_op jit(solution)/shard_map/tk,ctm->ckm/dot_general | solution.py:91
  31.6 0.7 %copy_bitcast_fusion = bf16[32,128,16]{1,2,0:T(8,128)(2,1)} fusion(bf16[16,4096]{1,0:T(8,128)(2,1)S(1)} %reshape.44), kind=kLoop, calls=%fused_computation.19 | loop fusion | bytes 262144 | tf_op jit(solution)/shard_map/all_to_all | solution.py:102
  32.3 4.9 %all-to-all-start.1 = ((bf16[32,128,16]{1,2,0:T(8,128)(2,1)}), bf16[32,128,16]{1,2,0:T(8,128)(2,1)S(1)}, u32[]{:S(2)}, u32[]{:S(2)}) async-start(bf16[32,128,16]{1,2,0:T(8,128)(2,1)} %copy_bitcast_fusion), calls=%async_computation.1 | async-start | bytes 262144 | tf_op jit(solution)/shard_map/all_to_all | solution.py:102
  37.2 1.2 %constant_dynamic-slice_fusion = (bf16[512,2,1,512]{0,3,2,1:T(8,128)(2,1)S(1)}, bf16[512,2,1,512]{0,3,2,1:T(8,128)(2,1)}) fusion(bf16[512,2,2,512]{0,3,2,1:T(8,128)(2,1)S(1)} %bitcast.48, s32[]{:T(128)S(6)} %select_n.26, s32[]{:T(128)S(6)} %select_n.25), kind=kLoop, calls=%fused_computation.29 | loop fusion | bytes 4194312 | tf_op jit(solution)/shard_map/jit(dynamic_index_in_dim)/dynamic_slice | solution.py:108
  38.4 6.4 %all-to-all-done.1 = bf16[32,128,16]{1,2,0:T(8,128)(2,1)S(1)} async-done(((bf16[32,128,16]{1,2,0:T(8,128)(2,1)}), bf16[32,128,16]{1,2,0:T(8,128)(2,1)S(1)}, u32[]{:S(2)}, u32[]{:S(2)}) %all-to-all-start.1) | async-done | bytes 131104 | tf_op jit(solution)/shard_map/all_to_all | solution.py:102
  44.8 0.5 convolution_convert_fusion
  45.3 2.7 %collective-permute-start = (bf16[128,1024]{1,0:T(8,128)(2,1)S(1)}, bf16[128,1024]{1,0:T(8,128)(2,1)S(1)}, u32[]{:S(2)}, u32[]{:S(2)}) collective-permute-start(bf16[128,1024]{1,0:T(8,128)(2,1)S(1)} %convolution_convert_fusion), channel_id=1, source_target_pairs={{0,1},{1,0},{2,3},{3,2},{4,5},{5,4},{6,7},{7,6},{8,9},{9,8},{10,11... | collective-permute-start | bytes 786440 | tf_op jit(solution)/shard_map/ppermute | solution.py:112
  48.0 1.2 %collective-permute-done = bf16[128,1024]{1,0:T(8,128)(2,1)S(1)} collective-permute-done((bf16[128,1024]{1,0:T(8,128)(2,1)S(1)}, bf16[128,1024]{1,0:T(8,128)(2,1)S(1)}, u32[]{:S(2)}, u32[]{:S(2)}) %collective-permute-start) | collective-permute-done | bytes 262176 | tf_op jit(solution)/shard_map/ppermute | solution.py:112
  49.2 0.5 convert_add_fusion
  49.7 2.7 %collective-permute-start.1 = (bf16[128,512]{1,0:T(8,128)(2,1)S(1)}, bf16[128,512]{1,0:T(8,128)(2,1)S(1)}, u32[]{:S(2)}, u32[]{:S(2)}) collective-permute-start(bf16[128,512]{1,0:T(8,128)(2,1)S(1)} %dynamic-slice_convert_fusion), channel_id=1, source_target_pairs={{0,2},{1,3},{2,0},{3,1},{4,6},{5,7},{6,4},{7,5},{8,10},{9,11},{10,... | collective-permute-start | bytes 393224 | tf_op jit(solution)/shard_map/ppermute | solution.py:118
  52.4 3.6 %collective-permute-done.1 = bf16[128,512]{1,0:T(8,128)(2,1)S(1)} collective-permute-done((bf16[128,512]{1,0:T(8,128)(2,1)S(1)}, bf16[128,512]{1,0:T(8,128)(2,1)S(1)}, u32[]{:S(2)}, u32[]{:S(2)}) %collective-permute-start.1) | collective-permute-done | bytes 131104 | tf_op jit(solution)/shard_map/ppermute | solution.py:118
  56.0 0.7 %add_convert_fusion = bf16[128,512]{1,0:T(8,128)(2,1)} fusion(bf16[128,512]{1,0:T(8,128)(2,1)S(1)} %collective-permute-done.1, f32[128,1024]{1,0:T(8,128)S(1)} %convert_add_fusion, s32[]{:T(128)S(6)} %select_n.28), kind=kLoop, calls=%fused_computation.17 | loop fusion | flops 196608 | bytes 524292 | tf_op jit(solution)/shard_map/convert_element_type | solution.py:121
  (25 shorter events, 1.3 us)
Async XLA Ops:
  0.0 12.6 %copy-start.2 = (s32[4096]{0:T(1024)S(1)}, s32[4096]{0:T(1024)}, u32[]{:S(2)}) copy-start(s32[4096]{0:T(1024)} %param.11) | copy-start | bytes 49156
  2.8 18.3 %all-to-all-start = ((bf16[128,32,32]{0,2,1:T(8,128)(2,1)}), bf16[128,32,32]{0,2,1:T(8,128)(2,1)S(1)}, u32[]{:S(2)}, u32[]{:S(2)}) async-start(bf16[128,32,32]{0,2,1:T(8,128)(2,1)} %bitcast.3), calls=%async_computation | async-start | bytes 524288 | tf_op jit(solution)/shard_map/all_to_all | solution.py:96
  15.2 3.0 %copy-start.1 = (bf16[128,512]{1,0:T(8,128)(2,1)S(1)}, bf16[128,512]{1,0:T(8,128)(2,1)}, u32[]{:S(2)}) copy-start(bf16[128,512]{1,0:T(8,128)(2,1)} %param.8) | copy-start | bytes 393220
  15.2 6.9 %copy-start.3 = (s32[64]{0:T(128)S(1)}, s32[64]{0:T(128)}, u32[]{:S(2)}) copy-start(s32[64]{0:T(128)} %param.12) | copy-start | bytes 772
  32.3 12.5 %all-to-all-start.1 = ((bf16[32,128,16]{1,2,0:T(8,128)(2,1)}), bf16[32,128,16]{1,2,0:T(8,128)(2,1)S(1)}, u32[]{:S(2)}, u32[]{:S(2)}) async-start(bf16[32,128,16]{1,2,0:T(8,128)(2,1)} %copy_bitcast_fusion), calls=%async_computation.1 | async-start | bytes 262144 | tf_op jit(solution)/shard_map/all_to_all | solution.py:102
  38.4 10.8 %copy-start = (bf16[512,2,1,512]{0,3,2,1:T(8,128)(2,1)S(1)}, bf16[512,2,1,512]{0,3,2,1:T(8,128)(2,1)}, u32[]{:S(2)}) copy-start(bf16[512,2,1,512]{0,3,2,1:T(8,128)(2,1)} %get-tuple-element.6) | copy-start | bytes 3145732
  45.3 3.9 %collective-permute-start = (bf16[128,1024]{1,0:T(8,128)(2,1)S(1)}, bf16[128,1024]{1,0:T(8,128)(2,1)S(1)}, u32[]{:S(2)}, u32[]{:S(2)}) collective-permute-start(bf16[128,1024]{1,0:T(8,128)(2,1)S(1)} %convolution_convert_fusion), channel_id=1, source_target_pairs={{0,1},{1,0},{2,3},{3,2},{4,5},{5,4},{6,7},{7,6},{8,9},{9,8},{10,11... | collective-permute-start | bytes 786440 | tf_op jit(solution)/shard_map/ppermute | solution.py:112
  49.7 6.3 %collective-permute-start.1 = (bf16[128,512]{1,0:T(8,128)(2,1)S(1)}, bf16[128,512]{1,0:T(8,128)(2,1)S(1)}, u32[]{:S(2)}, u32[]{:S(2)}) collective-permute-start(bf16[128,512]{1,0:T(8,128)(2,1)S(1)} %dynamic-slice_convert_fusion), channel_id=1, source_target_pairs={{0,2},{1,3},{2,0},{3,1},{4,6},{5,7},{6,4},{7,5},{8,10},{9,11},{10,... | collective-permute-start | bytes 393224 | tf_op jit(solution)/shard_map/ppermute | solution.py:118

commit v12 on v10

--- a/solution.py
+++ b/solution.py
@@ -29,11 +29,11 @@
         tt = pltpu.roll(fb, 0, 1, stride=1, stride_axis=0)[:, :seq].astype(jnp.bfloat16)
         x = x_ref[k]
         xf = x.astype(jnp.float32)
-        pair = jnp.concatenate([xf, pltpu.roll(xf, 1, 0)], axis=1).astype(jnp.bfloat16)
+        pair = jnp.concatenate([xf, pltpu.roll(xf, 1, 0)], axis=1)
         src = jnp.concatenate(
             [pair] + [pltpu.roll(pair, 2 * p, 0) for p in range(1, seq // lanes)], axis=1
         )
-        src = src * mask_ref[...]
+        src = src.astype(jnp.bfloat16) * mask_ref[...]
         y = lax.dot_general(src, tt, contract, preferred_element_type=jnp.float32)
         y = jnp.where(lead_rows, y, 0.0)
         zero = jnp.zeros_like(x)

time: 57.8 us -> 57.8 us (level)
  no operation moved by 1% of the time
where the time goes in v12:
time: 57.8 us; the launch traced here: 57.3 us
  starting transfers between devices  20 us (35%)
  waiting for transfers between devices  14.1 us (24%)
  local copies, waits for them, and re-layouts  10.1 us (17%)
  Pallas kernels  6.39 us (11%)
  matrix products  3.43 us (6%)
  other arithmetic  3.07 us (5%)
    all_to_all x1, starting transfers between devices, body(): arrived = lax.all_to_all(packed, 'ctx', 1, 0, tiled=True).T  9.71 us
    pallas_call x1, Pallas kernels, pallas_conv(): pl.pallas_call(conv_kernel, grid=(chans // step,), in_specs=[pl.BlockSpec...  6.39 us
    all_to_all x1, waiting for transfers between devices, body(): pre_local = lax.all_to_all(pre_slots, 'ctx', 0, 1, tiled=True)  6.36 us
    unnamed x12, local copies, waits for them, and re-layouts  5.08 us
    all_to_all x1, starting transfers between devices, body(): pre_local = lax.all_to_all(pre_slots, 'ctx', 0, 1, tiled=True)  4.86 us
    ppermute x1, waiting for transfers between devices, body(): lax.ppermute(send_high.astype(jnp.bfloat16), 'tp', [(i, i ^ 2) for i in r...  3.57 us
    all_to_all x1, waiting for transfers between devices, body(): arrived = lax.all_to_all(packed, 'ctx', 1, 0, tiled=True).T  3.01 us
    ppermute x1, starting transfers between devices, body(): lax.ppermute(p_other.astype(jnp.bfloat16), 'tp', [(i, i ^ 1) for i in ran...  2.77 us
  transfers between devices with their start and end apart: 4, of which 4 were waited for; matrix products, arithmetic and copies ran while one was open for 12% of the time, Pallas kernels for 0%

profile of v12, /device:TPU:1, one launch (start us, length us, event | category | flops | bytes accessed | tf_op | source)
XLA Modules:
  0.0 57.3 jit_solution(17065637625509273090)
XLA Ops:
  0.0 1.0 %copy.37 = bf16[128,512]{0,1:T(8,128)(2,1)S(1)} copy(bf16[128,512]{1,0:T(8,128)(2,1)} %param.7) | data formatting | bytes 262144 | tf_op args[0]
  1.0 1.0 %copy.38 = bf16[128,512]{0,1:T(8,128)(2,1)S(1)} copy(bf16[128,512]{1,0:T(8,128)(2,1)} %param.9) | data formatting | bytes 262144 | tf_op args[2]
  2.1 0.7 %copy.39 = bf16[128,32,2,16]{0,3,2,1:T(8,128)(2,1)} copy(bf16[128,32,2,16]{0,3,1,2:T(8,128)(2,1)S(1)} %pad_maximum_fusion) | data formatting | bytes 524288 | tf_op jit(solution)/shard_map/stack | solution.py:93
  2.8 9.7 %all-to-all-start = ((bf16[128,32,32]{0,2,1:T(8,128)(2,1)}), bf16[128,32,32]{0,2,1:T(8,128)(2,1)S(1)}, u32[]{:S(2)}, u32[]{:S(2)}) async-start(bf16[128,32,32]{0,2,1:T(8,128)(2,1)} %bitcast.3), calls=%async_computation | async-start | bytes 524288 | tf_op jit(solution)/shard_map/all_to_all | solution.py:96
  13.2 1.1 %fusion.3.mask_ref = bf16[64,4096]{1,0:T(8,128)(2,1)} fusion(s32[64]{0:T(128)S(1)} %convert_reduce_fusion, s32[4096]{0:T(1024)S(1)} %iota.60, s32[4096]{0:T(1024)S(1)} %iota.55), kind=kLoop, calls=%fused_computation.11 | loop fusion | flops 1835008 | bytes 557312 | tf_op jit(solution)/shard_map/convert_element_type | solution.py:60
  14.3 0.7 %rev.7.doc_ref = s32[64,64]{1,0:T(8,128)} reverse(s32[64,64]{1,0:T(8,128)S(1)} %reshape.43), dimensions={1} | reverse | bytes 32768 | tf_op jit(solution)/shard_map/rev | solution.py:74
  15.0 2.9 %copy.46 = bf16[512,2048]{0,1:T(8,128)(2,1)S(1)} copy(bf16[512,2048]{1,0:T(8,128)(2,1)} %param.13) | data formatting | bytes 4194304 | tf_op args[6]
  18.1 3.0 %all-to-all-done = bf16[128,32,32]{0,2,1:T(8,128)(2,1)S(1)} async-done(((bf16[128,32,32]{0,2,1:T(8,128)(2,1)}), bf16[128,32,32]{0,2,1:T(8,128)(2,1)S(1)}, u32[]{:S(2)}, u32[]{:S(2)}) %all-to-all-start) | async-done | bytes 262176 | tf_op jit(solution)/shard_map/all_to_all | solution.py:96
  21.1 0.7 %fusion.15 = (bf16[16,4096]{1,0:T(8,128)(2,1)S(1)}, bf16[16,4096]{1,0:T(8,128)(2,1)}) fusion(bf16[32,4096]{1,0:T(8,128)(2,1)S(1)} %bitcast_bitcast_fusion), kind=kLoop, calls=%fused_computation.32 | loop fusion | bytes 524288 | tf_op jit(solution)/shard_map/slice | solution.py:97
  22.1 1.1 %fusion.x_ref = bf16[16,64,64]{2,1,0:T(8,128)(2,1)} fusion(bf16[16,64,64]{2,1,0:T(8,128)(2,1)S(1)} %reshape.42, bf16[64,64]{1,0:T(8,128)(2,1)S(1)} %rev.6, s32[64]{0:T(128)S(1)} %copy-done.3), kind=kOutput, calls=%fused_computation.5 | convolution fusion | flops 16912384 | bytes 270592 | tf_op jit(solution)/shard_map/tk,ckm->ctm/dot_general | solution.py:91
  23.2 6.4 %shard_map.73 = bf16[16,64,64]{2,1,0:T(8,128)(2,1)} custom-call(s32[1]{0:T(128)} %bitcast.base_ref, f32[512]{0:T(512)} %bias_ref.1, bf16[16,4096]{1,0:T(8,128)(2,1)} %get-tuple-element.8.f_ref, bf16[16,64,64]{2,1,0:T(8,128)(2,1)} %fusion.x_ref, s32[64,64]{1,0:T(8,128)} %rev.7.doc_ref, bf16[64,4096]{1,0:T(8,128)(2,1)} %fusion.3.mask_ref), custom_call_target="tpu_custom_call" | custom-call | tf_op jit(solution)/shard_map/pallas_call | solution.py:61
  29.6 1.4 %fusion.1 = bf16[16,64,64]{1,2,0:T(8,128)(2,1)S(1)} fusion(bf16[16,64,64]{2,1,0:T(8,128)(2,1)} %shard_map.73, bf16[64,64]{1,0:T(8,128)(2,1)S(1)} %rev.6, s32[64]{0:T(128)S(1)} %copy-done.3), kind=kOutput, calls=%fused_computation.6 | convolution fusion | flops 16912384 | bytes 270592 | tf_op jit(solution)/shard_map/tk,ctm->ckm/dot_general | solution.py:91
  31.4 0.7 %copy_bitcast_fusion = bf16[32,128,16]{1,2,0:T(8,128)(2,1)} fusion(bf16[16,4096]{1,0:T(8,128)(2,1)S(1)} %reshape.44), kind=kLoop, calls=%fused_computation.19 | loop fusion | bytes 262144 | tf_op jit(solution)/shard_map/all_to_all | solution.py:102
  32.1 4.9 %all-to-all-start.1 = ((bf16[32,128,16]{1,2,0:T(8,128)(2,1)}), bf16[32,128,16]{1,2,0:T(8,128)(2,1)}, u32[]{:S(2)}, u32[]{:S(2)}) async-start(bf16[32,128,16]{1,2,0:T(8,128)(2,1)} %copy_bitcast_fusion), calls=%async_computation.1 | async-start | bytes 262144 | tf_op jit(solution)/shard_map/all_to_all | solution.py:102
  36.9 1.2 %constant_dynamic-slice_fusion = (bf16[512,2,1,512]{0,3,2,1:T(8,128)(2,1)S(1)}, bf16[512,2,1,512]{0,3,2,1:T(8,128)(2,1)}) fusion(bf16[512,2,2,512]{0,3,2,1:T(8,128)(2,1)S(1)} %bitcast.48, s32[]{:T(128)S(6)} %select_n.26, s32[]{:T(128)S(6)} %select_n.25), kind=kLoop, calls=%fused_computation.29 | loop fusion | bytes 4194312 | tf_op jit(solution)/shard_map/jit(dynamic_index_in_dim)/dynamic_slice | solution.py:108
  38.1 6.4 %all-to-all-done.1 = bf16[32,128,16]{1,2,0:T(8,128)(2,1)} async-done(((bf16[32,128,16]{1,2,0:T(8,128)(2,1)}), bf16[32,128,16]{1,2,0:T(8,128)(2,1)}, u32[]{:S(2)}, u32[]{:S(2)}) %all-to-all-start.1) | async-done | bytes 131104 | tf_op jit(solution)/shard_map/all_to_all | solution.py:102
  44.5 0.9 %fusion.4 = bf16[128,512]{0,1:T(8,128)(2,1)S(1)} fusion(bf16[128,512]{0,1:T(8,128)(2,1)S(1)} %copy.36, bf16[32,128,16]{1,2,0:T(8,128)(2,1)} %all-to-all-done.1), kind=kLoop, calls=%fused_computation.16 | loop fusion | flops 262144 | bytes 393216 | tf_op jit(solution)/shard_map/convert_element_type | solution.py:103
  45.4 0.5 convolution_convert_fusion
  45.9 2.8 %collective-permute-start = (bf16[128,1024]{1,0:T(8,128)(2,1)S(1)}, bf16[128,1024]{1,0:T(8,128)(2,1)S(1)}, u32[]{:S(2)}, u32[]{:S(2)}) collective-permute-start(bf16[128,1024]{1,0:T(8,128)(2,1)S(1)} %convolution_convert_fusion), channel_id=1, source_target_pairs={{0,1},{1,0},{2,3},{3,2},{4,5},{5,4},{6,7},{7,6},{8,9},{9,8},{10,11... | collective-permute-start | bytes 786440 | tf_op jit(solution)/shard_map/ppermute | solution.py:112
  48.7 1.2 %collective-permute-done = bf16[128,1024]{1,0:T(8,128)(2,1)S(1)} collective-permute-done((bf16[128,1024]{1,0:T(8,128)(2,1)S(1)}, bf16[128,1024]{1,0:T(8,128)(2,1)S(1)}, u32[]{:S(2)}, u32[]{:S(2)}) %collective-permute-start) | collective-permute-done | bytes 262176 | tf_op jit(solution)/shard_map/ppermute | solution.py:112
  49.9 0.5 convert_add_fusion
  50.4 2.7 %collective-permute-start.1 = (bf16[128,512]{1,0:T(8,128)(2,1)S(1)}, bf16[128,512]{1,0:T(8,128)(2,1)S(1)}, u32[]{:S(2)}, u32[]{:S(2)}) collective-permute-start(bf16[128,512]{1,0:T(8,128)(2,1)S(1)} %dynamic-slice_convert_fusion), channel_id=1, source_target_pairs={{0,2},{1,3},{2,0},{3,1},{4,6},{5,7},{6,4},{7,5},{8,10},{9,11},{10,... | collective-permute-start | bytes 393224 | tf_op jit(solution)/shard_map/ppermute | solution.py:118
  53.1 3.6 %collective-permute-done.1 = bf16[128,512]{1,0:T(8,128)(2,1)S(1)} collective-permute-done((bf16[128,512]{1,0:T(8,128)(2,1)S(1)}, bf16[128,512]{1,0:T(8,128)(2,1)S(1)}, u32[]{:S(2)}, u32[]{:S(2)}) %collective-permute-start.1) | collective-permute-done | bytes 131104 | tf_op jit(solution)/shard_map/ppermute | solution.py:118
  56.6 0.7 %add_convert_fusion = bf16[128,512]{1,0:T(8,128)(2,1)} fusion(bf16[128,512]{1,0:T(8,128)(2,1)S(1)} %collective-permute-done.1, f32[128,1024]{1,0:T(8,128)S(1)} %convert_add_fusion, s32[]{:T(128)S(6)} %select_n.28), kind=kLoop, calls=%fused_computation.17 | loop fusion | flops 196608 | bytes 524292 | tf_op jit(solution)/shard_map/convert_element_type | solution.py:121
  (25 shorter events, 1.5 us)
Async XLA Ops:
  0.0 12.6 %copy-start.2 = (s32[4096]{0:T(1024)S(1)}, s32[4096]{0:T(1024)}, u32[]{:S(2)}) copy-start(s32[4096]{0:T(1024)} %param.11) | copy-start | bytes 49156
  2.8 18.3 %all-to-all-start = ((bf16[128,32,32]{0,2,1:T(8,128)(2,1)}), bf16[128,32,32]{0,2,1:T(8,128)(2,1)S(1)}, u32[]{:S(2)}, u32[]{:S(2)}) async-start(bf16[128,32,32]{0,2,1:T(8,128)(2,1)} %bitcast.3), calls=%async_computation | async-start | bytes 524288 | tf_op jit(solution)/shard_map/all_to_all | solution.py:96
  15.0 3.0 %copy-start.1 = (bf16[128,512]{1,0:T(8,128)(2,1)S(1)}, bf16[128,512]{1,0:T(8,128)(2,1)}, u32[]{:S(2)}) copy-start(bf16[128,512]{1,0:T(8,128)(2,1)} %param.8) | copy-start | bytes 393220
  15.0 7.0 %copy-start.3 = (s32[64]{0:T(128)S(1)}, s32[64]{0:T(128)}, u32[]{:S(2)}) copy-start(s32[64]{0:T(128)} %param.12) | copy-start | bytes 772
  32.1 12.4 %all-to-all-start.1 = ((bf16[32,128,16]{1,2,0:T(8,128)(2,1)}), bf16[32,128,16]{1,2,0:T(8,128)(2,1)}, u32[]{:S(2)}, u32[]{:S(2)}) async-start(bf16[32,128,16]{1,2,0:T(8,128)(2,1)} %copy_bitcast_fusion), calls=%async_computation.1 | async-start | bytes 262144 | tf_op jit(solution)/shard_map/all_to_all | solution.py:102
  38.1 11.7 %copy-start = (bf16[512,2,1,512]{0,3,2,1:T(8,128)(2,1)S(1)}, bf16[512,2,1,512]{0,3,2,1:T(8,128)(2,1)}, u32[]{:S(2)}) copy-start(bf16[512,2,1,512]{0,3,2,1:T(8,128)(2,1)} %get-tuple-element.6) | copy-start | bytes 3145732
  45.9 3.9 %collective-permute-start = (bf16[128,1024]{1,0:T(8,128)(2,1)S(1)}, bf16[128,1024]{1,0:T(8,128)(2,1)S(1)}, u32[]{:S(2)}, u32[]{:S(2)}) collective-permute-start(bf16[128,1024]{1,0:T(8,128)(2,1)S(1)} %convolution_convert_fusion), channel_id=1, source_target_pairs={{0,1},{1,0},{2,3},{3,2},{4,5},{5,4},{6,7},{7,6},{8,9},{9,8},{10,11... | collective-permute-start | bytes 786440 | tf_op jit(solution)/shard_map/ppermute | solution.py:112
  50.4 6.3 %collective-permute-start.1 = (bf16[128,512]{1,0:T(8,128)(2,1)S(1)}, bf16[128,512]{1,0:T(8,128)(2,1)S(1)}, u32[]{:S(2)}, u32[]{:S(2)}) collective-permute-start(bf16[128,512]{1,0:T(8,128)(2,1)S(1)} %dynamic-slice_convert_fusion), channel_id=1, source_target_pairs={{0,2},{1,3},{2,0},{3,1},{4,6},{5,7},{6,4},{7,5},{8,10},{9,11},{10,... | collective-permute-start | bytes 393224 | tf_op jit(solution)/shard_map/ppermute | solution.py:118

commit v13 on v9

--- a/solution.py
+++ b/solution.py
@@ -104,21 +104,17 @@
     tp_index = lax.axis_index("tp")
     n_tp = out_weight.shape[1] // chans
     high, core = tp_index // 2, tp_index % 2
-    w_split = out_weight.reshape(chans, n_tp // 2, 2, chans)
-    w_other = lax.dynamic_index_in_dim(w_split, 1 - core, axis=2, keepdims=False)
-    p_other = jnp.dot(
-        gated_local, w_other.reshape(chans, -1), preferred_element_type=jnp.float32
-    )
-    recv_core = lax.ppermute(p_other.astype(jnp.bfloat16), "tp", [(i, i ^ 1) for i in range(n_tp)])
-    w_mine = lax.dynamic_index_in_dim(w_split, core, axis=2, keepdims=False)
-    p_mine = jnp.dot(gated_local, w_mine.reshape(chans, -1), preferred_element_type=jnp.float32)
-    p_mine = p_mine + recv_core.astype(jnp.float32)
-    send_high = lax.dynamic_slice_in_dim(p_mine, (1 - high) * chans, chans, axis=1)
-    keep_high = lax.dynamic_slice_in_dim(p_mine, high * chans, chans, axis=1)
-    recv_high = lax.ppermute(
-        send_high.astype(jnp.bfloat16), "tp", [(i, i ^ 2) for i in range(n_tp)]
-    )
-    return (keep_high + recv_high.astype(jnp.float32)).astype(jnp.bfloat16)
+    half = out_weight.shape[1] // 2
+    w_other = lax.dynamic_slice_in_dim(out_weight, (1 - high) * half, half, axis=1)
+    p_other = jnp.dot(gated_local, w_other, preferred_element_type=jnp.float32)
+    recv_high = lax.ppermute(p_other.astype(jnp.bfloat16), "tp", [(i, i ^ 2) for i in range(n_tp)])
+    w_mine = lax.dynamic_slice_in_dim(out_weight, high * half, half, axis=1)
+    p_mine = jnp.dot(gated_local, w_mine, preferred_element_type=jnp.float32)
+    p_mine = p_mine + recv_high.astype(jnp.float32)
+    send_core = lax.dynamic_slice_in_dim(p_mine, (1 - core) * chans, chans, axis=1)
+    keep_core = lax.dynamic_slice_in_dim(p_mine, core * chans, chans, axis=1)
+    recv_core = lax.ppermute(send_core.astype(jnp.bfloat16), "tp", [(i, i ^ 1) for i in range(n_tp)])
+    return (keep_core + recv_core.astype(jnp.float32)).astype(jnp.bfloat16)
 
 
 def solution(mesh):

time: 57.3 us -> 57.9 us (1.010)
  waiting for transfers between devices: 14 us -> 18.4 us
  local copies, waits for them, and re-layouts: 10.1 us -> 6.18 us
    all_to_all x1, waiting for transfers between devices: 2.85 us -> 5.91 us  [body(): arrived = lax.all_to_all(packed, 'ctx', 1, 0, tiled=True).T]
    unnamed x12 -> x11, local copies, waits for them, and re-layouts: 5.08 us -> 2.34 us
    ppermute x2, starting transfers between devices: 5.44 us -> 6.88 us  [the longest x1 4.19 us: body(): lax.ppermute(send_core.astype(jnp.bfloat16), 'tp', [(i, i ^ 1) for i in r...]
    dynamic_slice x1 -> x0, local copies, waits for them, and re-layouts: 1.18 us -> none  [body(): lax.dynamic_index_in_dim(w_split, 1 - core, axis=2, keepdims=False)]
    all_to_all x1, starting transfers between devices: 4.89 us -> 3.86 us  [body(): pre_local = lax.all_to_all(pre_slots, 'ctx', 0, 1, tiled=True)]
    all_to_all x1, waiting for transfers between devices: 6.39 us -> 7.41 us  [body(): pre_local = lax.all_to_all(pre_slots, 'ctx', 0, 1, tiled=True)]
  transfers between devices with their start and end apart: 4 -> 4, of which waited for: 4 -> 4; matrix products, arithmetic and copies ran while one was open for 12% -> 5% of each run, Pallas kernels for 0% -> 0%
where the time goes in v13:
time: 57.9 us; the launch traced here: 57.5 us
  starting transfers between devices  20.5 us (35%)
  waiting for transfers between devices  18.4 us (32%)
  Pallas kernels  6.83 us (12%)
  local copies, waits for them, and re-layouts  6.18 us (11%)
  matrix products  3.13 us (5%)
  other arithmetic  2.33 us (4%)
    all_to_all x1, starting transfers between devices, body(): arrived = lax.all_to_all(packed, 'ctx', 1, 0, tiled=True).T  9.71 us
    all_to_all x1, waiting for transfers between devices, body(): pre_local = lax.all_to_all(pre_slots, 'ctx', 0, 1, tiled=True)  7.41 us
    pallas_call x1, Pallas kernels, pallas_conv(): pl.pallas_call(conv_kernel, grid=(chans // step,), in_specs=[pl.BlockSpec...  6.83 us
    all_to_all x1, waiting for transfers between devices, body(): arrived = lax.all_to_all(packed, 'ctx', 1, 0, tiled=True).T  5.91 us
    ppermute x1, starting transfers between devices, body(): lax.ppermute(send_core.astype(jnp.bfloat16), 'tp', [(i, i ^ 1) for i in r...  4.19 us
    ppermute x1, waiting for transfers between devices, body(): lax.ppermute(p_other.astype(jnp.bfloat16), 'tp', [(i, i ^ 2) for i in ran...  4.11 us
    all_to_all x1, starting transfers between devices, body(): pre_local = lax.all_to_all(pre_slots, 'ctx', 0, 1, tiled=True)  3.86 us
    ppermute x1, starting transfers between devices, body(): lax.ppermute(p_other.astype(jnp.bfloat16), 'tp', [(i, i ^ 2) for i in ran...  2.7 us
  transfers between devices with their start and end apart: 4, of which 4 were waited for; matrix products, arithmetic and copies ran while one was open for 5% of the time, Pallas kernels for 0%

profile of v13, /device:TPU:1, one launch (start us, length us, event | category | flops | bytes accessed | tf_op | source)
XLA Modules:
  0.0 57.5 jit_solution(11908052306326685495)
XLA Ops:
  0.0 1.2 %copy.35 = bf16[128,512]{0,1:T(8,128)(2,1)S(1)} copy(bf16[128,512]{1,0:T(8,128)(2,1)} %param.7) | data formatting | bytes 262144 | tf_op args[0]
  1.2 1.0 %copy.36 = bf16[128,512]{0,1:T(8,128)(2,1)S(1)} copy(bf16[128,512]{1,0:T(8,128)(2,1)} %param.9) | data formatting | bytes 262144 | tf_op args[2]
  2.3 0.7 %copy.37 = bf16[128,32,2,16]{0,3,2,1:T(8,128)(2,1)} copy(bf16[128,32,2,16]{0,3,1,2:T(8,128)(2,1)S(1)} %pad_maximum_fusion) | data formatting | bytes 524288 | tf_op jit(solution)/shard_map/stack | solution.py:93
  3.0 9.7 %all-to-all-start = ((bf16[128,32,32]{0,2,1:T(8,128)(2,1)}), bf16[128,32,32]{0,2,1:T(8,128)(2,1)S(1)}, u32[]{:S(2)}, u32[]{:S(2)}) async-start(bf16[128,32,32]{0,2,1:T(8,128)(2,1)} %bitcast.3), calls=%async_computation | async-start | bytes 524288 | tf_op jit(solution)/shard_map/all_to_all | solution.py:96
  12.9 0.3 convert_reduce_fusion
  13.4 1.3 %fusion.6.mask_ref = f32[64,4096]{1,0:T(8,128)} fusion(s32[64]{0:T(128)S(1)} %convert_reduce_fusion, s32[4096]{0:T(1024)S(1)} %iota.60, s32[4096]{0:T(1024)S(1)} %iota.55), kind=kLoop, calls=%fused_computation.14 | loop fusion | flops 1835008 | bytes 1081600 | tf_op jit(solution)/shard_map/convert_element_type | solution.py:60
  14.6 0.7 %rev.7.doc_ref = s32[64,64]{1,0:T(8,128)} reverse(s32[64,64]{1,0:T(8,128)S(1)} %reshape.32), dimensions={1} | reverse | bytes 32768 | tf_op jit(solution)/shard_map/rev | solution.py:74
  15.4 5.9 %all-to-all-done = bf16[128,32,32]{0,2,1:T(8,128)(2,1)S(1)} async-done(((bf16[128,32,32]{0,2,1:T(8,128)(2,1)}), bf16[128,32,32]{0,2,1:T(8,128)(2,1)S(1)}, u32[]{:S(2)}, u32[]{:S(2)}) %all-to-all-start) | async-done | bytes 262176 | tf_op jit(solution)/shard_map/all_to_all | solution.py:96
  21.3 0.7 %fusion.22 = (bf16[16,4096]{1,0:T(8,128)(2,1)S(1)}, bf16[16,4096]{1,0:T(8,128)(2,1)}) fusion(bf16[32,4096]{1,0:T(8,128)(2,1)S(1)} %bitcast_bitcast_fusion), kind=kLoop, calls=%fused_computation.35 | loop fusion | bytes 524288 | tf_op jit(solution)/shard_map/slice | solution.py:97
  22.0 0.2 reshape.31
  22.2 1.1 %fusion.x_ref = bf16[16,64,64]{2,1,0:T(8,128)(2,1)} fusion(bf16[16,64,64]{2,1,0:T(8,128)(2,1)S(1)} %reshape.31, bf16[64,64]{1,0:T(8,128)(2,1)S(1)} %rev.6, s32[64]{0:T(128)S(1)} %copy-done.3), kind=kOutput, calls=%fused_computation.5 | convolution fusion | flops 16912384 | bytes 270592 | tf_op jit(solution)/shard_map/tk,ckm->ctm/dot_general | solution.py:91
  23.3 6.8 %shard_map.73 = bf16[16,64,64]{2,1,0:T(8,128)(2,1)} custom-call(s32[1]{0:T(128)} %bitcast.base_ref, f32[512]{0:T(512)} %bias_ref.1, bf16[16,4096]{1,0:T(8,128)(2,1)} %get-tuple-element.6.f_ref, bf16[16,64,64]{2,1,0:T(8,128)(2,1)} %fusion.x_ref, s32[64,64]{1,0:T(8,128)} %rev.7.doc_ref, f32[64,4096]{1,0:T(8,128)} %fusion.6.mask_ref), custom_call_target="tpu_custom_call" | custom-call | tf_op jit(solution)/shard_map/pallas_call | solution.py:61
  30.2 1.4 %fusion.1 = bf16[16,64,64]{1,2,0:T(8,128)(2,1)S(1)} fusion(bf16[16,64,64]{2,1,0:T(8,128)(2,1)} %shard_map.73, bf16[64,64]{1,0:T(8,128)(2,1)S(1)} %rev.6, s32[64]{0:T(128)S(1)} %copy-done.3), kind=kOutput, calls=%fused_computation.6 | convolution fusion | flops 16912384 | bytes 270592 | tf_op jit(solution)/shard_map/tk,ctm->ckm/dot_general | solution.py:91
  31.7 0.3 reshape.33
  32.0 0.7 %copy_bitcast_fusion = bf16[32,128,16]{1,2,0:T(8,128)(2,1)} fusion(bf16[16,4096]{1,0:T(8,128)(2,1)S(1)} %reshape.33), kind=kLoop, calls=%fused_computation.22 | loop fusion | bytes 262144 | tf_op jit(solution)/shard_map/all_to_all | solution.py:102
  32.7 3.9 %all-to-all-start.1 = ((bf16[32,128,16]{1,2,0:T(8,128)(2,1)}), bf16[32,128,16]{1,2,0:T(8,128)(2,1)S(1)}, u32[]{:S(2)}, u32[]{:S(2)}) async-start(bf16[32,128,16]{1,2,0:T(8,128)(2,1)} %copy_bitcast_fusion), calls=%async_computation.1 | async-start | bytes 262144 | tf_op jit(solution)/shard_map/all_to_all | solution.py:102
  36.7 7.4 %all-to-all-done.1 = bf16[32,128,16]{1,2,0:T(8,128)(2,1)S(1)} async-done(((bf16[32,128,16]{1,2,0:T(8,128)(2,1)}), bf16[32,128,16]{1,2,0:T(8,128)(2,1)S(1)}, u32[]{:S(2)}, u32[]{:S(2)}) %all-to-all-start.1) | async-done | bytes 131104 | tf_op jit(solution)/shard_map/all_to_all | solution.py:102
  44.2 0.3 convolution_convert_fusion
  44.5 2.7 %collective-permute-start = (bf16[128,1024]{1,0:T(8,128)(2,1)S(1)}, bf16[128,1024]{1,0:T(8,128)(2,1)S(1)}, u32[]{:S(2)}, u32[]{:S(2)}) collective-permute-start(bf16[128,1024]{1,0:T(8,128)(2,1)S(1)} %convolution_convert_fusion), channel_id=1, source_target_pairs={{0,2},{1,3},{2,0},{3,1},{4,6},{5,7},{6,4},{7,5},{8,10},{9,11},{10,... | collective-permute-start | bytes 786440 | tf_op jit(solution)/shard_map/ppermute | solution.py:110
  47.2 4.1 %collective-permute-done = bf16[128,1024]{1,0:T(8,128)(2,1)S(1)} collective-permute-done((bf16[128,1024]{1,0:T(8,128)(2,1)S(1)}, bf16[128,1024]{1,0:T(8,128)(2,1)S(1)}, u32[]{:S(2)}, u32[]{:S(2)}) %collective-permute-start) | collective-permute-done | bytes 262176 | tf_op jit(solution)/shard_map/ppermute | solution.py:110
  51.3 0.3 convert_add_fusion
  51.7 4.2 %collective-permute-start.1 = (bf16[128,512]{1,0:T(8,128)(2,1)S(1)}, bf16[128,512]{1,0:T(8,128)(2,1)S(1)}, u32[]{:S(2)}, u32[]{:S(2)}) collective-permute-start(bf16[128,512]{1,0:T(8,128)(2,1)S(1)} %dynamic-slice_convert_fusion), channel_id=1, source_target_pairs={{0,1},{1,0},{2,3},{3,2},{4,5},{5,4},{6,7},{7,6},{8,9},{9,8},{10,11... | collective-permute-start | bytes 393224 | tf_op jit(solution)/shard_map/ppermute | solution.py:116
  55.9 1.0 %collective-permute-done.1 = bf16[128,512]{1,0:T(8,128)(2,1)S(1)} collective-permute-done((bf16[128,512]{1,0:T(8,128)(2,1)S(1)}, bf16[128,512]{1,0:T(8,128)(2,1)S(1)}, u32[]{:S(2)}, u32[]{:S(2)}) %collective-permute-start.1) | collective-permute-done | bytes 131104 | tf_op jit(solution)/shard_map/ppermute | solution.py:116
  56.9 0.7 %add_convert_fusion = bf16[128,512]{1,0:T(8,128)(2,1)} fusion(bf16[128,512]{1,0:T(8,128)(2,1)S(1)} %collective-permute-done.1, f32[128,1024]{1,0:T(8,128)S(1)} %convert_add_fusion, s32[]{:T(128)S(6)} %select_n.27), kind=kLoop, calls=%fused_computation.20 | loop fusion | flops 196608 | bytes 524292 | tf_op jit(solution)/shard_map/convert_element_type | solution.py:117
  (23 shorter events, 0.8 us)
Async XLA Ops:
  0.0 44.2 %copy-start = (bf16[512,2048]{1,0:T(8,128)(2,1)S(1)}, bf16[512,2048]{1,0:T(8,128)(2,1)}, u32[]{:S(2)}) copy-start(bf16[512,2048]{1,0:T(8,128)(2,1)} %param.13) | copy-start | bytes 6291460
  0.0 12.7 %copy-start.2 = (s32[4096]{0:T(1024)S(1)}, s32[4096]{0:T(1024)}, u32[]{:S(2)}) copy-start(s32[4096]{0:T(1024)} %param.11) | copy-start | bytes 49156
  2.3 20.0 %copy-start.3 = (s32[64]{0:T(128)S(1)}, s32[64]{0:T(128)}, u32[]{:S(2)}) copy-start(s32[64]{0:T(128)} %param.12) | copy-start | bytes 772
  3.0 18.3 %all-to-all-start = ((bf16[128,32,32]{0,2,1:T(8,128)(2,1)}), bf16[128,32,32]{0,2,1:T(8,128)(2,1)S(1)}, u32[]{:S(2)}, u32[]{:S(2)}) async-start(bf16[128,32,32]{0,2,1:T(8,128)(2,1)} %bitcast.3), calls=%async_computation | async-start | bytes 524288 | tf_op jit(solution)/shard_map/all_to_all | solution.py:96
  22.2 14.3 %copy-start.1 = (bf16[128,512]{1,0:T(8,128)(2,1)S(1)}, bf16[128,512]{1,0:T(8,128)(2,1)}, u32[]{:S(2)}) copy-start(bf16[128,512]{1,0:T(8,128)(2,1)} %param.8) | copy-start | bytes 393220
  32.7 11.4 %all-to-all-start.1 = ((bf16[32,128,16]{1,2,0:T(8,128)(2,1)}), bf16[32,128,16]{1,2,0:T(8,128)(2,1)S(1)}, u32[]{:S(2)}, u32[]{:S(2)}) async-start(bf16[32,128,16]{1,2,0:T(8,128)(2,1)} %copy_bitcast_fusion), calls=%async_computation.1 | async-start | bytes 262144 | tf_op jit(solution)/shard_map/all_to_all | solution.py:102
  44.5 6.8 %collective-permute-start = (bf16[128,1024]{1,0:T(8,128)(2,1)S(1)}, bf16[128,1024]{1,0:T(8,128)(2,1)S(1)}, u32[]{:S(2)}, u32[]{:S(2)}) collective-permute-start(bf16[128,1024]{1,0:T(8,128)(2,1)S(1)} %convolution_convert_fusion), channel_id=1, source_target_pairs={{0,2},{1,3},{2,0},{3,1},{4,6},{5,7},{6,4},{7,5},{8,10},{9,11},{10,... | collective-permute-start | bytes 786440 | tf_op jit(solution)/shard_map/ppermute | solution.py:110
  51.7 5.2 %collective-permute-start.1 = (bf16[128,512]{1,0:T(8,128)(2,1)S(1)}, bf16[128,512]{1,0:T(8,128)(2,1)S(1)}, u32[]{:S(2)}, u32[]{:S(2)}) collective-permute-start(bf16[128,512]{1,0:T(8,128)(2,1)S(1)} %dynamic-slice_convert_fusion), channel_id=1, source_target_pairs={{0,1},{1,0},{2,3},{3,2},{4,5},{5,4},{6,7},{7,6},{8,9},{9,8},{10,11... | collective-permute-start | bytes 393224 | tf_op jit(solution)/shard_map/ppermute | solution.py:116
